TPU v7x, 32 devices: a whole 2x2x4 slice. The times are simulated.
32 devices in a mesh: blk: 16 (over z, y, core), grp: 2 (over x).
Axes of the slice: x: 2, y: 2, z: 4, core: 2. Of those that a mesh axis runs over, the one named last changes fastest.
Arguments:
- frames: float32 [6144, 1024], P(('blk', 'grp')), may hold values from -6 to 6
- lengths: int32 [12], replicated, may hold values from 1 to 4096, 6144 in all
- norm1_gain: float32 [1024], replicated, may hold values from 0.5 to 1.5
- w_query: bfloat16 [1024, 1024], replicated, may hold values from -0.1875 to 0.1875
- w_key: bfloat16 [1024, 1024], replicated, may hold values from -0.1875 to 0.1875
- w_value: bfloat16 [1024, 1024], replicated, may hold values from -0.1875 to 0.1875
- w_out: bfloat16 [1024, 1024], replicated, may hold values from -1.5 to 1.5
- norm2_gain: float32 [1024], replicated, may hold values from 0.5 to 1.5
- w_up: bfloat16 [1024, 4096], replicated, may hold values from -0.1875 to 0.1875
- b_up: float32 [4096], replicated, may hold values from -3 to 3
- w_down: bfloat16 [4096, 1024], replicated, may hold values from -0.09375 to 0.09375
- b_down: float32 [1024], replicated, may hold values from -3 to 3
- cotangent: float32 [6144, 1024], P(('blk', 'grp')), may hold values from -6 to 6
Outputs:
- layer_out: float32 [6144, 1024], P(('blk', 'grp'))
- frames_grad: float32 [6144, 1024], P(('blk', 'grp'))
- norm1_gain_grad: float32 [1024], P(('blk', 'grp'))
- w_query_grad: float32 [1024, 1024], P(('blk', 'grp'))
- w_key_grad: float32 [1024, 1024], P(('blk', 'grp'))
- w_value_grad: float32 [1024, 1024], P(('blk', 'grp'))
- w_out_grad: float32 [1024, 1024], P(('blk', 'grp'))
- norm2_gain_grad: float32 [1024], P(('blk', 'grp'))
- w_up_grad: float32 [1024, 4096], P(('blk', 'grp'))
- b_up_grad: float32 [4096], P(('blk', 'grp'))
- w_down_grad: float32 [4096, 1024], P(('blk', 'grp'))
- b_down_grad: float32 [1024], P(('blk', 'grp'))
Inputs may be any that keep to these rules, and one draw needn't show every extreme that they name: The lengths sum to 6144; the longest item has exactly 4096 frames.
All inputs are finite; a program needn't handle non-finite values.
Results may differ from a plain program's by a relative error of at most 0.012.
Values may be sent and summed in bfloat16 or wider, within the bound.
A program may use at most 192 MiB of HBM per device.

v0:
```python
import jax
import jax.numpy as jnp
from jax import lax
from jax.sharding import PartitionSpec as P

HEAD_DIM = 64
ITEM_MAX = 4096


EPSILON = 1e-05
MASKED = -1e30
SCALING = 0.125


def shortened(array):

    def short(part):
        return part.astype(jnp.bfloat16) if part.dtype == jnp.float32 else part

    return jax.tree.map(short, array)


def passed_along(block, axis, distance):
    devices = range(lax.axis_size(axis))
    route = [(i - distance, i) for i in devices if i - distance in devices]
    return lax.ppermute(block, axis, route)


def rms_norm(values, gain):
    return values * lax.rsqrt(jnp.mean(values * values, axis=-1, keepdims=True) + EPSILON) * gain


def gelu_exact(values):
    return jax.nn.gelu(values, approximate=False)


def item_starts(lengths, positions):
    ends = jnp.cumsum(lengths)
    offsets = ends - lengths
    before = offsets[None, :] <= positions[:, None]
    return jnp.max(jnp.where(before, offsets[None, :], 0), axis=1)


def live_mask(query_pos, query_start, key_first, key_count):
    key_pos = key_first + jnp.arange(key_count, dtype=jnp.int32)
    return (key_pos[None, :] >= query_start[:, None]) & (key_pos[None, :] <= query_pos[:, None])


def split_heads(matrix):
    return matrix.reshape(matrix.shape[0], matrix.shape[1] // HEAD_DIM, HEAD_DIM)


def merge_heads(tensor):
    return tensor.reshape(tensor.shape[0], tensor.shape[1] * tensor.shape[2])


def scores_of(queries3, keys_block, mask):
    raw = jnp.einsum(
        "qhd,khd->hqk", queries3, split_heads(keys_block), preferred_element_type=jnp.float32
    )
    return jnp.where(mask[None], raw * SCALING, MASKED)


def left_dot(left, right):
    return lax.dot_general(
        left, right, (((0,), (0,)), ((), ())), preferred_element_type=jnp.float32
    )


def right_dot(left, right):
    return lax.dot_general(
        left, right, (((1,), (1,)), ((), ())), preferred_element_type=jnp.float32
    )


def grad_parts(queries3, grad_out3, log_total, delta, keys_block, values_block, mask):
    probs = jnp.exp(scores_of(queries3, keys_block, mask) - log_total[:, :, None])
    grad_probs = jnp.einsum(
        "qhd,khd->hqk", grad_out3, split_heads(values_block), preferred_element_type=jnp.float32
    )
    grad_scores = (probs * (grad_probs - delta[:, :, None])).astype(jnp.bfloat16)
    return (probs.astype(jnp.bfloat16), grad_scores)


def key_terms(queries3, grad_out3, probs_low, grad_scores):
    grad_keys = jnp.einsum(
        "hqk,qhd->khd", grad_scores, queries3, preferred_element_type=jnp.float32
    )
    grad_values = jnp.einsum(
        "hqk,qhd->khd", probs_low, grad_out3, preferred_element_type=jnp.float32
    )
    return (merge_heads(grad_keys), merge_heads(grad_values))


def query_term(grad_scores, keys_block):
    return jnp.einsum(
        "hqk,khd->qhd", grad_scores, split_heads(keys_block), preferred_element_type=jnp.float32
    )


def shards(
    frames,
    lengths,
    norm1_gain,
    w_query,
    w_key,
    w_value,
    w_out,
    norm2_gain,
    w_up,
    b_up,
    w_down,
    b_down,
    cotangent,
):
    row_count = frames.shape[0]
    width = frames.shape[1]
    heads = width // HEAD_DIM
    groups = lax.axis_size("grp")
    block_rows = row_count * groups
    span = (ITEM_MAX + block_rows - 2) // block_rows
    blk_index = lax.axis_index("blk")
    sub_index = lax.axis_index("grp")
    block_first = blk_index * block_rows
    query_pos = block_first + sub_index * row_count + jnp.arange(row_count, dtype=jnp.int32)
    query_start = item_starts(lengths, query_pos)
    back_steps = jnp.arange(span + 1, dtype=jnp.int32)
    normed1, norm1_back = jax.vjp(rms_norm, frames, norm1_gain)
    act1 = normed1.astype(jnp.bfloat16)
    queries = jnp.dot(act1, w_query, preferred_element_type=jnp.float32).astype(jnp.bfloat16)
    keys_own = jnp.dot(act1, w_key, preferred_element_type=jnp.float32).astype(jnp.bfloat16)
    values_own = jnp.dot(act1, w_value, preferred_element_type=jnp.float32).astype(jnp.bfloat16)
    queries3 = split_heads(queries)
    block_keys, block_values = (
        lax.all_gather(keys_own, "grp", axis=0, tiled=True),
        lax.all_gather(values_own, "grp", axis=0, tiled=True),
    )

    def cycle_step(carry, unused_input):
        moved = jax.tree.map(
            lambda part, own: part.astype(own.dtype),
            passed_along(shortened(carry), "blk", 1),
            carry,
        )
        return (moved, moved)

    unused_last, far_blocks = lax.scan(cycle_step, (block_keys, block_values), None, length=span)
    keys_all = jnp.concatenate([block_keys[None], far_blocks[0]], axis=0)
    values_all = jnp.concatenate([block_values[None], far_blocks[1]], axis=0)

    def mask_for(back):
        return live_mask(query_pos, query_start, block_first - back * block_rows, block_rows)

    def total_step(carry, inputs):
        run_max, run_sum = carry
        keys_block, back = inputs
        scores = scores_of(queries3, keys_block, mask_for(back))
        new_max = jnp.maximum(run_max, jnp.max(scores, axis=-1))
        run_sum = run_sum * jnp.exp(run_max - new_max) + jnp.sum(
            jnp.exp(scores - new_max[:, :, None]), axis=-1
        )
        return ((new_max, run_sum), None)

    start_max = jnp.full((heads, row_count), MASKED, jnp.float32)
    start_sum = jnp.zeros((heads, row_count), jnp.float32)
    (top_max, top_sum), unused_out = lax.scan(
        total_step, (start_max, start_sum), (keys_all, back_steps)
    )
    log_total = top_max + jnp.log(top_sum)

    def mix_step(total, inputs):
        keys_block, values_block, back = inputs
        probs = jnp.exp(
            scores_of(queries3, keys_block, mask_for(back)) - log_total[:, :, None]
        ).astype(jnp.bfloat16)
        return (
            total
            + jnp.einsum(
                "hqk,khd->qhd", probs, split_heads(values_block), preferred_element_type=jnp.float32
            ),
            None,
        )

    zero_query = jnp.zeros((row_count, heads, HEAD_DIM), jnp.float32)
    mixed_sum, unused_out = lax.scan(mix_step, zero_query, (keys_all, values_all, back_steps))
    mixed = merge_heads(mixed_sum).astype(jnp.bfloat16)
    middle = frames + jnp.dot(mixed, w_out, preferred_element_type=jnp.float32)
    normed2, norm2_back = jax.vjp(rms_norm, middle, norm2_gain)
    act2 = normed2.astype(jnp.bfloat16)
    before = jnp.dot(act2, w_up, preferred_element_type=jnp.float32) + b_up
    activated, gelu_back = jax.vjp(gelu_exact, before)
    hidden = activated.astype(jnp.bfloat16)
    layer_out = middle + jnp.dot(hidden, w_down, preferred_element_type=jnp.float32) + b_down
    grad_low = cotangent.astype(jnp.bfloat16)
    b_down_grad = jnp.sum(grad_low.astype(jnp.float32), axis=0)
    w_down_grad = left_dot(hidden, grad_low)
    grad_before = gelu_back(right_dot(grad_low, w_down))[0].astype(jnp.bfloat16)
    b_up_grad = jnp.sum(grad_before.astype(jnp.float32), axis=0)
    w_up_grad = left_dot(act2, grad_before)
    grad_mid_norm, norm2_gain_grad = norm2_back(right_dot(grad_before, w_up))
    grad_middle = cotangent + grad_mid_norm
    grad_attn = grad_middle.astype(jnp.bfloat16)
    w_out_grad = left_dot(mixed, grad_attn)
    grad_mixed = right_dot(grad_attn, w_out).astype(jnp.bfloat16)
    grad_out3 = split_heads(grad_mixed)

    def delta_step(total, inputs):
        keys_block, values_block, back = inputs
        probs = jnp.exp(scores_of(queries3, keys_block, mask_for(back)) - log_total[:, :, None])
        grad_probs = jnp.einsum(
            "qhd,khd->hqk", grad_out3, split_heads(values_block), preferred_element_type=jnp.float32
        )
        return (total + jnp.sum(probs * grad_probs, axis=-1), None)

    delta, unused_out = lax.scan(
        delta_step, jnp.zeros((heads, row_count), jnp.float32), (keys_all, values_all, back_steps)
    )
    zero_block = jnp.zeros((block_rows, width), jnp.float32)

    def return_step(carry, inputs):
        grad_q, travel = carry
        keys_block, values_block, back = inputs
        probs_low, grad_scores = grad_parts(
            queries3, grad_out3, log_total, delta, keys_block, values_block, mask_for(back)
        )
        grad_keys, grad_values = key_terms(queries3, grad_out3, probs_low, grad_scores)
        moved = (
            passed_along((travel[0] + grad_keys).astype(jnp.bfloat16), "blk", -1).astype(
                jnp.float32
            ),
            passed_along((travel[1] + grad_values).astype(jnp.bfloat16), "blk", -1).astype(
                jnp.float32
            ),
        )
        return ((grad_q + query_term(grad_scores, keys_block), moved), None)

    (grad_q, travel), unused_out = lax.scan(
        return_step,
        (zero_query, (zero_block, zero_block)),
        (far_blocks[0], far_blocks[1], back_steps[1:]),
        reverse=True,
    )
    probs_low, grad_scores = grad_parts(
        queries3, grad_out3, log_total, delta, block_keys, block_values, mask_for(0)
    )
    grad_keys, grad_values = key_terms(queries3, grad_out3, probs_low, grad_scores)
    grad_q = grad_q + query_term(grad_scores, block_keys)
    block_grad_keys = travel[0] + grad_keys
    block_grad_values = travel[1] + grad_values
    grad_keys_rows, grad_values_rows = (
        lax.psum_scatter(
            block_grad_keys.astype(jnp.bfloat16), "grp", scatter_dimension=0, tiled=True
        ).astype(jnp.float32),
        lax.psum_scatter(
            block_grad_values.astype(jnp.bfloat16), "grp", scatter_dimension=0, tiled=True
        ).astype(jnp.float32),
    )
    grad_keys_low = (grad_keys_rows * SCALING).astype(jnp.bfloat16)
    grad_values_low = grad_values_rows.astype(jnp.bfloat16)
    grad_queries_low = (merge_heads(grad_q) * SCALING).astype(jnp.bfloat16)
    w_query_grad = left_dot(act1, grad_queries_low)
    w_key_grad = left_dot(act1, grad_keys_low)
    w_value_grad = left_dot(act1, grad_values_low)
    grad_act1 = (
        right_dot(grad_queries_low, w_query)
        + right_dot(grad_keys_low, w_key)
        + right_dot(grad_values_low, w_value)
    )
    grad_frames_norm, norm1_gain_grad = norm1_back(grad_act1)
    frames_grad = grad_middle + grad_frames_norm
    shares = (
        lax.psum_scatter(norm1_gain_grad, ("blk", "grp"), scatter_dimension=0, tiled=True),
        lax.psum_scatter(w_query_grad, ("blk", "grp"), scatter_dimension=0, tiled=True),
        lax.psum_scatter(w_key_grad, ("blk", "grp"), scatter_dimension=0, tiled=True),
        lax.psum_scatter(w_value_grad, ("blk", "grp"), scatter_dimension=0, tiled=True),
        lax.psum_scatter(w_out_grad, ("blk", "grp"), scatter_dimension=0, tiled=True),
        lax.psum_scatter(norm2_gain_grad, ("blk", "grp"), scatter_dimension=0, tiled=True),
        lax.psum_scatter(w_up_grad, ("blk", "grp"), scatter_dimension=0, tiled=True),
        lax.psum_scatter(b_up_grad, ("blk", "grp"), scatter_dimension=0, tiled=True),
        lax.psum_scatter(w_down_grad, ("blk", "grp"), scatter_dimension=0, tiled=True),
        lax.psum_scatter(b_down_grad, ("blk", "grp"), scatter_dimension=0, tiled=True),
    )
    return (
        layer_out,
        frames_grad,
        shares[0],
        shares[1],
        shares[2],
        shares[3],
        shares[4],
        shares[5],
        shares[6],
        shares[7],
        shares[8],
        shares[9],
    )


def solution(mesh):
    placed = (
        P(("blk", "grp"), None),
        P(),
        P(),
        P(),
        P(),
        P(),
        P(),
        P(),
        P(),
        P(),
        P(),
        P(),
        P(("blk", "grp"), None),
    )
    return jax.shard_map(
        shards,
        mesh=mesh,
        in_specs=placed,
        out_specs=(
            P(("blk", "grp"), None),
            P(("blk", "grp"), None),
            P(("blk", "grp")),
            P(("blk", "grp"), None),
            P(("blk", "grp"), None),
            P(("blk", "grp"), None),
            P(("blk", "grp"), None),
            P(("blk", "grp")),
            P(("blk", "grp"), None),
            P(("blk", "grp")),
            P(("blk", "grp"), None),
            P(("blk", "grp")),
        ),
        check_vma=False,
    )
```

profile of v0, /device:TPU:0, one launch (start us, length us, event | category | flops | bytes accessed | tf_op | source)
XLA Modules:
  0.0 2577.7 jit_solution(17751020805881900035)
XLA Ops:
  48.7 332.0 %while.70 = (s32[]{:T(128)}, bf16[384,1024]{1,0:T(8,128)(2,1)}, bf16[384,1024]{1,0:T(8,128)(2,1)S(1)}, bf16[11,384,1024]{1,2,0:T(8,128)(2,1)}, bf16[11,384,1024]{1,2,0:T(8,128)(2,1)}, /*index=5*/s32[]{:T(128)}) while((s32[]{:T(128)}, bf16[384,1024]{1,0:T(8,128)(2,1)}, bf16[384,1024]{1,0:T(8,128)(2,1)S(1)}, bf16[11,384,1024]{1,2,0:T(8,128)(2,1)}, ...), condition=%wide.region_2.3_spmd, body=%wide.region_1.2_spmd.sunk | while | flops 2 | bytes 18874560 | solution.py:147
  67.1 15.4 collective-permute-start
  98.5 15.4 collective-permute-start
  130.0 15.4 collective-permute-start
  161.5 15.4 collective-permute-start
  192.9 15.4 collective-permute-start
  224.4 15.4 collective-permute-start
  255.8 15.4 collective-permute-start
  287.3 15.4 collective-permute-start
  318.8 15.4 collective-permute-start
  350.2 15.4 collective-permute-start
  395.5 109.3 %while.71 = (s32[]{:T(128)}, f32[16,192]{1,0:T(8,128)S(1)}, f32[16,192]{1,0:T(8,128)S(1)}, s32[12]{0:T(128)S(1)}, s32[]{:T(128)}, /*index=5*/s32[192]{0:T(256)S(...) while((s32[]{:T(128)}, f32[16,192]{1,0:T(8,128)S(1)}, ...), condition=%wide.region_8.9_spmd.clone, body=%wide.region_5.8_spmd.clone.sunk | while | flops 159489600 | bytes 12576184 | solution.py:166
  504.9 109.8 %while.72 = (s32[]{:T(128)}, f32[192,16,64]{0,2,1:T(8,128)}, bf16[12,384,1024]{1,2,0:T(8,128)(2,1)}, s32[12]{0:T(128)S(1)}, s32[]{:T(128)}, /*index=5*/s32[192]{...) while((s32[]{:T(128)}, f32[192,16,64]{0,2,1:T(8,128)}, ...), condition=%wide.region_10.11_spmd.clone, body=%wide.region_9.10_spmd.clone.sunk | while | flops 307323456 | bytes 6849983 | solution.py:185
  647.2 140.9 %while.73 = (s32[]{:T(128)}, f32[16,192]{1,0:T(8,128)}, s32[12]{0:T(128)S(1)}, s32[]{:T(128)}, s32[192]{0:T(256)}, /*index=5*/bf16[12,384,1024]{1,2,0:T(8,128)(2...) while((s32[]{:T(128)}, f32[16,192]{1,0:T(8,128)}, ...), condition=%wide.region_15.16_spmd.clone, body=%wide.region_13.15_spmd.clone.sunk | while | flops 308112960 | bytes 15258139 | solution.py:215
  794.3 417.3 %while.74 = (s32[]{:T(128)}, f32[192,16,64]{0,2,1:T(8,128)}, f32[384,1024]{0,1:T(8,128)}, f32[384,1024]{0,1:T(8,128)}, bf16[11,384,1024]{1,2,0:T(8,128)(2,1)}, /...) while((s32[]{:T(128)}, f32[192,16,64]{0,2,1:T(8,128)}, ...), condition=%wide.region_17.18_spmd.clone, body=%wide.region_16.17_spmd.clone.sunk | while | flops 770531904 | bytes 80479968 | solution.py:237
  1235.3 26.7 %reduce-scatter.25.cloned.1.call-done = bf16[192,1024]{1,0:T(8,128)(2,1)} async-done(((bf16[384,1024]{1,0:T(8,128)(2,1)}), bf16[192,1024]{1,0:T(8,128)(2,1)}) %reduce-scatter.25.cloned.1.call-update) | async-done | bytes 393232
  1266.0 15.8 reduce-scatter.27.cloned.1.call-done
  1319.2 40.3 %all-reduce.4 = (f32[1024]{0:T(1024)S(1)}, f32[1024]{0:T(1024)S(1)}, f32[4096]{0:T(1024)S(1)}, f32[1024]{0:T(1024)S(1)}) all-reduce(f32[1024]{0:T(1024)S(1)} %get-tuple-element.736, f32[1024]{0:T(1024)S(1)} %copy-done.52, f32[4096]{0:T(1024)S(1)} %copy-done.44, ...), channel_id=4, replica_groups=mesh['blk'=16,'grp'=2] {'blk','grp'}, use_global_device_ids=true, to_apply=%region_22.23.clone | all-reduce | flops 7168 | bytes 57344
  1364.3 62.4 %reduce-scatter.13.cloned.1.call-done = f32[32,1024]{1,0:T(8,128)} async-done(((f32[1024,1024]{1,0:T(8,128)}), f32[32,1024]{1,0:T(8,128)}) %reduce-scatter.13.cloned.1.call-update) | async-done | bytes 131088 | tf_op jit(solution)/shard_map/reduce_scatter | solution.py:273
  1426.6 142.0 %reduce-scatter.19.cloned.1.call-done = f32[32,1024]{1,0:T(8,128)} async-done(((f32[1024,1024]{1,0:T(8,128)}), f32[32,1024]{1,0:T(8,128)}) %reduce-scatter.19.cloned.1.call-update) | async-done | bytes 131088 | tf_op jit(solution)/shard_map/reduce_scatter | solution.py:276
  1568.6 141.8 %reduce-scatter.15.cloned.1.call-done = f32[32,1024]{1,0:T(8,128)} async-done(((f32[1024,1024]{1,0:T(8,128)}), f32[32,1024]{1,0:T(8,128)}) %reduce-scatter.15.cloned.1.call-update) | async-done | bytes 131088 | tf_op jit(solution)/shard_map/reduce_scatter | solution.py:274
  1710.4 141.8 %reduce-scatter.17.cloned.1.call-done = f32[32,1024]{1,0:T(8,128)} async-done(((f32[1024,1024]{1,0:T(8,128)}), f32[32,1024]{1,0:T(8,128)}) %reduce-scatter.17.cloned.1.call-update) | async-done | bytes 131088 | tf_op jit(solution)/shard_map/reduce_scatter | solution.py:275
  1852.2 356.8 %reduce-scatter.21.cloned.1.call-done = f32[32,4096]{1,0:T(8,128)} async-done(((f32[1024,4096]{1,0:T(8,128)}), f32[32,4096]{1,0:T(8,128)}) %reduce-scatter.21.cloned.1.call-update) | async-done | bytes 524304 | tf_op jit(solution)/shard_map/reduce_scatter | solution.py:278
  2209.0 361.5 %reduce-scatter.23.cloned.1.call-done = f32[128,1024]{1,0:T(8,128)} async-done(((f32[4096,1024]{1,0:T(8,128)}), f32[128,1024]{1,0:T(8,128)}) %reduce-scatter.23.cloned.1.call-update) | async-done | bytes 524304 | tf_op jit(solution)/shard_map/reduce_scatter | solution.py:280
  (1009 shorter events, 1084.4 us)
Async XLA Ops:
  7.2 1254.8 %reduce-scatter.25.cloned.1.call-start = ((), (), s32[]{:S(2)}) async-start(), calls=%async_computation.14 | async-start | bytes 1179648
  67.1 20.7 collective-permute-start
  98.5 20.7 collective-permute-start
  130.0 20.7 collective-permute-start
  161.5 20.7 collective-permute-start
  192.9 20.7 collective-permute-start
  224.4 20.7 collective-permute-start
  255.8 20.7 collective-permute-start
  287.3 20.7 collective-permute-start
  318.8 20.7 collective-permute-start
  350.2 20.7 collective-permute-start
  807.3 18.4 collective-permute-start.2
  812.4 18.9 collective-permute-start.3
  851.6 17.9 collective-permute-start.3
  1114.4 18.0 collective-permute-start.3
  1152.8 18.0 collective-permute-start.3
  1191.1 18.0 collective-permute-start.3
  1216.8 65.0 %reduce-scatter.27.cloned.1.call-start = ((), (), s32[]{:S(2)}) async-start(), calls=%async_computation.15 | async-start | bytes 1179648
  1223.6 203.1 %reduce-scatter.13.cloned.1.call-start = ((), (), s32[]{:S(2)}) async-start(), calls=%async_computation.8 | async-start | bytes 4325376 | tf_op jit(solution)/shard_map/reduce_scatter | solution.py:273
  1230.4 338.2 %reduce-scatter.19.cloned.1.call-start = ((), (), s32[]{:S(2)}) async-start(), calls=%async_computation.11 | async-start | bytes 4325376 | tf_op jit(solution)/shard_map/reduce_scatter | solution.py:276
  1235.3 475.2 %reduce-scatter.15.cloned.1.call-start = ((), (), s32[]{:S(2)}) async-start(), calls=%async_computation.9 | async-start | bytes 4325376 | tf_op jit(solution)/shard_map/reduce_scatter | solution.py:274
  1266.0 586.3 %reduce-scatter.17.cloned.1.call-start = ((), (), s32[]{:S(2)}) async-start(), calls=%async_computation.10 | async-start | bytes 4325376 | tf_op jit(solution)/shard_map/reduce_scatter | solution.py:275
  1285.5 923.5 %reduce-scatter.21.cloned.1.call-start = ((), (), s32[]{:S(2)}) async-start(), calls=%async_computation.12 | async-start | bytes 17301504 | tf_op jit(solution)/shard_map/reduce_scatter | solution.py:278
  1296.3 1274.3 %reduce-scatter.23.cloned.1.call-start = ((), (), s32[]{:S(2)}) async-start(), calls=%async_computation.13 | async-start | bytes 17301504 | tf_op jit(solution)/shard_map/reduce_scatter | solution.py:280
  (190 other events, 1237.4 us)
Sparse Core Ops, SparseCore 0:
  1216.9 45.0 reduce-scatter.24
  1264.3 17.4 reduce-scatter.26
  1284.6 141.9 reduce-scatter.12
  1429.3 139.2 reduce-scatter.18
  1571.3 139.0 reduce-scatter.14
  1713.1 139.0 reduce-scatter.16
  1855.1 353.8 reduce-scatter.20
  2211.9 358.6 reduce-scatter.22
where the time goes:
time: 2590 us; the launch traced here: 2580 us
  waiting for transfers between devices  1360 us (53%)
  matrix products  397 us (15%)
  local copies, waits for them, and re-layouts  313 us (12%)
  starting transfers between devices  244 us (9%)
  other arithmetic  151 us (6%)
  blocking collectives  64.1 us (2%)
  loops' own time  34.8 us (1%)
    reduce_scatter x1, waiting for transfers between devices, shards(): lax.psum_scatter(w_down_grad, ('blk', 'grp'), scatter_dimension=0, tiled=...  362 us
    reduce_scatter x1, waiting for transfers between devices, shards(): lax.psum_scatter(w_up_grad, ('blk', 'grp'), scatter_dimension=0, tiled=True)  357 us
    ppermute x44, starting transfers between devices, passed_along(): return lax.ppermute(block, axis, route)  243 us
    reduce_scatter x1, waiting for transfers between devices, shards(): lax.psum_scatter(w_out_grad, ('blk', 'grp'), scatter_dimension=0, tiled=T...  142 us
    reduce_scatter x1, waiting for transfers between devices, shards(): lax.psum_scatter(w_key_grad, ('blk', 'grp'), scatter_dimension=0, tiled=T...  142 us
    reduce_scatter x1, waiting for transfers between devices, shards(): lax.psum_scatter(w_value_grad, ('blk', 'grp'), scatter_dimension=0, tiled...  142 us
    ppermute x44, waiting for transfers between devices, passed_along(): return lax.ppermute(block, axis, route)  110 us
    dynamic_slice x72, local copies, waits for them, and re-layouts, shards(): lax.scan(total_step, (start_max, start_sum), (keys_all, back_steps))  96.6 us
  transfers between devices with their start and end apart: 52, of which 41 were waited for; matrix products, arithmetic and copies ran while one was open for 7% of the time, Pallas kernels for 0%

commit v1 on v0

--- a/solution.py
+++ b/solution.py
@@ -1,6 +1,11 @@
+import functools
+
 import jax
 import jax.numpy as jnp
+import numpy as np
 from jax import lax
+from jax.experimental import pallas as pl
+from jax.experimental.pallas import tpu as pltpu
 from jax.sharding import PartitionSpec as P
 
 HEAD_DIM = 64
@@ -98,7 +103,7 @@
     )
 
 
-def shards(
+def shards_ring(
     frames,
     lengths,
     norm1_gain,
@@ -296,7 +301,7 @@
     )
 
 
-def solution(mesh):
+def solution_ring(mesh):
     placed = (
         P(("blk", "grp"), None),
         P(),
@@ -313,7 +318,7 @@
         P(("blk", "grp"), None),
     )
     return jax.shard_map(
-        shards,
+        shards_ring,
         mesh=mesh,
         in_specs=placed,
         out_specs=(
@@ -332,3 +337,656 @@
         ),
         check_vma=False,
     )
+
+
+LOG2E = 1.4426950408889634
+F32, BF16 = jnp.float32, jnp.bfloat16
+
+
+def nt_dot(a, b):
+    return lax.dot_general(a, b, (((1,), (1,)), ((), ())), preferred_element_type=F32)
+
+
+def nn_dot(a, b):
+    return lax.dot_general(a, b, (((1,), (0,)), ((), ())), preferred_element_type=F32)
+
+
+def low_lanes(shape):
+    return lax.broadcasted_iota(jnp.int32, shape, 1) < 64
+
+
+def pack_kernel(half, frames_ref, gain_ref, wq_ref, wk_ref, wv_ref, kv_ref, q_ref, act_ref):
+    @pl.when(pl.program_id(0) == 0)
+    def _():
+        x = frames_ref[...]
+        r = lax.rsqrt(jnp.mean(x * x, axis=-1, keepdims=True) + EPSILON)
+        act_ref[...] = (x * r * gain_ref[...]).astype(BF16)
+
+    act = act_ref[...]
+    q = nn_dot(act, wq_ref[...]).astype(BF16).astype(F32) * 0.125
+    k = nn_dot(act, wk_ref[...])
+    v = nn_dot(act, wv_ref[...])
+    rows = q.shape[0]
+    low = low_lanes((rows, 128))
+    low_h = low_lanes((half // 2, 128))
+    for p in range(q.shape[1] // 128):
+        at = slice(p * 128, (p + 1) * 128)
+        k2, v2, q2 = k[:, at], v[:, at], q[:, at]
+        kv_a = jnp.where(low, k2, pltpu.roll(v2, 64, 1)).astype(BF16)
+        kv_b = jnp.where(low, pltpu.roll(k2, 64, 1), v2).astype(BF16)
+        for s in range(2):
+            span = slice(s * half, (s + 1) * half)
+            kv_ref[2 * p, s] = kv_a[span]
+            kv_ref[2 * p + 1, s] = kv_b[span]
+            top = q2[s * half : s * half + half // 2]
+            bot = q2[s * half + half // 2 : (s + 1) * half]
+            q_ref[2 * p, s] = jnp.where(low_h, top, pltpu.roll(bot, 64, 1)).astype(BF16)
+            q_ref[2 * p + 1, s] = jnp.where(low_h, pltpu.roll(top, 64, 1), bot).astype(BF16)
+
+
+def project_and_pack(frames, gain, w_query, w_key, w_value):
+    rows, width = frames.shape
+    heads, half, step = width // 64, rows // 2, 256
+    w_spec = pl.BlockSpec((width, step), lambda i: (0, i))
+    whole = lambda i: (0, 0)
+    return pl.pallas_call(
+        functools.partial(pack_kernel, half),
+        grid=(width // step,),
+        in_specs=[pl.BlockSpec((rows, width), whole), pl.BlockSpec((1, width), whole), w_spec, w_spec, w_spec],
+        out_specs=[
+            pl.BlockSpec((step // 64, 2, half, 128), lambda i: (i, 0, 0, 0)),
+            pl.BlockSpec((step // 64, 2, half // 2, 128), lambda i: (i, 0, 0, 0)),
+            pl.BlockSpec((rows, width), whole),
+        ],
+        out_shape=[
+            jax.ShapeDtypeStruct((heads, 2, half, 128), BF16),
+            jax.ShapeDtypeStruct((heads, 2, half // 2, 128), BF16),
+            jax.ShapeDtypeStruct((rows, width), BF16),
+        ],
+        compiler_params=pltpu.CompilerParams(vmem_limit_bytes=40 << 20),
+        name="project_and_pack",
+    )(frames, gain.reshape(1, width), w_query, w_key, w_value)
+
+
+def block_bounds(len_ref, items, qpos, first, last, key_block):
+    off = jnp.int32(0)
+    start = jnp.zeros(qpos.shape, jnp.int32)
+    s_first, s_last = jnp.int32(0), jnp.int32(0)
+    for i in range(items):
+        start = jnp.where(qpos >= off, off, start)
+        s_first = jnp.where(first >= off, off, s_first)
+        s_last = jnp.where(last >= off, off, s_last)
+        off = off + len_ref[i]
+    lo, hi = s_first // key_block, last // key_block + 1
+    f0 = jnp.clip((s_last + key_block - 1) // key_block, lo, hi)
+    f1 = jnp.clip((first + 1) // key_block, f0, hi)
+    return start, lo, f0, f1, hi
+
+
+def query_ends(i, chunks, half, core):
+    first = i * chunks * 2 * half + core * half
+    return first, first + (chunks - 1) * 2 * half + half - 1
+
+
+def spread(packed, low, to_high):
+    f = packed.astype(F32)
+    other = pltpu.roll(f, 64, 1)
+    zero = jnp.zeros_like(f)
+    if to_high:
+        return jnp.where(low, zero, other).astype(BF16), jnp.where(low, zero, f).astype(BF16)
+    return jnp.where(low, f, zero).astype(BF16), jnp.where(low, other, zero).astype(BF16)
+
+
+def mix_kernel(
+    items, chunks, key_block,
+    len_ref, core_ref, kv_ref, qp_ref, qpos_ref,
+    out_t_ref, lse_ref, out_ref,
+    kv_t, qz, acc, m_ref, l_ref,
+):
+    i = pl.program_id(0)
+    half = 2 * qp_ref.shape[1]
+    n = chunks * half
+    core = core_ref[0]
+
+    @pl.when(i == 0)
+    def _():
+        for c in range(kv_ref.shape[0] // 512):
+            at = slice(c * 512, (c + 1) * 512)
+            kv_t[:, at] = kv_ref[at, :].astype(F32).T.astype(BF16)
+
+    low = low_lanes((half // 2, 128))
+    for c in range(chunks):
+        a, b = spread(qp_ref[c], low, False)
+        qz[c * half : c * half + half // 2] = a
+        qz[c * half + half // 2 : (c + 1) * half] = b
+    qpos = qpos_ref[...] + core * half
+    first, last = query_ends(i, chunks, half, core)
+    start, lo, f0, f1, hi = block_bounds(len_ref, items, qpos, first, last, key_block)
+    acc[...] = jnp.zeros_like(acc)
+    m_ref[...] = jnp.full_like(m_ref, MASKED)
+    l_ref[...] = jnp.zeros_like(l_ref)
+
+    def step(j, masked):
+        at = pl.ds(pl.multiple_of(j * key_block, key_block), key_block)
+        s = nt_dot(kv_ref[at, :], qz[...]) * LOG2E
+        if masked:
+            kpos = j * key_block + lax.broadcasted_iota(jnp.int32, (key_block, 1), 0)
+            s = jnp.where((kpos >= start) & (kpos <= qpos), s, MASKED)
+        m_old = m_ref[...]
+        m_new = jnp.maximum(m_old, jnp.max(s, axis=0, keepdims=True))
+        p = jnp.exp2(s - m_new)
+        alpha = jnp.exp2(m_old - m_new)
+        m_ref[...] = m_new
+        l_ref[...] = l_ref[...] * alpha + jnp.sum(p, axis=0, keepdims=True)
+        acc[...] = acc[...] * alpha + nn_dot(kv_t[64:, at], p.astype(BF16))
+
+    lax.fori_loop(lo, f0, lambda j, c: (step(j, True), c)[1], 0)
+    lax.fori_loop(f0, f1, lambda j, c: (step(j, False), c)[1], 0)
+    lax.fori_loop(f1, hi, lambda j, c: (step(j, True), c)[1], 0)
+    out_t = acc[...] / l_ref[...]
+    out_t_ref[...] = out_t
+    lse_ref[...] = m_ref[...] + jnp.log2(l_ref[...])
+    doubled = jnp.concatenate([out_t, out_t], axis=0).T
+    for c in range(chunks):
+        a = doubled[c * half : c * half + half // 2]
+        b = doubled[c * half + half // 2 : (c + 1) * half]
+        out_ref[c] = jnp.where(low, a, b).astype(BF16)
+
+
+def mix(lengths, core, kv, qp, qpos, chunks=4, key_block=768):
+    total = kv.shape[0]
+    n_src, quarter = qp.shape[0], qp.shape[1]
+    half = 2 * quarter
+    n = chunks * half
+    whole = lambda i, *_: (0, 0)
+    return pl.pallas_call(
+        functools.partial(mix_kernel, lengths.shape[0], chunks, key_block),
+        grid_spec=pltpu.PrefetchScalarGridSpec(
+            num_scalar_prefetch=2,
+            grid=(n_src // chunks,),
+            in_specs=[
+                pl.BlockSpec((total, 128), whole),
+                pl.BlockSpec((chunks, quarter, 128), lambda i, *_: (i, 0, 0)),
+                pl.BlockSpec((1, n), lambda i, *_: (0, i)),
+            ],
+            out_specs=[
+                pl.BlockSpec((64, n), lambda i, *_: (0, i)),
+                pl.BlockSpec((1, n), lambda i, *_: (0, i)),
+                pl.BlockSpec((chunks, quarter, 128), lambda i, *_: (i, 0, 0)),
+            ],
+            scratch_shapes=[
+                pltpu.VMEM((128, total), BF16),
+                pltpu.VMEM((n, 128), BF16),
+                pltpu.VMEM((64, n), F32),
+                pltpu.VMEM((1, n), F32),
+                pltpu.VMEM((1, n), F32),
+            ],
+        ),
+        out_shape=[
+            jax.ShapeDtypeStruct((64, n_src * half), F32),
+            jax.ShapeDtypeStruct((1, n_src * half), F32),
+            jax.ShapeDtypeStruct((n_src, quarter, 128), BF16),
+        ],
+        compiler_params=pltpu.CompilerParams(vmem_limit_bytes=40 << 20),
+        name="mix",
+    )(lengths, core, kv, qp, qpos)
+
+
+def back_kernel(
+    items, chunks, key_block,
+    len_ref, core_ref, kv_ref, qp_ref, dp_ref, qpos_ref, out_t_ref, lse_ref,
+    dkv_ref, dq_ref,
+    kv_t, qd, dq_acc,
+):
+    i = pl.program_id(0)
+    half = 2 * qp_ref.shape[1]
+    n = chunks * half
+    core = core_ref[0]
+
+    @pl.when(i == 0)
+    def _():
+        for c in range(kv_ref.shape[0] // 512):
+            at = slice(c * 512, (c + 1) * 512)
+            kv_t[:, at] = kv_ref[at, :].astype(F32).T.astype(BF16)
+        dkv_ref[...] = jnp.zeros_like(dkv_ref)
+
+    low = low_lanes((half // 2, 128))
+    for c in range(chunks):
+        a, b = spread(qp_ref[c], low, False)
+        qd[c * half : c * half + half // 2] = a
+        qd[c * half + half // 2 : (c + 1) * half] = b
+        a, b = spread(dp_ref[c], low, True)
+        qd[n + c * half : n + c * half + half // 2] = a
+        qd[n + c * half + half // 2 : n + (c + 1) * half] = b
+    do_t = qd[n:, :].astype(F32).T[64:]
+    delta = jnp.sum(do_t * out_t_ref[...], axis=0, keepdims=True)
+    lse = lse_ref[...]
+    qpos = qpos_ref[...] + core * half
+    first, last = query_ends(i, chunks, half, core)
+    start, lo, f0, f1, hi = block_bounds(len_ref, items, qpos, first, last, key_block)
+    dq_acc[...] = jnp.zeros_like(dq_acc)
+
+    def step(j, masked):
+        at = pl.ds(pl.multiple_of(j * key_block, key_block), key_block)
+        both = nt_dot(kv_ref[at, :], qd[...])
+        s = both[:, :n] * LOG2E
+        if masked:
+            kpos = j * key_block + lax.broadcasted_iota(jnp.int32, (key_block, 1), 0)
+            s = jnp.where((kpos >= start) & (kpos <= qpos), s, MASKED)
+        p = jnp.exp2(s - lse)
+        ds = (p * (both[:, n:] - delta)).astype(BF16)
+        dq_acc[...] += nn_dot(kv_t[:64, at], ds)
+        dkv_ref[at, :] += nn_dot(ds, qd[:n, :]) + nn_dot(p.astype(BF16), qd[n:, :])
+
+    lax.fori_loop(lo, f0, lambda j, c: (step(j, True), c)[1], 0)
+    lax.fori_loop(f0, f1, lambda j, c: (step(j, False), c)[1], 0)
+    lax.fori_loop(f1, hi, lambda j, c: (step(j, True), c)[1], 0)
+    dq_t = dq_acc[...] * 0.125
+    doubled = jnp.concatenate([dq_t, dq_t], axis=0).T
+    for c in range(chunks):
+        a = doubled[c * half : c * half + half // 2]
+        b = doubled[c * half + half // 2 : (c + 1) * half]
+        dq_ref[c] = jnp.where(low, a, b).astype(BF16)
+
+
+def mix_back(lengths, core, kv, qp, dp, qpos, out_t, lse, chunks=4, key_block=768):
+    total = kv.shape[0]
+    n_src, quarter = qp.shape[0], qp.shape[1]
+    half = 2 * quarter
+    n = chunks * half
+    whole = lambda i, *_: (0, 0)
+    rows = lambda i, *_: (0, i)
+    blocks = pl.BlockSpec((chunks, quarter, 128), lambda i, *_: (i, 0, 0))
+    return pl.pallas_call(
+        functools.partial(back_kernel, lengths.shape[0], chunks, key_block),
+        grid_spec=pltpu.PrefetchScalarGridSpec(
+            num_scalar_prefetch=2,
+            grid=(n_src // chunks,),
+            in_specs=[
+                pl.BlockSpec((total, 128), whole),
+                blocks,
+                blocks,
+                pl.BlockSpec((1, n), rows),
+                pl.BlockSpec((64, n), rows),
+                pl.BlockSpec((1, n), rows),
+            ],
+            out_specs=[pl.BlockSpec((total, 128), whole), blocks],
+            scratch_shapes=[
+                pltpu.VMEM((128, total), BF16),
+                pltpu.VMEM((2 * n, 128), BF16),
+                pltpu.VMEM((64, n), F32),
+            ],
+        ),
+        out_shape=[
+            jax.ShapeDtypeStruct((total, 128), F32),
+            jax.ShapeDtypeStruct((n_src, quarter, 128), BF16),
+        ],
+        compiler_params=pltpu.CompilerParams(vmem_limit_bytes=48 << 20),
+        name="mix_back",
+    )(lengths, core, kv, qp, dp, qpos, out_t, lse)
+
+
+def packed_positions(n_src, half):
+    j = np.arange(n_src * half)
+    return ((j // half) * 2 * half + j % half).astype(np.int32)[None]
+
+
+MESH = pl.DeviceIdType.MESH
+ALL = ("blk", "grp")
+
+
+def place(index):
+    return {"blk": lax.div(index, 2), "grp": lax.rem(index, 2)}
+
+
+def head_of(index):
+    blk, grp = lax.div(index, 2), lax.rem(index, 2)
+    return lax.div(blk, 2) * 2 + grp, lax.rem(blk, 2)
+
+
+def own_index():
+    return lax.axis_index("blk") * 2 + lax.axis_index("grp")
+
+
+def greet_all(me, n):
+    barrier = pltpu.get_barrier_semaphore()
+
+    @pl.loop(1, n)
+    def _(i):
+        pl.semaphore_signal(barrier, inc=1, device_id=place(lax.rem(me + i, n)), device_id_type=MESH)
+
+    pl.semaphore_wait(barrier, n - 1)
+
+
+def remote(src, dst, send_sem, recv_sem, device):
+    return pltpu.make_async_remote_copy(
+        src_ref=src, dst_ref=dst, send_sem=send_sem, recv_sem=recv_sem, device_id=device, device_id_type=MESH
+    )
+
+
+def to_heads_kernel(n, kv_in, q_in, kv_out, q_out, send, recv, local, pair):
+    me = own_index()
+    head, core = head_of(me)
+    greet_all(me, n)
+
+    def copies(i, src):
+        other = lax.rem(me + i, n)
+        h, c = head_of(other)
+        kv_at = core if src is not me else c
+        return (
+            remote(kv_in.at[h, c], kv_out.at[src, kv_at], send.at[0, i], recv.at[0, src], place(other)),
+            remote(q_in.at[h, c], q_out.at[src], send.at[1, i], recv.at[1, src], place(other)),
+        )
+
+    @pl.loop(1, n)
+    def _(i):
+        for copy in copies(i, me):
+            copy.start()
+
+    own = (
+        pltpu.make_async_copy(kv_in.at[head, core], kv_out.at[me, core], local.at[0]),
+        pltpu.make_async_copy(q_in.at[head, core], q_out.at[me], local.at[1]),
+    )
+    for copy in own:
+        copy.start()
+    for copy in own:
+        copy.wait()
+
+    @pl.loop(1, n)
+    def _(i):
+        for copy in copies(i, lax.rem(me + i, n)):
+            copy.wait()
+
+    sibling = {"blk": lax.axis_index("blk") + 1 - 2 * core, "grp": lax.axis_index("grp")}
+    swap = remote(kv_out.at[:, core], kv_out.at[:, core], pair.at[0], pair.at[1], sibling)
+    swap.start()
+    swap.wait()
+
+
+def to_heads(kv, q, n):
+    half = kv.shape[2]
+    anywhere = pl.BlockSpec(memory_space=pl.ANY)
+    return pl.pallas_call(
+        functools.partial(to_heads_kernel, n),
+        in_specs=[anywhere] * 2,
+        out_specs=[anywhere] * 2,
+        out_shape=[
+            jax.ShapeDtypeStruct((n, 2, half, 128), BF16),
+            jax.ShapeDtypeStruct((n, half // 2, 128), BF16),
+        ],
+        scratch_shapes=[
+            pltpu.SemaphoreType.DMA((2, n)),
+            pltpu.SemaphoreType.DMA((2, n)),
+            pltpu.SemaphoreType.DMA((2,)),
+            pltpu.SemaphoreType.DMA((2,)),
+        ],
+        compiler_params=pltpu.CompilerParams(collective_id=0, has_side_effects=True),
+        name="to_heads",
+    )(kv, q)
+
+
+def exchange_kernel(n, x_in, x_out, send, recv, local):
+    me = own_index()
+    greet_all(me, n)
+
+    def copy_with(i, src):
+        other = lax.rem(me + i, n)
+        return remote(x_in.at[other], x_out.at[src], send.at[i], recv.at[src], place(other))
+
+    @pl.loop(1, n)
+    def _(i):
+        copy_with(i, me).start()
+
+    own = pltpu.make_async_copy(x_in.at[me], x_out.at[me], local)
+    own.start()
+    own.wait()
+
+    @pl.loop(1, n)
+    def _(i):
+        copy_with(i, lax.rem(me + i, n)).wait()
+
+
+def exchange(x, n, collective_id):
+    anywhere = pl.BlockSpec(memory_space=pl.ANY)
+    return pl.pallas_call(
+        functools.partial(exchange_kernel, n),
+        in_specs=[anywhere],
+        out_specs=anywhere,
+        out_shape=jax.ShapeDtypeStruct(x.shape, x.dtype),
+        scratch_shapes=[
+            pltpu.SemaphoreType.DMA((n,)),
+            pltpu.SemaphoreType.DMA((n,)),
+            pltpu.SemaphoreType.DMA,
+        ],
+        compiler_params=pltpu.CompilerParams(collective_id=collective_id, has_side_effects=True),
+        name="exchange",
+    )(x)
+
+
+def from_heads_kernel(n, dkv_in, dq_in, dkv_out, dq_out, theirs, total, send, recv, local, pair):
+    me = own_index()
+    head, core = head_of(me)
+    greet_all(me, n)
+    sibling = {"blk": lax.axis_index("blk") + 1 - 2 * core, "grp": lax.axis_index("grp")}
+    swap = remote(dkv_in.at[:, 1 - core], theirs, pair.at[0], pair.at[1], sibling)
+    swap.start()
+
+    def dq_copy(i, src):
+        other = lax.rem(me + i, n)
+        return remote(dq_in.at[other], dq_out.at[src], send.at[1, i], recv.at[1, src], place(other))
+
+    def dkv_copy(i, src):
+        other = lax.rem(me + i, n)
+        return remote(total.at[other], dkv_out.at[src], send.at[0, i], recv.at[0, src], place(other))
+
+    @pl.loop(1, n)
+    def _(i):
+        dq_copy(i, me).start()
+
+    own_q = pltpu.make_async_copy(dq_in.at[me], dq_out.at[me], local.at[1])
+    own_q.start()
+    swap.wait()
+
+    def add(j):
+        total[j] = (dkv_in[j, core] + theirs[j]).astype(BF16)
+
+    @pl.loop(1, n)
+    def _(i):
+        add(lax.rem(me + i, n))
+        dkv_copy(i, me).start()
+
+    add(me)
+    own = pltpu.make_async_copy(total.at[me], dkv_out.at[me], local.at[0])
+    own.start()
+    own.wait()
+    own_q.wait()
+
+    @pl.loop(1, n)
+    def _(i):
+        src = lax.rem(me + i, n)
+        dkv_copy(i, src).wait()
+        dq_copy(i, src).wait()
+
+
+def from_heads(dkv, dq, n):
+    half = dkv.shape[2]
+    anywhere = pl.BlockSpec(memory_space=pl.ANY)
+    return pl.pallas_call(
+        functools.partial(from_heads_kernel, n),
+        in_specs=[pl.BlockSpec(memory_space=pltpu.VMEM), anywhere],
+        out_specs=[anywhere] * 2,
+        out_shape=[
+            jax.ShapeDtypeStruct((n, half, 128), BF16),
+            jax.ShapeDtypeStruct(dq.shape, BF16),
+        ],
+        scratch_shapes=[
+            pltpu.VMEM((n, half, 128), F32),
+            pltpu.VMEM((n, half, 128), BF16),
+            pltpu.SemaphoreType.DMA((2, n)),
+            pltpu.SemaphoreType.DMA((2, n)),
+            pltpu.SemaphoreType.DMA((2,)),
+            pltpu.SemaphoreType.DMA((2,)),
+        ],
+        compiler_params=pltpu.CompilerParams(
+            collective_id=1, has_side_effects=True, vmem_limit_bytes=24 << 20
+        ),
+        name="from_heads",
+    )(dkv, dq)
+
+
+def flipped(x, axis):
+    if axis == "x":
+        return lax.ppermute(x, "grp", [(0, 1), (1, 0)])
+    bit = {"core": 1, "y": 2, "z0": 4, "z1": 8}[axis]
+    return lax.ppermute(x, "blk", [(i, i ^ bit) for i in range(lax.axis_size("blk"))])
+
+
+def bit_of(axis):
+    if axis == "x":
+        return lax.axis_index("grp")
+    bit = {"core": 1, "y": 2, "z0": 4, "z1": 8}[axis]
+    return lax.rem(lax.div(lax.axis_index("blk"), bit), 2)
+
+
+def pick(x, dim, index):
+    return lax.dynamic_index_in_dim(x, index, dim, keepdims=False)
+
+
+def scattered_sum(x, order):
+    dims = ["z1", "z0", "y", "x"]
+    total = x
+    for axis in order:
+        mine, at = bit_of(axis), dims.index(axis)
+        got = flipped(pick(total, at, 1 - mine), axis)
+        total = pick(total, at, mine).astype(F32) + got.astype(F32)
+        dims.remove(axis)
+        if dims:
+            total = total.astype(BF16)
+    return total
+
+
+def halves(x, core, per_device):
+    parts = x.reshape(x.shape[0], 8, 2, 2 * per_device)
+    take = lambda c: pick(parts, 2, c).reshape(x.shape[0], 16 * per_device)
+    return take(core), take(1 - core)
+
+
+def both(x):
+    return jnp.concatenate([x, flipped(x, "core")], axis=0)
+
+
+def row_gradients(left, right, core, per_device):
+    mine, others = halves(left, core, per_device)
+    lefts = jnp.concatenate([mine, flipped(others, "core")], axis=0)
+    grad = left_dot(lefts, right).astype(BF16)
+    return grad.reshape(2, 2, 2, 2, per_device, grad.shape[1])
+
+
+def unpacked(blocks, rows):
+    parts = blocks.reshape(8, 2, 2, rows // 4, 2, 64)
+    return parts.transpose(1, 4, 3, 0, 2, 5).reshape(rows, 1024)
+
+
+def shards_heads(
+    frames, lengths, norm1_gain, w_query, w_key, w_value, w_out, norm2_gain, w_up, b_up, w_down, b_down, cotangent
+):
+    rows, width = frames.shape
+    n = lax.axis_size("blk") * lax.axis_size("grp")
+    half = rows // 2
+    core = bit_of("core")
+    core_word = core.astype(jnp.int32).reshape(1)
+    qpos = jnp.asarray(packed_positions(n, half))
+
+    kv_blocks, q_blocks, act1 = project_and_pack(frames, norm1_gain, w_query, w_key, w_value)
+    kv, q = to_heads(kv_blocks, q_blocks, n)
+    kv_rows = kv.reshape(n * rows, 128)
+    out_t, lse, out_blocks = mix(lengths, core_word, kv_rows, q, qpos)
+    mixed = unpacked(exchange(out_blocks, n, 2), rows)
+
+    middle = frames + jnp.dot(mixed, w_out, preferred_element_type=F32)
+    normed2, norm2_back = jax.vjp(rms_norm, middle, norm2_gain)
+    act2 = normed2.astype(BF16)
+    before = jnp.dot(act2, w_up, preferred_element_type=F32) + b_up
+    activated, gelu_back = jax.vjp(gelu_exact, before)
+    hidden = activated.astype(BF16)
+    layer_out = middle + jnp.dot(hidden, w_down, preferred_element_type=F32) + b_down
+    grad_low = cotangent.astype(BF16)
+    b_down_grad = jnp.sum(grad_low.astype(F32), axis=0)
+    grad_before = gelu_back(right_dot(grad_low, w_down))[0].astype(BF16)
+    b_up_grad = jnp.sum(grad_before.astype(F32), axis=0)
+    grad_mid_norm, norm2_gain_grad = norm2_back(right_dot(grad_before, w_up))
+    grad_middle = cotangent + grad_mid_norm
+    grad_attn = grad_middle.astype(BF16)
+    grad_mixed = right_dot(grad_attn, w_out).astype(BF16)
+
+    grad_blocks = exchange(to_blocks(grad_mixed), n, 3)
+    dkv, dq = mix_back(lengths, core_word, kv_rows, q, grad_blocks, qpos, out_t, lse)
+
+    grads_low = both(grad_low)
+    w_down_part = row_gradients(hidden, grads_low, core, 128)
+    w_up_part = row_gradients(act2, both(grad_before), core, 32)
+    w_out_part = row_gradients(mixed, both(grad_attn), core, 32)
+    w_down_grad = scattered_sum(w_down_part, ("x", "y", "z0", "z1"))
+    w_up_grad = scattered_sum(w_up_part, ("y", "x", "z0", "z1"))
+    w_out_grad = scattered_sum(w_out_part, ("x", "y", "z0", "z1"))
+
+    dkv_blocks, dq_blocks = from_heads(dkv.reshape(n, 2, half, 128), dq, n)
+    grad_queries = unpacked(dq_blocks, rows)
+    grad_kv = dkv_blocks.reshape(8, 2, 2, half, 2, 64).transpose(4, 1, 3, 0, 2, 5).reshape(2, rows, width)
+    grad_keys, grad_values = grad_kv[0], grad_kv[1]
+    grad_act1 = right_dot(grad_queries, w_query) + right_dot(grad_keys, w_key) + right_dot(grad_values, w_value)
+    unused_out, norm1_back = jax.vjp(rms_norm, frames, norm1_gain)
+    grad_frames_norm, norm1_gain_grad = norm1_back(grad_act1)
+    frames_grad = grad_middle + grad_frames_norm
+
+    qkv = both(jnp.concatenate([grad_queries, grad_keys, grad_values], axis=1))
+    qkv_part = row_gradients(act1, qkv, core, 32)
+    w_query_grad = scattered_sum(qkv_part[..., :width], ("x", "y", "z0", "z1"))
+    w_key_grad = scattered_sum(qkv_part[..., width : 2 * width], ("y", "x", "z0", "z1"))
+    w_value_grad = scattered_sum(qkv_part[..., 2 * width :], ("x", "y", "z0", "z1"))
+
+    small = jnp.concatenate(
+        [
+            norm1_gain_grad.reshape(n, -1),
+            norm2_gain_grad.reshape(n, -1),
+            b_down_grad.reshape(n, -1),
+            b_up_grad.reshape(n, -1),
+        ],
+        axis=1,
+    )
+    part = width // n
+    small = jnp.pad(small, ((0, 0), (0, 1024 - small.shape[1]))).reshape(n, 8, 128)
+    small = jnp.sum(exchange(small, n, 4), axis=0).reshape(1024)
+    return (
+        layer_out,
+        frames_grad,
+        small[:part],
+        w_query_grad,
+        w_key_grad,
+        w_value_grad,
+        w_out_grad,
+        small[part : 2 * part],
+        w_up_grad,
+        small[3 * part : 3 * part + b_up.shape[0] // n],
+        w_down_grad,
+        small[2 * part : 3 * part],
+    )
+
+
+def to_blocks(grad_mixed):
+    rows = grad_mixed.shape[0]
+    parts = grad_mixed.reshape(2, 2, rows // 4, 8, 2, 64)
+    return parts.transpose(3, 0, 4, 2, 1, 5).reshape(32, rows // 4, 128)
+
+
+def solution(mesh):
+    if mesh.shape["blk"] != 16 or mesh.shape["grp"] != 2:
+        return solution_ring(mesh)
+    split = P(ALL, None)
+    return jax.shard_map(
+        shards_heads,
+        mesh=mesh,
+        in_specs=(split, P(), P(), P(), P(), P(), P(), P(), P(), P(), P(), P(), split),
+        out_specs=(split, split, P(ALL), split, split, split, split, P(ALL), split, P(ALL), split, P(ALL)),
+        check_vma=False,
+    )

time: 2590 us -> 485 us (0.19)
  waiting for transfers between devices: 1360 us -> 111 us
  matrix products: 397 us -> 55.5 us
  local copies, waits for them, and re-layouts: 313 us -> 90.2 us
  starting transfers between devices: 244 us -> 30.6 us
  Pallas kernels: 0 us -> 167 us
  other arithmetic: 151 us -> 20.1 us
  blocking collectives: 64.1 us -> 0 us
  loops' own time: 34.8 us -> 0 us
    reduce_scatter x6 -> x0, waiting for transfers between devices: 1210 us -> none  [the longest x1 362 us: shards(): lax.psum_scatter(w_down_grad, ('blk', 'grp'), scatter_dimension=0, tiled=...]
    dot_general x114 -> x3, matrix products: 346 us -> 13.6 us  [the longest x1 6.33 us: shards_heads(): jnp.dot(hidden, w_down, preferred_element_type=F32)]
    ppermute x44 -> x32, starting transfers between devices: 243 us -> 30.6 us  [the longest x26 23.9 us: flipped(): lax.ppermute(x, 'blk', [(i, i ^ bit) for i in range(lax.axis_size('blk'))])]
    pallas_call x0 -> x8, Pallas kernels: none -> 167 us  [the longest x3 49.6 us: exchange(): pl.pallas_call(functools.partial(exchange_kernel, n), in_specs=[anywhere]...]
    dynamic_slice x105 -> x14, local copies, waits for them, and re-layouts: 139 us -> 19.9 us  [pick(): return lax.dynamic_index_in_dim(x, index, dim, keepdims=False)]
    dynamic_update_slice x44 -> x0, local copies, waits for them, and re-layouts: 84.9 us -> none  [shards(): lax.scan(cycle_step, (block_keys, block_values), None, length=span)]
    convert_element_type x48 -> x21, other arithmetic: 83.5 us -> 10.1 us  [the longest x1 4.51 us: shards_heads(): hidden = activated.astype(BF16)]
    while x260 -> x0, local copies, waits for them, and re-layouts: 66.7 us -> none
  transfers between devices with their start and end apart: 52 -> 32, of which waited for: 41 -> 15; matrix products, arithmetic and copies ran while one was open for 7% -> 30% of each run, Pallas kernels for 0% -> 35%
where the time goes in v1:
time: 485 us; the launch traced here: 476 us
  Pallas kernels  167 us (34%)
  waiting for transfers between devices  111 us (23%)
  local copies, waits for them, and re-layouts  90.2 us (19%)
  matrix products  55.5 us (11%)
  starting transfers between devices  30.6 us (6%)
  other arithmetic  20.1 us (4%)
    ppermute x26, waiting for transfers between devices, flipped(): lax.ppermute(x, 'blk', [(i, i ^ bit) for i in range(lax.axis_size('blk'))])  66.3 us
    pallas_call x3, Pallas kernels, exchange(): pl.pallas_call(functools.partial(exchange_kernel, n), in_specs=[anywhere]...  49.6 us
    ppermute x6, waiting for transfers between devices, flipped(): return lax.ppermute(x, 'grp', [(0, 1), (1, 0)])  44.8 us
    pallas_call x1, Pallas kernels, mix_back(): pl.pallas_call(functools.partial(back_kernel, lengths.shape[0], chunks, k...  33.7 us
    pallas_call x1, Pallas kernels, to_heads(): pl.pallas_call(functools.partial(to_heads_kernel, n), in_specs=[anywhere]...  29.8 us
    dot_general x6, matrix products, right_dot(): lax.dot_general(left, right, (((1,), (1,)), ((), ())), preferred_element_...  28.8 us
    pallas_call x1, Pallas kernels, from_heads(): pl.pallas_call(functools.partial(from_heads_kernel, n), in_specs=[pl.Bloc...  28.1 us
    ppermute x26, starting transfers between devices, flipped(): lax.ppermute(x, 'blk', [(i, i ^ bit) for i in range(lax.axis_size('blk'))])  23.9 us
  transfers between devices with their start and end apart: 32, of which 15 were waited for; matrix products, arithmetic and copies ran while one was open for 30% of the time, Pallas kernels for 35%

profile of v1, /device:TPU:0, one launch (start us, length us, event | category | flops | bytes accessed | tf_op | source)
XLA Modules:
  0.0 476.2 jit_solution(18036443872025536226)
XLA Ops:
  14.7 29.8 %to_heads.1 = (bf16[32,2,96,128]{3,2,1,0:T(8,128)(2,1)}, bf16[32,48,128]{2,1,0:T(8,128)(2,1)}) custom-call(bf16[16,2,96,128]{3,2,1,0:T(8,128)(2,1)} %copy-done.17, bf16[16,2,48,128]{3,2,1,0:T(8,128)(2,1)} %copy-done.21), custom_call_target="tpu_custom_call" | custom-call | tf_op jit(solution)/shard_map/to_heads/pallas_call | solution.py:709
  47.0 22.2 %mix.1 = (f32[64,3072]{1,0:T(8,128)S(1)}, f32[1,3072]{1,0:T(1,128)S(1)}, bf16[32,48,128]{2,1,0:T(8,128)(2,1)S(1)}) custom-call(s32[12]{0:T(128)S(1)} %copy-done.26, s32[1]{0:T(128)} %bitcast.core_ref, bf16[6144,128]{1,0:T(8,128)(2,1)S(1)} %bitcast.198, bf16[32,48,128]{2,1,0:T(8,128)(2,1)S(1)} %copy-done.13, s32[1,3072]{1,0:T(1,128)S(1)} %copy-done.23), custom_call_target="tpu_custom_call" | custom-call | tf_op jit(solution)/shard_map/mix/pallas_call | solution.py:502
  70.8 19.2 %exchange.3 = bf16[32,48,128]{2,1,0:T(8,128)(2,1)} custom-call(bf16[32,48,128]{2,1,0:T(8,128)(2,1)} %copy-done.20), custom_call_target="tpu_custom_call" | custom-call | tf_op jit(solution)/shard_map/exchange/pallas_call | solution.py:751
  102.4 5.5 %convolution_add_fusion = f32[192,4096]{1,0:T(8,128)S(1)} fusion(bf16[192,1024]{1,0:T(8,128)(2,1)S(1)} %multiply_convert_fusion.1, bf16[1024,4096]{1,0:T(8,128)(2,1)} %param.22, f32[4096]{0:T(1024)S(1)} %copy-done.47), kind=kOutput, calls=%fused_computation.1 | convolution fusion | flops 1611399168 | bytes 11943936 | tf_op jit(solution)/shard_map/dot_general | solution.py:909
  108.0 13.4 %convert_reduce_fusion = (f32[4096]{0:T(1024)S(1)}, bf16[192,4096]{1,0:T(8,128)(2,1)}, f32[192,4096]{1,0:T(8,128)}) fusion(f32[192,4096]{1,0:T(8,128)S(1)} %convolution_add_fusion, bf16[192,1024]{1,0:T(8,128)(2,1)} %get-tuple-element.43, bf16[4096,1024]{1,0:T(8,128)(2,1)S(1)} %bitcast.232), kind=kOutput, calls=%fused_computation.13 | convolution fusion | flops 1668804608 | bytes 16662528 | tf_op jit(solution)/shard_map/dot_general | solution.py:76
  121.6 4.5 multiply_reduce_fusion
  131.9 4.5 multiply_convert_fusion
  136.4 4.2 reshape.253
  140.6 12.2 %dynamic-slice_reduce_fusion.1 = (bf16[192,8,256]{2,1,0:T(8,128)(2,1)}, bf16[192,8,256]{2,1,0:T(8,128)(2,1)S(1)}) fusion(bf16[192,8,2,256]{3,2,1,0:T(2,128)(2,1)} %reshape.253, s32[]{:T(128)S(6)} %select_n.91, s32[]{:T(128)S(6)} %select_n.92), kind=kLoop, calls=%fused_computation.48 | loop fusion | bytes 3145736 | tf_op jit(solution)/shard_map/jit(dynamic_index_in_dim)/dynamic_slice | solution.py:852
  157.0 6.3 %fusion.23 = f32[192,1024]{1,0:T(8,128)} fusion(f32[192,1024]{1,0:T(8,128)S(1)} %copy-done.30, bf16[192,4096]{1,0:T(8,128)(2,1)S(1)} %copy-done.31, bf16[4096,1024]{1,0:T(8,128)(2,1)} %param.24, f32[1024]{0:T(1024)S(1)} %copy-done.48), kind=kOutput, calls=%fused_computation.54 | convolution fusion | flops 1611005952 | bytes 11538432 | tf_op jit(solution)/shard_map/dot_general | solution.py:912
  172.0 15.0 %exchange.4.dp_ref = bf16[32,48,128]{2,1,0:T(8,128)(2,1)} custom-call(bf16[32,48,128]{2,1,0:T(8,128)(2,1)} %reshape.231.x_in), custom_call_target="tpu_custom_call" | custom-call | tf_op jit(solution)/shard_map/exchange/pallas_call | solution.py:751
  189.2 33.7 %mix_back.1 = (f32[6144,128]{1,0:T(8,128)}, bf16[32,48,128]{2,1,0:T(8,128)(2,1)S(1)}) custom-call(s32[12]{0:T(128)S(1)} %copy-done.26, s32[1]{0:T(128)} %bitcast.core_ref, bf16[6144,128]{1,0:T(8,128)(2,1)S(1)} %bitcast.199, bf16[32,48,128]{2,1,0:T(8,128)(2,1)S(1)} %copy-done.14, bf16[32,48,128]{2,1,0:T(8,128)(2,1)S(1)} %copy-done.15, ...), custom_call_target="tpu_custom_call" | custom-call | tf_op jit(solution)/shard_map/mix_back/pallas_call | solution.py:600
  224.8 28.1 %from_heads.1 = (bf16[32,96,128]{2,1,0:T(8,128)(2,1)S(1)}, bf16[32,48,128]{2,1,0:T(8,128)(2,1)S(1)}) custom-call(f32[32,2,96,128]{3,2,1,0:T(8,128)S(1)} %bitcast.200, bf16[32,48,128]{2,1,0:T(8,128)(2,1)S(1)} %get-tuple-element.32.dq_in), custom_call_target="tpu_custom_call" | custom-call | tf_op jit(solution)/shard_map/from_heads/pallas_call | solution.py:814
  290.5 15.4 %exchange.5 = f32[32,8,128]{2,1,0:T(8,128)} custom-call(f32[32,8,128]{2,1,0:T(8,128)} %bitcast.223), custom_call_target="tpu_custom_call" | custom-call | tf_op jit(solution)/shard_map/exchange/pallas_call | solution.py:751
  315.1 3.7 convolution_convert_fusion.2
  319.5 5.9 %collective-permute-done.16 = bf16[2,2,2,32,1024]{4,3,0,1,2:T(8,128)(2,1)S(1)} collective-permute-done((bf16[2,2,2,32,1024]{4,3,0,1,2:T(8,128)(2,1)}, bf16[2,2,2,32,1024]{4,3,0,1,2:T(8,128)(2,1)S(1)}, u32[]{:S(2)}, u32[]{:S(2)}) %collective-permute-start.16) | collective-permute-done | bytes 524320 | tf_op jit(solution)/shard_map/ppermute | solution.py:839
  348.5 4.3 convolution_convert_fusion
  353.9 31.4 %collective-permute-done.2 = bf16[2,2,2,32,1024]{4,3,0,1,2:T(8,128)(2,1)S(1)} collective-permute-done((bf16[2,2,2,32,1024]{4,3,0,1,2:T(8,128)(2,1)S(1)}, bf16[2,2,2,32,1024]{4,3,0,1,2:T(8,128)(2,1)S(1)}, u32[]{:S(2)}, u32[]{:S(2)}) %collective-permute-start.2) | collective-permute-done | bytes 524320 | tf_op jit(solution)/shard_map/ppermute | solution.py:839
  389.6 6.9 %collective-permute-done.10 = bf16[2,2,2,32,1024]{4,3,0,1,2:T(8,128)(2,1)S(1)} collective-permute-done((bf16[2,2,2,32,1024]{4,3,0,1,2:T(8,128)(2,1)S(1)}, bf16[2,2,2,32,1024]{4,3,0,1,2:T(8,128)(2,1)S(1)}, u32[]{:S(2)}, u32[]{:S(2)}) %collective-permute-start.10) | collective-permute-done | bytes 524320 | tf_op jit(solution)/shard_map/ppermute | solution.py:839
  399.0 11.3 %collective-permute-done.3 = bf16[2,2,32,1024]{3,2,0,1:T(8,128)(2,1)S(1)} collective-permute-done((bf16[2,2,32,1024]{3,2,0,1:T(8,128)(2,1)S(1)}, bf16[2,2,32,1024]{3,2,0,1:T(8,128)(2,1)S(1)}, u32[]{:S(2)}, u32[]{:S(2)}) %collective-permute-start.3) | collective-permute-done | bytes 262176 | tf_op jit(solution)/shard_map/ppermute | solution.py:841
  425.3 13.8 %collective-permute-done.29 = bf16[2,2,128,1024]{3,2,0,1:T(8,128)(2,1)S(1)} collective-permute-done((bf16[2,2,128,1024]{3,2,0,1:T(8,128)(2,1)S(1)}, bf16[2,2,128,1024]{3,2,0,1:T(8,128)(2,1)S(1)}, u32[]{:S(2)}, u32[]{:S(2)}) %collective-permute-start.29) | collective-permute-done | bytes 1048608 | tf_op jit(solution)/shard_map/ppermute | solution.py:841
  442.7 13.3 %collective-permute-done.30 = bf16[2,128,1024]{2,1,0:T(8,128)(2,1)S(1)} collective-permute-done((bf16[2,128,1024]{2,1,0:T(8,128)(2,1)S(1)}, bf16[2,128,1024]{2,1,0:T(8,128)(2,1)S(1)}, u32[]{:S(2)}, u32[]{:S(2)}) %collective-permute-start.30) | collective-permute-done | bytes 524320 | tf_op jit(solution)/shard_map/ppermute | solution.py:841
  456.3 7.6 %collective-permute-done.24 = bf16[2,32,4096]{2,1,0:T(8,128)(2,1)S(1)} collective-permute-done((bf16[2,32,4096]{2,1,0:T(8,128)(2,1)S(1)}, bf16[2,32,4096]{2,1,0:T(8,128)(2,1)S(1)}, u32[]{:S(2)}, u32[]{:S(2)}) %collective-permute-start.24) | collective-permute-done | bytes 524320 | tf_op jit(solution)/shard_map/ppermute | solution.py:841
  464.8 7.3 %collective-permute-done.31 = bf16[128,1024]{1,0:T(8,128)(2,1)S(1)} collective-permute-done((bf16[128,1024]{1,0:T(8,128)(2,1)S(1)}, bf16[128,1024]{1,0:T(8,128)(2,1)S(1)}, u32[]{:S(2)}, u32[]{:S(2)}) %collective-permute-start.31) | collective-permute-done | bytes 262176 | tf_op jit(solution)/shard_map/ppermute | solution.py:841
  (271 shorter events, 154.5 us)
Async XLA Ops:
  2.8 311.8 %collective-permute-start.27 = (bf16[192,1024]{1,0:T(8,128)(2,1)}, bf16[192,1024]{1,0:T(8,128)(2,1)}, u32[]{:S(2)}, u32[]{:S(2)}) collective-permute-start(bf16[192,1024]{1,0:T(8,128)(2,1)} %get-tuple-element.43), channel_id=1, source_target_pairs={{0,2},{2,0},{4,6},{6,4},{8,10},{10,8},{12,14},{14,12},{16,18},{18,... | collective-permute-start | bytes 1179656 | tf_op jit(solution)/shard_map/ppermute | solution.py:841
  121.4 227.1 %collective-permute-start.21 = (bf16[192,4096]{1,0:T(8,128)(2,1)}, bf16[192,4096]{1,0:T(8,128)(2,1)}, u32[]{:S(2)}, u32[]{:S(2)}) collective-permute-start(bf16[192,4096]{1,0:T(8,128)(2,1)} %get-tuple-element.45), channel_id=1, source_target_pairs={{0,2},{2,0},{4,6},{6,4},{8,10},{10,8},{12,14},{14,12},{16,18},{18,... | collective-permute-start | bytes 4718600 | tf_op jit(solution)/shard_map/ppermute | solution.py:841
  127.4 180.8 %collective-permute-start.15 = (bf16[192,1024]{1,0:T(8,128)(2,1)}, bf16[192,1024]{1,0:T(8,128)(2,1)}, u32[]{:S(2)}, u32[]{:S(2)}) collective-permute-start(bf16[192,1024]{1,0:T(8,128)(2,1)} %get-tuple-element.47), channel_id=1, source_target_pairs={{0,2},{2,0},{4,6},{6,4},{8,10},{10,8},{12,14},{14,12},{16,18},{18,... | collective-permute-start | bytes 1179656 | tf_op jit(solution)/shard_map/ppermute | solution.py:841
  131.7 176.3 %collective-permute-start.14 = (bf16[192,512]{0,1:T(8,128)(2,1)}, bf16[192,512]{0,1:T(8,128)(2,1)}, u32[]{:S(2)}, u32[]{:S(2)}) collective-permute-start(bf16[192,512]{0,1:T(8,128)(2,1)} %bitcast.224), channel_id=1, source_target_pairs={{0,2},{2,0},{4,6},{6,4},{8,10},{10,8},{12,14},{14,12},{16,18},{18,... | collective-permute-start | bytes 589832 | tf_op jit(solution)/shard_map/ppermute | solution.py:841
  153.9 160.7 %collective-permute-start.26 = (bf16[192,2048]{1,0:T(8,128)(2,1)}, bf16[192,2048]{1,0:T(8,128)(2,1)}, u32[]{:S(2)}, u32[]{:S(2)}) collective-permute-start(bf16[192,2048]{1,0:T(8,128)(2,1)} %bitcast.105), channel_id=1, source_target_pairs={{0,2},{2,0},{4,6},{6,4},{8,10},{10,8},{12,14},{14,12},{16,18},{18,... | collective-permute-start | bytes 2359304 | tf_op jit(solution)/shard_map/ppermute | solution.py:841
  308.0 21.5 %collective-permute-start.1 = (bf16[192,3072]{1,0:T(8,128)(2,1)}, bf16[192,3072]{1,0:T(8,128)(2,1)}, u32[]{:S(2)}, u32[]{:S(2)}) collective-permute-start(bf16[192,3072]{1,0:T(8,128)(2,1)} %pad_maximum_fusion), channel_id=1, source_target_pairs={{0,2},{2,0},{4,6},{6,4},{8,10},{10,8},{12,14},{14,12},{16,18},{18,... | collective-permute-start | bytes 3538952 | tf_op jit(solution)/shard_map/ppermute | solution.py:841
  311.1 14.3 %collective-permute-start.16 = (bf16[2,2,2,32,1024]{4,3,0,1,2:T(8,128)(2,1)}, bf16[2,2,2,32,1024]{4,3,0,1,2:T(8,128)(2,1)S(1)}, u32[]{:S(2)}, u32[]{:S(2)}) collective-permute-start(bf16[2,2,2,32,1024]{4,3,0,1,2:T(8,128)(2,1)} %bitcast.197), channel_id=1, source_target_pairs={{0,1},{1,0},{2,3},{3,2},{4,5},{5,4},{6,7},{7,6},{8,9},{9,8},{10,11... | collective-permute-start | bytes 1572872 | tf_op jit(solution)/shard_map/ppermute | solution.py:839
  314.5 12.8 %collective-permute-start = (bf16[192,512]{0,1:T(8,128)(2,1)}, bf16[192,512]{0,1:T(8,128)(2,1)S(1)}, u32[]{:S(2)}, u32[]{:S(2)}) collective-permute-start(bf16[192,512]{0,1:T(8,128)(2,1)} %bitcast.14), channel_id=1, source_target_pairs={{0,2},{2,0},{4,6},{6,4},{8,10},{10,8},{12,14},{14,12},{16,18},{18,... | collective-permute-start | bytes 589832 | tf_op jit(solution)/shard_map/ppermute | solution.py:841
  314.6 33.5 %collective-permute-start.20 = (bf16[192,512]{0,1:T(8,128)(2,1)}, bf16[192,512]{0,1:T(8,128)(2,1)S(1)}, u32[]{:S(2)}, u32[]{:S(2)}) collective-permute-start(bf16[192,512]{0,1:T(8,128)(2,1)} %bitcast.55), channel_id=1, source_target_pairs={{0,2},{2,0},{4,6},{6,4},{8,10},{10,8},{12,14},{14,12},{16,18},{18,... | collective-permute-start | bytes 589832 | tf_op jit(solution)/shard_map/ppermute | solution.py:841
  325.5 92.0 %collective-permute-start.28 = (bf16[2,2,2,128,1024]{4,3,0,1,2:T(8,128)(2,1)S(1)}, bf16[2,2,2,128,1024]{4,3,0,1,2:T(8,128)(2,1)S(1)}, u32[]{:S(2)}, u32[]{:S(2)}) collective-permute-start(bf16[2,2,2,128,1024]{4,3,0,1,2:T(8,128)(2,1)S(1)} %bitcast.214), channel_id=1, source_target_pairs={{0,1},{1,0},{2,3},{3,2},{4,5},{5,4},{6,7},{7,6},{8,9},{9,8},{10,11... | collective-permute-start | bytes 6291464 | tf_op jit(solution)/shard_map/ppermute | solution.py:839
  333.2 52.1 %collective-permute-start.2 = (bf16[2,2,2,32,1024]{4,3,0,1,2:T(8,128)(2,1)S(1)}, bf16[2,2,2,32,1024]{4,3,0,1,2:T(8,128)(2,1)S(1)}, u32[]{:S(2)}, u32[]{:S(2)}) collective-permute-start(bf16[2,2,2,32,1024]{4,3,0,1,2:T(8,128)(2,1)S(1)} %bitcast.220), channel_id=1, source_target_pairs={{0,1},{1,0},{2,3},{3,2},{4,5},{5,4},{6,7},{7,6},{8,9},{9,8},{10,11... | collective-permute-start | bytes 1572872 | tf_op jit(solution)/shard_map/ppermute | solution.py:839
  345.7 42.0 %collective-permute-start.6 = (bf16[2,2,2,32,1024]{4,3,0,1,2:T(8,128)(2,1)S(1)}, bf16[2,2,2,32,1024]{4,3,0,1,2:T(8,128)(2,1)S(1)}, u32[]{:S(2)}, u32[]{:S(2)}) collective-permute-start(bf16[2,2,2,32,1024]{4,3,0,1,2:T(8,128)(2,1)S(1)} %bitcast.222), channel_id=1, source_target_pairs={{0,4},{2,6},{4,0},{6,2},{8,12},{10,14},{12,8},{14,10},{16,20},{18,... | collective-permute-start | bytes 1572872 | tf_op jit(solution)/shard_map/ppermute | solution.py:841
  348.1 48.4 %collective-permute-start.10 = (bf16[2,2,2,32,1024]{4,3,0,1,2:T(8,128)(2,1)S(1)}, bf16[2,2,2,32,1024]{4,3,0,1,2:T(8,128)(2,1)S(1)}, u32[]{:S(2)}, u32[]{:S(2)}) collective-permute-start(bf16[2,2,2,32,1024]{4,3,0,1,2:T(8,128)(2,1)S(1)} %bitcast.221), channel_id=1, source_target_pairs={{0,1},{1,0},{2,3},{3,2},{4,5},{5,4},{6,7},{7,6},{8,9},{9,8},{10,11... | collective-permute-start | bytes 1572872 | tf_op jit(solution)/shard_map/ppermute | solution.py:839
  353.6 66.2 %collective-permute-start.22 = (bf16[2,2,2,32,4096]{4,3,0,1,2:T(8,128)(2,1)S(1)}, bf16[2,2,2,32,4096]{4,3,0,1,2:T(8,128)(2,1)S(1)}, u32[]{:S(2)}, u32[]{:S(2)}) collective-permute-start(bf16[2,2,2,32,4096]{4,3,0,1,2:T(8,128)(2,1)S(1)} %bitcast.215), channel_id=1, source_target_pairs={{0,4},{2,6},{4,0},{6,2},{8,12},{10,14},{12,8},{14,10},{16,20},{18,... | collective-permute-start | bytes 6291464 | tf_op jit(solution)/shard_map/ppermute | solution.py:841
  385.5 24.7 %collective-permute-start.3 = (bf16[2,2,32,1024]{3,2,0,1:T(8,128)(2,1)S(1)}, bf16[2,2,32,1024]{3,2,0,1:T(8,128)(2,1)S(1)}, u32[]{:S(2)}, u32[]{:S(2)}) collective-permute-start(bf16[2,2,32,1024]{3,2,0,1:T(8,128)(2,1)S(1)} %dynamic-slice_bitcast_fusion.9), channel_id=1, source_target_pairs={{0,4},{2,6},{4,0},{6,2},{8,12},{10,14},{12,8},{14,10},{16,20},{18,... | collective-permute-start | bytes 786440 | tf_op jit(solution)/shard_map/ppermute | solution.py:841
  388.0 22.8 %collective-permute-start.7 = (bf16[2,2,32,1024]{3,2,0,1:T(8,128)(2,1)S(1)}, bf16[2,2,32,1024]{3,2,0,1:T(8,128)(2,1)S(1)}, u32[]{:S(2)}, u32[]{:S(2)}) collective-permute-start(bf16[2,2,32,1024]{3,2,0,1:T(8,128)(2,1)S(1)} %dynamic-slice_bitcast_fusion.8), channel_id=1, source_target_pairs={{0,1},{1,0},{2,3},{3,2},{4,5},{5,4},{6,7},{7,6},{8,9},{9,8},{10,11... | collective-permute-start | bytes 786440 | tf_op jit(solution)/shard_map/ppermute | solution.py:839
  396.7 16.3 %collective-permute-start.11 = (bf16[2,2,32,1024]{3,2,0,1:T(8,128)(2,1)S(1)}, bf16[2,2,32,1024]{3,2,0,1:T(8,128)(2,1)S(1)}, u32[]{:S(2)}, u32[]{:S(2)}) collective-permute-start(bf16[2,2,32,1024]{3,2,0,1:T(8,128)(2,1)S(1)} %dynamic-slice_bitcast_fusion.7), channel_id=1, source_target_pairs={{0,4},{2,6},{4,0},{6,2},{8,12},{10,14},{12,8},{14,10},{16,20},{18,... | collective-permute-start | bytes 786440 | tf_op jit(solution)/shard_map/ppermute | solution.py:841
  418.8 20.2 %collective-permute-start.29 = (bf16[2,2,128,1024]{3,2,0,1:T(8,128)(2,1)S(1)}, bf16[2,2,128,1024]{3,2,0,1:T(8,128)(2,1)S(1)}, u32[]{:S(2)}, u32[]{:S(2)}) collective-permute-start(bf16[2,2,128,1024]{3,2,0,1:T(8,128)(2,1)S(1)} %dynamic-slice_bitcast_fusion), channel_id=1, source_target_pairs={{0,4},{2,6},{4,0},{6,2},{8,12},{10,14},{12,8},{14,10},{16,20},{18,... | collective-permute-start | bytes 3145736 | tf_op jit(solution)/shard_map/ppermute | solution.py:841
  420.7 19.7 %collective-permute-start.23 = (bf16[2,2,32,4096]{3,2,0,1:T(8,128)(2,1)S(1)}, bf16[2,2,32,4096]{3,2,0,1:T(8,128)(2,1)S(1)}, u32[]{:S(2)}, u32[]{:S(2)}) collective-permute-start(bf16[2,2,32,4096]{3,2,0,1:T(8,128)(2,1)S(1)} %dynamic-slice_bitcast_fusion.1), channel_id=1, source_target_pairs={{0,1},{1,0},{2,3},{3,2},{4,5},{5,4},{6,7},{7,6},{8,9},{9,8},{10,11... | collective-permute-start | bytes 3145736 | tf_op jit(solution)/shard_map/ppermute | solution.py:839
  421.5 20.4 %collective-permute-start.9 = (bf16[32,1024]{1,0:T(8,128)(2,1)S(1)}, bf16[32,1024]{1,0:T(8,128)(2,1)S(1)}, u32[]{:S(2)}, u32[]{:S(2)}) collective-permute-start(bf16[32,1024]{1,0:T(8,128)(2,1)S(1)} %dynamic-slice_bitcast_fusion.16), channel_id=1, source_target_pairs={{0,16},{2,18},{4,20},{6,22},{8,24},{10,26},{12,28},{14,30},{16,0},... | collective-permute-start | bytes 196616 | tf_op jit(solution)/shard_map/ppermute | solution.py:841
  423.7 40.5 %collective-permute-start.13 = (bf16[32,1024]{1,0:T(8,128)(2,1)S(1)}, bf16[32,1024]{1,0:T(8,128)(2,1)S(1)}, u32[]{:S(2)}, u32[]{:S(2)}) collective-permute-start(bf16[32,1024]{1,0:T(8,128)(2,1)S(1)} %dynamic-slice_bitcast_fusion.15), channel_id=1, source_target_pairs={{0,16},{2,18},{4,20},{6,22},{8,24},{10,26},{12,28},{14,30},{16,0},... | collective-permute-start | bytes 196616 | tf_op jit(solution)/shard_map/ppermute | solution.py:841
  439.5 16.5 %collective-permute-start.30 = (bf16[2,128,1024]{2,1,0:T(8,128)(2,1)S(1)}, bf16[2,128,1024]{2,1,0:T(8,128)(2,1)S(1)}, u32[]{:S(2)}, u32[]{:S(2)}) collective-permute-start(bf16[2,128,1024]{2,1,0:T(8,128)(2,1)S(1)} %dynamic-slice_bitcast_fusion.2), channel_id=1, source_target_pairs={{0,8},{2,10},{4,12},{6,14},{8,0},{10,2},{12,4},{14,6},{16,24},{18,... | collective-permute-start | bytes 1572872 | tf_op jit(solution)/shard_map/ppermute | solution.py:841
  440.8 23.2 %collective-permute-start.24 = (bf16[2,32,4096]{2,1,0:T(8,128)(2,1)S(1)}, bf16[2,32,4096]{2,1,0:T(8,128)(2,1)S(1)}, u32[]{:S(2)}, u32[]{:S(2)}) collective-permute-start(bf16[2,32,4096]{2,1,0:T(8,128)(2,1)S(1)} %dynamic-slice_bitcast_fusion.3), channel_id=1, source_target_pairs={{0,8},{2,10},{4,12},{6,14},{8,0},{10,2},{12,4},{14,6},{16,24},{18,... | collective-permute-start | bytes 1572872 | tf_op jit(solution)/shard_map/ppermute | solution.py:841
  456.2 15.9 %collective-permute-start.31 = (bf16[128,1024]{1,0:T(8,128)(2,1)S(1)}, bf16[128,1024]{1,0:T(8,128)(2,1)S(1)}, u32[]{:S(2)}, u32[]{:S(2)}) collective-permute-start(bf16[128,1024]{1,0:T(8,128)(2,1)S(1)} %dynamic-slice_bitcast_fusion.4), channel_id=1, source_target_pairs={{0,16},{2,18},{4,20},{6,22},{8,24},{10,26},{12,28},{14,30},{16,0},... | collective-permute-start | bytes 786440 | tf_op jit(solution)/shard_map/ppermute | solution.py:841
  (61 other events, 619.1 us)

commit v2 on v1

--- a/solution.py
+++ b/solution.py
@@ -355,12 +355,30 @@
     return lax.broadcasted_iota(jnp.int32, shape, 1) < 64
 
 
-def pack_kernel(half, frames_ref, gain_ref, wq_ref, wk_ref, wv_ref, kv_ref, q_ref, act_ref):
+def pair_low(a, b, low):
+    return jnp.where(low, a, pltpu.roll(b, 64, 1))
+
+
+def pair_high(a, b, low):
+    return jnp.where(low, pltpu.roll(a, 64, 1), b)
+
+
+def store_halves(ref, x):
+    low = low_lanes((x.shape[0], 128))
+    for p in range(x.shape[1] // 256):
+        a, b = x[:, p * 256 : p * 256 + 128], x[:, p * 256 + 128 : (p + 1) * 256]
+        ref[0, :, p * 128 : (p + 1) * 128] = pair_low(a, b, low).astype(BF16)
+        ref[1, :, p * 128 : (p + 1) * 128] = pair_high(a, b, low).astype(BF16)
+
+
+def pack_kernel(half, frames_ref, gain_ref, wq_ref, wk_ref, wv_ref, kv_ref, q_ref, halves_ref, act_ref):
     @pl.when(pl.program_id(0) == 0)
     def _():
         x = frames_ref[...]
         r = lax.rsqrt(jnp.mean(x * x, axis=-1, keepdims=True) + EPSILON)
-        act_ref[...] = (x * r * gain_ref[...]).astype(BF16)
+        normed = x * r * gain_ref[...]
+        act_ref[...] = normed.astype(BF16)
+        store_halves(halves_ref, normed)
 
     act = act_ref[...]
     q = nn_dot(act, wq_ref[...]).astype(BF16).astype(F32) * 0.125
@@ -396,13 +414,14 @@
         out_specs=[
             pl.BlockSpec((step // 64, 2, half, 128), lambda i: (i, 0, 0, 0)),
             pl.BlockSpec((step // 64, 2, half // 2, 128), lambda i: (i, 0, 0, 0)),
-            pl.BlockSpec((rows, width), whole),
+            pl.BlockSpec((2, rows, width // 2), lambda i: (0, 0, 0)),
         ],
         out_shape=[
             jax.ShapeDtypeStruct((heads, 2, half, 128), BF16),
             jax.ShapeDtypeStruct((heads, 2, half // 2, 128), BF16),
-            jax.ShapeDtypeStruct((rows, width), BF16),
+            jax.ShapeDtypeStruct((2, rows, width // 2), BF16),
         ],
+        scratch_shapes=[pltpu.VMEM((rows, width), BF16)],
         compiler_params=pltpu.CompilerParams(vmem_limit_bytes=40 << 20),
         name="project_and_pack",
     )(frames, gain.reshape(1, width), w_query, w_key, w_value)
@@ -527,7 +546,8 @@
             jax.ShapeDtypeStruct((1, n_src * half), F32),
             jax.ShapeDtypeStruct((n_src, quarter, 128), BF16),
         ],
-        compiler_params=pltpu.CompilerParams(vmem_limit_bytes=40 << 20),
+        compiler_params=pltpu.CompilerParams(vmem_limit_bytes=32 << 20),
+        cost_estimate=pl.CostEstimate(flops=25_000_000_000, bytes_accessed=8 << 20, transcendentals=0),
         name="mix",
     )(lengths, core, kv, qp, qpos)
 
@@ -621,7 +641,8 @@
             jax.ShapeDtypeStruct((total, 128), F32),
             jax.ShapeDtypeStruct((n_src, quarter, 128), BF16),
         ],
-        compiler_params=pltpu.CompilerParams(vmem_limit_bytes=48 << 20),
+        compiler_params=pltpu.CompilerParams(vmem_limit_bytes=32 << 20),
+        cost_estimate=pl.CostEstimate(flops=40_000_000_000, bytes_accessed=8 << 20, transcendentals=0),
         name="mix_back",
     )(lengths, core, kv, qp, dp, qpos, out_t, lse)
 
@@ -629,6 +650,192 @@
 def packed_positions(n_src, half):
     j = np.arange(n_src * half)
     return ((j // half) * 2 * half + j % half).astype(np.int32)[None]
+
+
+def feed_kernel(
+    blocks_ref, frames_ref, cot_ref, w_out_ref, gain_ref, w_up_ref, b_up_ref, w_down_ref, b_down_ref,
+    out_ref, grad_mid_ref, grad_blocks_ref, hidden_ref, grad_before_ref, act2_ref, mixed_ref, low_ref, attn_ref,
+    gain_grad_ref, b_up_grad_ref, b_down_grad_ref,
+    mixed, act2, act_grad,
+):
+    i = pl.program_id(0)
+    rows = frames_ref.shape[0]
+    quarter = rows // 4
+    low_q = low_lanes((quarter, 128))
+
+    @pl.when(i == 0)
+    def _():
+        for zy in range(8):
+            for s in range(2):
+                a = blocks_ref[(zy * 2 + s) * 2].astype(F32)
+                b = blocks_ref[(zy * 2 + s) * 2 + 1].astype(F32)
+                at = slice(zy * 128, (zy + 1) * 128)
+                first = 2 * s * quarter
+                mixed[first : first + quarter, at] = pair_low(a, b, low_q)
+                mixed[first + quarter : first + 2 * quarter, at] = pair_high(a, b, low_q)
+        store_halves(mixed_ref, mixed[...])
+        middle = frames_ref[...] + nn_dot(mixed[...].astype(BF16), w_out_ref[...])
+        r = lax.rsqrt(jnp.mean(middle * middle, axis=-1, keepdims=True) + EPSILON)
+        normed = middle * r * gain_ref[...]
+        act2[...] = normed.astype(BF16)
+        store_halves(act2_ref, normed)
+        grad_mid_ref[...] = middle
+        out_ref[...] = middle + b_down_ref[...]
+        grad_low = cot_ref[...].astype(BF16)
+        low_ref[...] = grad_low
+        b_down_grad_ref[...] = jnp.sum(grad_low.astype(F32), axis=0, keepdims=True)
+        act_grad[...] = jnp.zeros_like(act_grad)
+
+    before = nn_dot(act2[...], w_up_ref[...]) + b_up_ref[...]
+    cdf = 0.5 + 0.5 * lax.erf(before * 0.7071067811865476)
+    pdf = jnp.exp(-0.5 * before * before) * 0.3989422804014327
+    hidden = (before * cdf).astype(BF16)
+    step = hidden.shape[1] // 2
+    hidden_ref[0] = hidden[:, :step]
+    hidden_ref[1] = hidden[:, step:]
+    out_ref[...] += nn_dot(hidden, w_down_ref[...])
+    grad_before = (nt_dot(low_ref[...], w_down_ref[...]) * (cdf + before * pdf)).astype(BF16)
+    grad_before_ref[...] = grad_before
+    b_up_grad_ref[...] = jnp.sum(grad_before.astype(F32), axis=0, keepdims=True)
+    act_grad[...] += nt_dot(grad_before, w_up_ref[...])
+
+    @pl.when(i == pl.num_programs(0) - 1)
+    def _():
+        middle = grad_mid_ref[...]
+        r = lax.rsqrt(jnp.mean(middle * middle, axis=-1, keepdims=True) + EPSILON)
+        n = middle * r
+        g = act_grad[...]
+        gain_grad_ref[...] = jnp.sum(g * n, axis=0, keepdims=True)
+        g = g * gain_ref[...]
+        grad_mid = cot_ref[...] + r * (g - n * jnp.mean(g * n, axis=-1, keepdims=True))
+        grad_mid_ref[...] = grad_mid
+        grad_attn = grad_mid.astype(BF16)
+        attn_ref[...] = grad_attn
+        grad_mixed = nt_dot(grad_attn, w_out_ref[...])
+        for zy in range(8):
+            for s in range(2):
+                at = slice(zy * 128, (zy + 1) * 128)
+                first = 2 * s * quarter
+                a = grad_mixed[first : first + quarter, at]
+                b = grad_mixed[first + quarter : first + 2 * quarter, at]
+                grad_blocks_ref[(zy * 2 + s) * 2] = pair_low(a, b, low_q).astype(BF16)
+                grad_blocks_ref[(zy * 2 + s) * 2 + 1] = pair_high(a, b, low_q).astype(BF16)
+
+
+def feed(blocks, frames, cotangent, w_out, gain, w_up, b_up, w_down, b_down):
+    rows, width = frames.shape
+    ff = w_up.shape[1]
+    steps = 8
+    step = ff // steps
+    fixed = lambda *shape: pl.BlockSpec(shape, lambda i: (0,) * len(shape))
+    columns = lambda *shape: pl.BlockSpec(shape, lambda i: (0,) * (len(shape) - 1) + (i,))
+    shape = jax.ShapeDtypeStruct
+    return pl.pallas_call(
+        feed_kernel,
+        grid=(steps,),
+        in_specs=[
+            fixed(*blocks.shape),
+            fixed(rows, width),
+            fixed(rows, width),
+            fixed(width, width),
+            fixed(1, width),
+            columns(width, step),
+            columns(1, step),
+            pl.BlockSpec((step, width), lambda i: (i, 0)),
+            fixed(1, width),
+        ],
+        out_specs=[
+            fixed(rows, width),
+            fixed(rows, width),
+            fixed(*blocks.shape),
+            columns(2, rows, step // 2),
+            columns(rows, step),
+            fixed(2, rows, width // 2),
+            fixed(2, rows, width // 2),
+            fixed(rows, width),
+            fixed(rows, width),
+            fixed(1, width),
+            columns(1, step),
+            fixed(1, width),
+        ],
+        out_shape=[
+            shape((rows, width), F32),
+            shape((rows, width), F32),
+            shape(blocks.shape, BF16),
+            shape((2, rows, ff // 2), BF16),
+            shape((rows, ff), BF16),
+            shape((2, rows, width // 2), BF16),
+            shape((2, rows, width // 2), BF16),
+            shape((rows, width), BF16),
+            shape((rows, width), BF16),
+            shape((1, width), F32),
+            shape((1, ff), F32),
+            shape((1, width), F32),
+        ],
+        scratch_shapes=[
+            pltpu.VMEM((rows, width), F32),
+            pltpu.VMEM((rows, width), BF16),
+            pltpu.VMEM((rows, width), F32),
+        ],
+        compiler_params=pltpu.CompilerParams(vmem_limit_bytes=40 << 20),
+        name="feed",
+    )(
+        blocks, frames, cotangent, w_out, gain.reshape(1, width), w_up, b_up.reshape(1, ff), w_down,
+        b_down.reshape(1, width),
+    )
+
+
+def input_grad_kernel(
+    dkv_ref, dq_ref, frames_ref, grad_mid_ref, gain_ref, wq_ref, wk_ref, wv_ref, gain2_grad_ref, b_up_grad_ref,
+    b_down_grad_ref, grads_ref, out_ref, small_ref,
+):
+    rows, width = frames_ref.shape
+    quarter = rows // 4
+    low_q, low_h = low_lanes((quarter, 128)), low_lanes((2 * quarter, 128))
+    for zy in range(8):
+        for s in range(2):
+            j = (zy * 2 + s) * 2
+            first = 2 * s * quarter
+            a, b = dq_ref[j].astype(F32), dq_ref[j + 1].astype(F32)
+            at = slice(zy * 128, (zy + 1) * 128)
+            grads_ref[first : first + quarter, at] = pair_low(a, b, low_q).astype(BF16)
+            grads_ref[first + quarter : first + 2 * quarter, at] = pair_high(a, b, low_q).astype(BF16)
+            a, b = dkv_ref[j].astype(F32), dkv_ref[j + 1].astype(F32)
+            at = slice(width + zy * 128, width + (zy + 1) * 128)
+            grads_ref[first : first + 2 * quarter, at] = pair_low(a, b, low_h).astype(BF16)
+            at = slice(2 * width + zy * 128, 2 * width + (zy + 1) * 128)
+            grads_ref[first : first + 2 * quarter, at] = pair_high(a, b, low_h).astype(BF16)
+    g = nt_dot(grads_ref[:, :width], wq_ref[...])
+    g += nt_dot(grads_ref[:, width : 2 * width], wk_ref[...])
+    g += nt_dot(grads_ref[:, 2 * width :], wv_ref[...])
+    x = frames_ref[...]
+    r = lax.rsqrt(jnp.mean(x * x, axis=-1, keepdims=True) + EPSILON)
+    n = x * r
+    gain_grad = jnp.sum(g * n, axis=0, keepdims=True)
+    small_ref[...] = jnp.zeros_like(small_ref)
+    for d in range(small_ref.shape[0]):
+        at = slice(d // 4 * 128, (d // 4 + 1) * 128)
+        small_ref[d, 0:1] = gain_grad[:, at]
+        small_ref[d, 1:2] = gain2_grad_ref[:, at]
+        small_ref[d, 2:3] = b_down_grad_ref[:, at]
+        small_ref[d, 3:4] = b_up_grad_ref[:, d * 128 : (d + 1) * 128]
+    g = g * gain_ref[...]
+    out_ref[...] = grad_mid_ref[...] + r * (g - n * jnp.mean(g * n, axis=-1, keepdims=True))
+
+
+def input_grad(dkv, dq, frames, grad_mid, gain, w_query, w_key, w_value, gain2_grad, b_up_grad, b_down_grad):
+    rows, width = frames.shape
+    shape = jax.ShapeDtypeStruct
+    return pl.pallas_call(
+        input_grad_kernel,
+        in_specs=[pl.BlockSpec(memory_space=pltpu.VMEM)] * 11,
+        out_specs=[pl.BlockSpec(memory_space=pltpu.VMEM)] * 3,
+        out_shape=[shape((rows, 3 * width), BF16), shape((rows, width), F32), shape((32, 8, 128), F32)],
+        compiler_params=pltpu.CompilerParams(vmem_limit_bytes=24 << 20),
+        name="input_grad",
+    )(
+        dkv, dq, frames, grad_mid, gain.reshape(1, width), w_query, w_key, w_value, gain2_grad, b_up_grad, b_down_grad
+    )
 
 
 MESH = pl.DeviceIdType.MESH
@@ -834,57 +1041,316 @@
     )(dkv, dq)
 
 
+BITS = {"core": 1, "y": 2, "z0": 4, "z1": 8}
+
+
 def flipped(x, axis):
     if axis == "x":
         return lax.ppermute(x, "grp", [(0, 1), (1, 0)])
-    bit = {"core": 1, "y": 2, "z0": 4, "z1": 8}[axis]
-    return lax.ppermute(x, "blk", [(i, i ^ bit) for i in range(lax.axis_size("blk"))])
+    return lax.ppermute(x, "blk", [(i, i ^ BITS[axis]) for i in range(lax.axis_size("blk"))])
 
 
 def bit_of(axis):
     if axis == "x":
         return lax.axis_index("grp")
-    bit = {"core": 1, "y": 2, "z0": 4, "z1": 8}[axis]
-    return lax.rem(lax.div(lax.axis_index("blk"), bit), 2)
-
-
-def pick(x, dim, index):
-    return lax.dynamic_index_in_dim(x, index, dim, keepdims=False)
-
-
-def scattered_sum(x, order):
-    dims = ["z1", "z0", "y", "x"]
-    total = x
-    for axis in order:
-        mine, at = bit_of(axis), dims.index(axis)
-        got = flipped(pick(total, at, 1 - mine), axis)
-        total = pick(total, at, mine).astype(F32) + got.astype(F32)
-        dims.remove(axis)
-        if dims:
-            total = total.astype(BF16)
-    return total
-
-
-def halves(x, core, per_device):
-    parts = x.reshape(x.shape[0], 8, 2, 2 * per_device)
-    take = lambda c: pick(parts, 2, c).reshape(x.shape[0], 16 * per_device)
-    return take(core), take(1 - core)
-
-
-def both(x):
-    return jnp.concatenate([x, flipped(x, "core")], axis=0)
-
-
-def row_gradients(left, right, core, per_device):
-    mine, others = halves(left, core, per_device)
-    lefts = jnp.concatenate([mine, flipped(others, "core")], axis=0)
-    grad = left_dot(lefts, right).astype(BF16)
-    return grad.reshape(2, 2, 2, 2, per_device, grad.shape[1])
-
-
-def unpacked(blocks, rows):
-    parts = blocks.reshape(8, 2, 2, rows // 4, 2, 64)
-    return parts.transpose(1, 4, 3, 0, 2, 5).reshape(rows, 1024)
+    return lax.rem(lax.div(lax.axis_index("blk"), BITS[axis]), 2)
+
+
+def sibling_of(core):
+    return {"blk": lax.axis_index("blk") + 1 - 2 * core, "grp": lax.axis_index("grp")}
+
+
+def across(axis):
+    blk, grp = lax.axis_index("blk"), lax.axis_index("grp")
+    if axis == "x":
+        return {"blk": blk, "grp": 1 - grp}
+    bit = BITS[axis]
+    return {"blk": blk + bit - 2 * bit * bit_of(axis), "grp": grp}
+
+
+def tn_dot(a, b):
+    return lax.dot_general(a, b, (((0,), (0,)), ((), ())), preferred_element_type=F32)
+
+
+def share_kernel(
+    n, blocks_in, hidden, grad_before, act2, mixed, low, attn,
+    blocks_out, keep_a, send_a, keep_b, send_b, keep_c, send_c,
+    hidden2, before2, act2_2, mixed2, low2, attn2, tile, send, recv, local, pair_send, pair_recv,
+):
+    me = own_index()
+    head, core = head_of(me)
+    rows = low.shape[0]
+    greet_all(me, n)
+    sibling = sibling_of(core)
+    theirs = pl.ds(rows, rows)
+    pairs = [
+        remote(src, dst.at[theirs], pair_send.at[k], pair_recv.at[k], sibling)
+        for k, (src, dst) in enumerate(
+            (
+                (low, low2),
+                (hidden.at[1 - core], hidden2),
+                (act2.at[1 - core], act2_2),
+                (grad_before, before2),
+                (mixed.at[1 - core], mixed2),
+                (attn, attn2),
+            )
+        )
+    ]
+    for copy in pairs:
+        copy.start()
+
+    def copy_with(i, src):
+        other = lax.rem(me + i, n)
+        return remote(blocks_in.at[other], blocks_out.at[src], send.at[i], recv.at[src], place(other))
+
+    @pl.loop(1, n)
+    def _(i):
+        copy_with(i, me).start()
+
+    own = pltpu.make_async_copy(blocks_in.at[me], blocks_out.at[me], local)
+    own.start()
+    low2[:rows] = low[...]
+    hidden2[:rows] = hidden[core]
+    act2_2[:rows] = act2[core]
+    before2[:rows] = grad_before[...]
+    mixed2[:rows] = mixed[core]
+    attn2[:rows] = attn[...]
+
+    x_mine, y_mine, z_mine = bit_of("x"), bit_of("y"), bit_of("z0")
+
+    def put(keep, away, mine, bit, at, row, value):
+        @pl.when(mine == bit)
+        def _():
+            keep[at, row : row + value.shape[0]] = value
+
+        @pl.when(mine != bit)
+        def _():
+            away[at, row : row + value.shape[0]] = value
+
+    pairs[0].wait()
+    pairs[1].wait()
+
+    @pl.loop(0, 8)
+    def _(zy):
+        columns = pl.ds(pl.multiple_of(zy * 256, 256), 256)
+        value = tn_dot(hidden2[:, columns], low2[...]).astype(BF16)
+        z1, z0, y = lax.div(zy, 4), lax.rem(lax.div(zy, 2), 2), lax.rem(zy, 2)
+        for x in range(2):
+            put(keep_a, send_a, x_mine, x, zy, 0, value[x * 128 : x * 128 + 96])
+            put(keep_c, send_c, z_mine, z0, (z1 * 2 + y) * 2 + x, 0, value[x * 128 + 96 : (x + 1) * 128])
+
+    def spread_rows(left, right, slab, to_b, row):
+        tile[...] = tn_dot(left[...], right[:, slab * 1024 : (slab + 1) * 1024]).astype(BF16)
+
+        @pl.loop(0, 16)
+        def _(j):
+            value = tile[pl.ds(pl.multiple_of(j * 32, 32), 32)]
+            z1, z0 = lax.div(j, 8), lax.rem(lax.div(j, 4), 2)
+            y, x = lax.rem(lax.div(j, 2), 2), lax.rem(j, 2)
+            if to_b:
+                put(keep_b, send_b, y_mine, y, (z1 * 2 + z0) * 2 + x, row, value)
+            else:
+                put(keep_c, send_c, z_mine, z0, (z1 * 2 + y) * 2 + x, row, value)
+
+    pairs[2].wait()
+    pairs[3].wait()
+    for slab in range(3):
+        spread_rows(act2_2, before2, slab, True, 32 * slab)
+    spread_rows(act2_2, before2, 3, False, 32)
+    pairs[4].wait()
+    pairs[5].wait()
+    spread_rows(mixed2, attn2, 0, False, 64)
+    own.wait()
+
+    @pl.loop(1, n)
+    def _(i):
+        copy_with(i, lax.rem(me + i, n)).wait()
+
+
+def share(blocks, hidden, grad_before, act2, mixed, low, attn, n):
+    rows, width = low.shape
+    vmem = pl.BlockSpec(memory_space=pltpu.VMEM)
+    shape = jax.ShapeDtypeStruct
+    return pl.pallas_call(
+        functools.partial(share_kernel, n),
+        in_specs=[vmem] * 7,
+        out_specs=[vmem] * 7,
+        out_shape=[shape(blocks.shape, BF16)] + [shape((8, 96, width), BF16)] * 6,
+        scratch_shapes=[
+            pltpu.VMEM((2 * rows, hidden.shape[2]), BF16),
+            pltpu.VMEM((2 * rows, grad_before.shape[1]), BF16),
+            pltpu.VMEM((2 * rows, width // 2), BF16),
+            pltpu.VMEM((2 * rows, width // 2), BF16),
+            pltpu.VMEM((2 * rows, width), BF16),
+            pltpu.VMEM((2 * rows, width), BF16),
+            pltpu.VMEM((width // 2, 1024), BF16),
+            pltpu.SemaphoreType.DMA((n,)),
+            pltpu.SemaphoreType.DMA((n,)),
+            pltpu.SemaphoreType.DMA,
+            pltpu.SemaphoreType.DMA((6,)),
+            pltpu.SemaphoreType.DMA((6,)),
+        ],
+        compiler_params=pltpu.CompilerParams(
+            collective_id=3, has_side_effects=True, vmem_limit_bytes=40 << 20
+        ),
+        name="share",
+    )(blocks, hidden, grad_before, act2, mixed, low, attn)
+
+
+class Part:
+    def __init__(self, total, dims, order, landing, send, recv):
+        self.view, self.dims, self.order = total, list(dims), list(order)
+        self.landing, self.send, self.recv = landing, send, recv
+        self.stage, self.copy, self.kept = 0, None, None
+
+    def start(self):
+        axis = self.order[self.stage]
+        at, mine = self.dims.index(axis), bit_of(axis)
+        ahead = (slice(None),) * at
+        self.copy = remote(
+            self.view.at[ahead + (1 - mine,)],
+            self.landing[self.stage],
+            self.send.at[self.stage],
+            self.recv.at[self.stage],
+            across(axis),
+        )
+        self.copy.start()
+        self.kept = self.view.at[ahead + (mine,)]
+        self.dims.remove(axis)
+        self.stage += 1
+
+    def finish(self):
+        self.copy.wait()
+        got, kept = self.landing[self.stage - 1], self.kept
+        lead = len(self.dims)
+
+        @pl.loop(0, 2**lead)
+        def _(k):
+            at = tuple(lax.rem(lax.div(k, 2**d), 2) for d in reversed(range(lead)))
+            kept[at] = (kept[at].astype(F32) + got[at].astype(F32)).astype(BF16)
+
+        self.view = kept
+
+    def last(self):
+        self.copy.wait()
+        return self.kept[...].astype(F32) + self.landing[self.stage - 1][...].astype(F32)
+
+
+def gather_kernel(
+    n, act1, qkv, keep_a, got_a, keep_b, got_b, keep_c, got_c, small_in,
+    q_out, k_out, v_out, o_out, up_out, down_out, small_out,
+    act1_2, qkv2, sum_a, sum_b, sum_c, sum_q, sum_k, sum_v,
+    a2, a3, a4, b2, b3, b4, c2, c3, c4,
+    q1, q2, q3, q4, k1, k2, k3, k4, v1, v2, v3, v4, small_all,
+    send, recv, small_send, small_recv, pair_send, pair_recv,
+):
+    me = own_index()
+    head, core = head_of(me)
+    rows, width = qkv.shape[0], qkv.shape[1] // 3
+    greet_all(me, n)
+    sibling = sibling_of(core)
+    theirs = pl.ds(rows, rows)
+    pairs = [
+        remote(act1.at[1 - core], act1_2.at[theirs], pair_send.at[0], pair_recv.at[0], sibling),
+        remote(qkv, qkv2.at[theirs], pair_send.at[1], pair_recv.at[1], sibling),
+    ]
+    for copy in pairs:
+        copy.start()
+    sums = [sum_a, sum_b, sum_c, sum_q, sum_k, sum_v]
+    dims = [("z1", "z0", "y"), ("z1", "z0", "x"), ("z1", "y", "x")] + [("z1", "z0", "y", "x")] * 3
+    orders = [
+        ("y", "z0", "z1"), ("z0", "x", "z1"), ("x", "y", "z1"),
+        ("x", "y", "z0", "z1"), ("y", "z0", "x", "z1"), ("z0", "x", "y", "z1"),
+    ]
+    landings = [(a2, a3, a4), (b2, b3, b4), (c2, c3, c4), (q1, q2, q3, q4), (k1, k2, k3, k4), (v1, v2, v3, v4)]
+    parts = [
+        Part(total, names, order, landing, send.at[k], recv.at[k])
+        for k, (total, names, order, landing) in enumerate(zip(sums, dims, orders, landings))
+    ]
+    for part, total, keep, got in zip(parts, sums, (keep_a, keep_b, keep_c), (got_a, got_b, got_c)):
+
+        @pl.loop(0, 8)
+        def _(k):
+            at = (lax.div(k, 4), lax.rem(lax.div(k, 2), 2), lax.rem(k, 2))
+            total[at] = (keep[k].astype(F32) + got[k].astype(F32)).astype(BF16)
+
+        part.start()
+
+    def small_copy(i, src):
+        other = lax.rem(me + i, n)
+        return remote(small_in.at[other], small_all.at[src], small_send.at[i], small_recv.at[src], place(other))
+
+    @pl.loop(1, n)
+    def _(i):
+        small_copy(i, me).start()
+
+    act1_2[:rows] = act1[core]
+    qkv2[:rows] = qkv[...]
+    for copy in pairs:
+        copy.wait()
+    for k in range(3):
+        value = tn_dot(act1_2[...], qkv2[:, k * width : (k + 1) * width]).astype(BF16)
+        for j in range(16):
+            sums[3 + k][j // 8, j // 4 % 2, j // 2 % 2, j % 2] = value[j * 32 : (j + 1) * 32]
+        parts[3 + k].start()
+
+    for turn in range(2):
+        for part in parts:
+            part.finish()
+            part.start()
+    for part in parts[3:]:
+        part.finish()
+        part.start()
+    small_all[me] = small_in[me]
+
+    @pl.loop(1, n)
+    def _(i):
+        small_copy(i, lax.rem(me + i, n)).wait()
+
+    small_out[...] = jnp.sum(small_all[...], axis=0)
+    down_out[:96] = parts[0].last()
+    value = parts[1].last()
+    for slab in range(3):
+        up_out[:, slab * 1024 : (slab + 1) * 1024] = value[slab * 32 : (slab + 1) * 32]
+    value = parts[2].last()
+    down_out[96:] = value[:32]
+    up_out[:, 3072:] = value[32:64]
+    o_out[...] = value[64:]
+    q_out[...] = parts[3].last()
+    k_out[...] = parts[4].last()
+    v_out[...] = parts[5].last()
+
+
+def gather(act1, qkv, keeps, gots, small, n):
+    rows, width = qkv.shape[0], qkv.shape[1] // 3
+    vmem = pl.BlockSpec(memory_space=pltpu.VMEM)
+    shape = jax.ShapeDtypeStruct
+    thin, wide = (32, width), (96, width)
+    buffers = [pltpu.VMEM((2, 2, 2, *wide), BF16)] * 3 + [pltpu.VMEM((2, 2, 2, 2, *thin), BF16)] * 3
+    buffers += [pltpu.VMEM((2,) * k + wide, BF16) for k in (2, 1, 0)] * 3
+    buffers += [pltpu.VMEM((2,) * k + thin, BF16) for k in (3, 2, 1, 0)] * 3
+    return pl.pallas_call(
+        functools.partial(gather_kernel, n),
+        in_specs=[vmem] * 9,
+        out_specs=[vmem] * 7,
+        out_shape=[shape(thin, F32)] * 4 + [shape((32, 4 * width), F32), shape((128, width), F32), shape((8, 128), F32)],
+        scratch_shapes=[
+            pltpu.VMEM((2 * rows, width // 2), BF16),
+            pltpu.VMEM((2 * rows, 3 * width), BF16),
+            *buffers,
+            pltpu.VMEM((n, 8, 128), F32),
+            pltpu.SemaphoreType.DMA((6, 4)),
+            pltpu.SemaphoreType.DMA((6, 4)),
+            pltpu.SemaphoreType.DMA((n,)),
+            pltpu.SemaphoreType.DMA((n,)),
+            pltpu.SemaphoreType.DMA((2,)),
+            pltpu.SemaphoreType.DMA((2,)),
+        ],
+        compiler_params=pltpu.CompilerParams(
+            collective_id=4, has_side_effects=True, vmem_limit_bytes=40 << 20
+        ),
+        name="gather",
+    )(act1, qkv, keeps[0], gots[0], keeps[1], gots[1], keeps[2], gots[2], small)
 
 
 def shards_heads(
@@ -893,90 +1359,49 @@
     rows, width = frames.shape
     n = lax.axis_size("blk") * lax.axis_size("grp")
     half = rows // 2
-    core = bit_of("core")
-    core_word = core.astype(jnp.int32).reshape(1)
+    core_word = bit_of("core").astype(jnp.int32).reshape(1)
     qpos = jnp.asarray(packed_positions(n, half))
 
     kv_blocks, q_blocks, act1 = project_and_pack(frames, norm1_gain, w_query, w_key, w_value)
     kv, q = to_heads(kv_blocks, q_blocks, n)
     kv_rows = kv.reshape(n * rows, 128)
     out_t, lse, out_blocks = mix(lengths, core_word, kv_rows, q, qpos)
-    mixed = unpacked(exchange(out_blocks, n, 2), rows)
-
-    middle = frames + jnp.dot(mixed, w_out, preferred_element_type=F32)
-    normed2, norm2_back = jax.vjp(rms_norm, middle, norm2_gain)
-    act2 = normed2.astype(BF16)
-    before = jnp.dot(act2, w_up, preferred_element_type=F32) + b_up
-    activated, gelu_back = jax.vjp(gelu_exact, before)
-    hidden = activated.astype(BF16)
-    layer_out = middle + jnp.dot(hidden, w_down, preferred_element_type=F32) + b_down
-    grad_low = cotangent.astype(BF16)
-    b_down_grad = jnp.sum(grad_low.astype(F32), axis=0)
-    grad_before = gelu_back(right_dot(grad_low, w_down))[0].astype(BF16)
-    b_up_grad = jnp.sum(grad_before.astype(F32), axis=0)
-    grad_mid_norm, norm2_gain_grad = norm2_back(right_dot(grad_before, w_up))
-    grad_middle = cotangent + grad_mid_norm
-    grad_attn = grad_middle.astype(BF16)
-    grad_mixed = right_dot(grad_attn, w_out).astype(BF16)
-
-    grad_blocks = exchange(to_blocks(grad_mixed), n, 3)
+    mixed_blocks = exchange(out_blocks, n, 2)
+    (
+        layer_out, grad_middle, grad_blocks, hidden, grad_before, act2, mixed, grad_low, grad_attn,
+        norm2_gain_grad, b_up_grad, b_down_grad,
+    ) = feed(mixed_blocks, frames, cotangent, w_out, norm2_gain, w_up, b_up, w_down, b_down)
+
+    grad_blocks, *parts = share(grad_blocks, hidden, grad_before, act2, mixed, grad_low, grad_attn, n)
+    keeps = parts[0::2]
+    gots = [flipped(part, axis) for part, axis in zip(parts[1::2], ("x", "y", "z0"))]
     dkv, dq = mix_back(lengths, core_word, kv_rows, q, grad_blocks, qpos, out_t, lse)
 
-    grads_low = both(grad_low)
-    w_down_part = row_gradients(hidden, grads_low, core, 128)
-    w_up_part = row_gradients(act2, both(grad_before), core, 32)
-    w_out_part = row_gradients(mixed, both(grad_attn), core, 32)
-    w_down_grad = scattered_sum(w_down_part, ("x", "y", "z0", "z1"))
-    w_up_grad = scattered_sum(w_up_part, ("y", "x", "z0", "z1"))
-    w_out_grad = scattered_sum(w_out_part, ("x", "y", "z0", "z1"))
-
     dkv_blocks, dq_blocks = from_heads(dkv.reshape(n, 2, half, 128), dq, n)
-    grad_queries = unpacked(dq_blocks, rows)
-    grad_kv = dkv_blocks.reshape(8, 2, 2, half, 2, 64).transpose(4, 1, 3, 0, 2, 5).reshape(2, rows, width)
-    grad_keys, grad_values = grad_kv[0], grad_kv[1]
-    grad_act1 = right_dot(grad_queries, w_query) + right_dot(grad_keys, w_key) + right_dot(grad_values, w_value)
-    unused_out, norm1_back = jax.vjp(rms_norm, frames, norm1_gain)
-    grad_frames_norm, norm1_gain_grad = norm1_back(grad_act1)
-    frames_grad = grad_middle + grad_frames_norm
-
-    qkv = both(jnp.concatenate([grad_queries, grad_keys, grad_values], axis=1))
-    qkv_part = row_gradients(act1, qkv, core, 32)
-    w_query_grad = scattered_sum(qkv_part[..., :width], ("x", "y", "z0", "z1"))
-    w_key_grad = scattered_sum(qkv_part[..., width : 2 * width], ("y", "x", "z0", "z1"))
-    w_value_grad = scattered_sum(qkv_part[..., 2 * width :], ("x", "y", "z0", "z1"))
-
-    small = jnp.concatenate(
-        [
-            norm1_gain_grad.reshape(n, -1),
-            norm2_gain_grad.reshape(n, -1),
-            b_down_grad.reshape(n, -1),
-            b_up_grad.reshape(n, -1),
-        ],
-        axis=1,
+    qkv, frames_grad, small = input_grad(
+        dkv_blocks, dq_blocks, frames, grad_middle, norm1_gain, w_query, w_key, w_value,
+        norm2_gain_grad, b_up_grad, b_down_grad,
+    )
+    w_query_grad, w_key_grad, w_value_grad, w_out_grad, w_up_grad, w_down_grad, small = gather(
+        act1, qkv, keeps, gots, small, n
     )
     part = width // n
-    small = jnp.pad(small, ((0, 0), (0, 1024 - small.shape[1]))).reshape(n, 8, 128)
-    small = jnp.sum(exchange(small, n, 4), axis=0).reshape(1024)
+    turn = lax.rem(own_index(), 128 // part) * part
+    vectors = lax.dynamic_slice(small, (0, turn), (3, part))
     return (
         layer_out,
         frames_grad,
-        small[:part],
+        vectors[0],
         w_query_grad,
         w_key_grad,
         w_value_grad,
         w_out_grad,
-        small[part : 2 * part],
+        vectors[1],
         w_up_grad,
-        small[3 * part : 3 * part + b_up.shape[0] // n],
+        small[3],
         w_down_grad,
-        small[2 * part : 3 * part],
-    )
-
-
-def to_blocks(grad_mixed):
-    rows = grad_mixed.shape[0]
-    parts = grad_mixed.reshape(2, 2, rows // 4, 8, 2, 64)
-    return parts.transpose(3, 0, 4, 2, 1, 5).reshape(32, rows // 4, 128)
+        vectors[2],
+    )
 
 
 def solution(mesh):

time: 485 us -> 309 us (0.64); the launches traced: 476 us -> 313 us
  Pallas kernels: 167 us -> 278 us
  waiting for transfers between devices: 111 us -> 0.01 us
  local copies, waits for them, and re-layouts: 90.2 us -> 32.2 us
  matrix products: 55.5 us -> 0 us
  starting transfers between devices: 30.6 us -> 1.67 us
  other arithmetic: 20.1 us -> 0 us
    pallas_call x0 -> x4, Pallas kernels: none -> 135 us  [the longest x1 90.2 us: gather(): pl.pallas_call(functools.partial(gather_kernel, n), in_specs=[vmem] * 9,...]
    ppermute x26 -> x2, waiting for transfers between devices: 66.3 us -> 0.01 us  [flipped(): lax.ppermute(x, 'blk', [(i, i ^ BITS[axis]) for i in range(lax.axis_size(...]
    dot_general x13 -> x0, matrix products: 55.5 us -> none  [the longest x6 28.8 us: right_dot(): lax.dot_general(left, right, (((1,), (1,)), ((), ())), preferred_element_...]
    ppermute x6 -> x1, waiting for transfers between devices: 44.8 us -> 0.01 us  [flipped(): return lax.ppermute(x, 'grp', [(0, 1), (1, 0)])]
    pallas_call x3 -> x1, Pallas kernels: 49.6 us -> 19.2 us  [exchange(): pl.pallas_call(functools.partial(exchange_kernel, n), in_specs=[anywhere]...]
    reshape x13 -> x0, local copies, waits for them, and re-layouts: 29.8 us -> none  [the longest x4 9.94 us: unpacked(): parts = blocks.reshape(8, 2, 2, rows // 4, 2, 64)]
    ppermute x26 -> x2, starting transfers between devices: 23.9 us -> 1.13 us  [flipped(): lax.ppermute(x, 'blk', [(i, i ^ BITS[axis]) for i in range(lax.axis_size(...]
    dynamic_slice x14 -> x1, local copies, waits for them, and re-layouts: 19.9 us -> 0.07 us  [shards_heads(): vectors = lax.dynamic_slice(small, (0, turn), (3, part))]
  transfers between devices with their start and end apart: 32 -> 3, of which waited for: 15 -> 0; matrix products, arithmetic and copies ran while one was open for 30% -> 0% of each run, Pallas kernels for 35% -> 21%
where the time goes in v2:
time: 309 us; the launch traced here: 313 us
  Pallas kernels  278 us (90%)
  local copies, waits for them, and re-layouts  32.2 us (10%)
    pallas_call x1, Pallas kernels, gather(): pl.pallas_call(functools.partial(gather_kernel, n), in_specs=[vmem] * 9,...  90.2 us
    pallas_call x1, Pallas kernels, mix_back(): pl.pallas_call(functools.partial(back_kernel, lengths.shape[0], chunks, k...  38.1 us
    unnamed x86, local copies, waits for them, and re-layouts  31.1 us
    pallas_call x1, Pallas kernels, to_heads(): pl.pallas_call(functools.partial(to_heads_kernel, n), in_specs=[anywhere]...  30.1 us
    pallas_call x1, Pallas kernels, mix(): pl.pallas_call(functools.partial(mix_kernel, lengths.shape[0], chunks, ke...  26.1 us
    pallas_call x1, Pallas kernels, from_heads(): pl.pallas_call(functools.partial(from_heads_kernel, n), in_specs=[pl.Bloc...  25.6 us
    pallas_call x1, Pallas kernels, share(): pl.pallas_call(functools.partial(share_kernel, n), in_specs=[vmem] * 7, o...  24.7 us
    pallas_call x1, Pallas kernels, exchange(): pl.pallas_call(functools.partial(exchange_kernel, n), in_specs=[anywhere]...  19.2 us
  transfers between devices with their start and end apart: 3, of which 0 were waited for; matrix products, arithmetic and copies ran while one was open for 0% of the time, Pallas kernels for 21%

profile of v2, /device:TPU:0, one launch (start us, length us, event | category | flops | bytes accessed | tf_op | source)
XLA Modules:
  0.0 312.8 jit_solution(336671827853842830)
XLA Ops:
  0.7 1.6 copy-done
  2.2 1.6 copy-done.2
  3.8 1.6 copy-done.4
  5.4 1.1 copy-done.6
  7.3 3.5 %project_and_pack.1 = (bf16[16,2,96,128]{3,2,1,0:T(8,128)(2,1)S(1)}, bf16[16,2,48,128]{3,2,1,0:T(8,128)(2,1)S(1)}, bf16[2,192,512]{2,1,0:T(8,128)(2,1)S(1)}) custom-call(f32[192,1024]{1,0:T(8,128)S(1)} %copy-done.6, f32[1,1024]{1,0:T(1,128)S(1)} %bitcast.16, bf16[1024,1024]{1,0:T(8,128)(2,1)S(1)} %copy-done, bf16[1024,1024]{1,0:T(8,128)(2,1)S(1)} %copy-done.2, ...), custom_call_target="tpu_custom_call" | custom-call | tf_op jit(solution)/shard_map/project_and_pack/pallas_call | solution.py:410
  12.3 30.1 %to_heads.1 = (bf16[32,2,96,128]{3,2,1,0:T(8,128)(2,1)}, bf16[32,48,128]{2,1,0:T(8,128)(2,1)}) custom-call(bf16[16,2,96,128]{3,2,1,0:T(8,128)(2,1)} %copy-done.22, bf16[16,2,48,128]{3,2,1,0:T(8,128)(2,1)} %copy-done.26), custom_call_target="tpu_custom_call" | custom-call | tf_op jit(solution)/shard_map/to_heads/pallas_call | solution.py:916
  42.5 1.4 copy-done.32
  43.9 1.0 copy-done.34
  44.9 26.1 %mix.1 = (f32[64,3072]{1,0:T(8,128)S(1)}, f32[1,3072]{1,0:T(1,128)S(1)}, bf16[32,48,128]{2,1,0:T(8,128)(2,1)S(1)}) custom-call(s32[12]{0:T(128)S(1)} %copy-done.36, s32[1]{0:T(128)} %bitcast.core_ref, bf16[6144,128]{1,0:T(8,128)(2,1)S(1)} %bitcast.21, bf16[32,48,128]{2,1,0:T(8,128)(2,1)S(1)} %copy-done.34, s32[1,3072]{1,0:T(1,128)S(1)} %copy-done.37), custom_call_target="tpu_custom_call" | custom-call | flops 24999999488 | bytes 8388608 | tf_op jit(solution)/shard_map/mix/pallas_call | solution.py:521
  72.7 19.2 %exchange.1.blocks_ref = bf16[32,48,128]{2,1,0:T(8,128)(2,1)} custom-call(bf16[32,48,128]{2,1,0:T(8,128)(2,1)} %copy-done.25), custom_call_target="tpu_custom_call" | custom-call | tf_op jit(solution)/shard_map/exchange/pallas_call | solution.py:958
  93.0 1.1 copy-done.19
  94.1 17.0 %feed.1 = (f32[192,1024]{1,0:T(8,128)}, f32[192,1024]{1,0:T(8,128)S(1)}, bf16[32,48,128]{2,1,0:T(8,128)(2,1)S(1)}, bf16[2,192,2048]{2,1,0:T(8,128)(2,1)S(1)}, bf...) custom-call(bf16[32,48,128]{2,1,0:T(8,128)(2,1)S(1)} %copy-done.18, ...), custom_call_target="tpu_custom_call" | custom-call | tf_op jit(solution)/shard_map/feed/pallas_call | solution.py:733
  111.1 1.1 copy-done.11
  113.1 24.7 %share.1 = (bf16[32,48,128]{2,1,0:T(8,128)(2,1)S(1)}, bf16[8,96,1024]{2,1,0:T(8,128)(2,1)S(1)}, bf16[8,96,1024]{2,1,0:T(8,128)(2,1)}, bf16[8,96,1024]{2,1,0:T(8,...) custom-call(bf16[32,48,128]{2,1,0:T(8,128)(2,1)S(1)} %get-tuple-element., ...), custom_call_target="tpu_custom_call" | custom-call | tf_op jit(solution)/shard_map/share/pallas_call | solution.py:1174
  137.8 1.2 copy-done.12
  139.1 1.2 copy-done.14
  140.3 1.2 copy-done.16
  143.1 38.1 %mix_back.1 = (f32[6144,128]{1,0:T(8,128)S(1)}, bf16[32,48,128]{2,1,0:T(8,128)(2,1)S(1)}) custom-call(s32[12]{0:T(128)S(1)} %copy-done.36, s32[1]{0:T(128)} %bitcast.core_ref, bf16[6144,128]{1,0:T(8,128)(2,1)S(1)} %bitcast.22, bf16[32,48,128]{2,1,0:T(8,128)(2,1)S(1)} %copy-done.35, bf16[32,48,128]{2,1,0:T(8,128)(2,1)S(1)} %get-tuple-element.66.dp_ref, ...), custom_call_target="tpu_custom_call" | custom-call | flops 40000000000 | bytes 8388608 | tf_op jit(solution)/shard_map/mix_back/pallas_call | solution.py:620
  181.3 1.6 copy-done.8
  183.7 1.9 copy-done.9
  186.6 25.6 %from_heads.1 = (bf16[32,96,128]{2,1,0:T(8,128)(2,1)S(1)}, bf16[32,48,128]{2,1,0:T(8,128)(2,1)S(1)}) custom-call(f32[32,2,96,128]{3,2,1,0:T(8,128)S(1)} %bitcast.15, bf16[32,48,128]{2,1,0:T(8,128)(2,1)S(1)} %copy-done.24), custom_call_target="tpu_custom_call" | custom-call | tf_op jit(solution)/shard_map/from_heads/pallas_call | solution.py:1021
  212.2 1.6 copy-done.5
  213.8 3.4 %input_grad.1 = (bf16[192,3072]{1,0:T(8,128)(2,1)S(1)}, f32[192,1024]{1,0:T(8,128)}, f32[32,8,128]{2,1,0:T(8,128)S(1)}) custom-call(bf16[32,96,128]{2,1,0:T(8,128)(2,1)S(1)} %get-tuple-element.71.dkv_ref, bf16[32,48,128]{2,1,0:T(8,128)(2,1)S(1)} %get-tuple-element.72.dq_ref, f32[192,1024]{1,0:T(8,128)S(1)} %copy-done.7, f32[192,1024]{1,0:T(8,128)S(1)} %copy-done.21, ...), custom_call_target="tpu_custom_call" | custom-call | tf_op jit(solution)/shard_map/input_grad/pallas_call | solution.py:829
  217.3 90.2 %gather.1 = (f32[32,1024]{1,0:T(8,128)S(1)}, f32[32,1024]{1,0:T(8,128)S(1)}, f32[32,1024]{1,0:T(8,128)S(1)}, f32[32,1024]{1,0:T(8,128)S(1)}, f32[32,4096]{1,0:T(...) custom-call(bf16[2,192,512]{2,1,0:T(8,128)(2,1)S(1)} %get-tuple-element.78.act1, ...), custom_call_target="tpu_custom_call" | custom-call | tf_op jit(solution)/shard_map/gather/pallas_call | solution.py:1332
  (81 shorter events, 14.6 us)
Async XLA Ops:
  0.6 1.6 copy-start
  7.2 35.2 %copy-start.36 = (s32[12]{0:T(128)S(1)}, s32[12]{0:T(128)}, u32[]{:S(2)}) copy-start(s32[12]{0:T(128)} %len_ref.3) | copy-start | bytes 148
  7.2 35.3 %copy-start.37 = (s32[1,3072]{1,0:T(1,128)S(1)}, s32[1,3072]{1,0:T(1,128)}, u32[]{:S(2)}) copy-start(s32[1,3072]{1,0:T(1,128)} %constant.26.clone.qpos_ref) | copy-start | bytes 36868
  44.9 47.0 %copy-start.7 = (f32[192,1024]{1,0:T(8,128)S(1)}, f32[192,1024]{1,0:T(8,128)}, u32[]{:S(2)}) copy-start(f32[192,1024]{1,0:T(8,128)} %frames_ref.5) | copy-start | bytes 2359300
  44.9 47.0 %copy-start.10 = (bf16[1024,1024]{1,0:T(8,128)(2,1)S(1)}, bf16[1024,1024]{1,0:T(8,128)(2,1)}, u32[]{:S(2)}) copy-start(bf16[1024,1024]{1,0:T(8,128)(2,1)} %w_out_ref.1) | copy-start | bytes 6291460
  44.9 47.0 %copy-start.29 = (f32[4096]{0:T(1024)S(1)}, f32[4096]{0:T(1024)}, u32[]{:S(2)}) copy-start(f32[4096]{0:T(1024)} %param.23) | copy-start | bytes 49156
  44.9 47.0 %copy-start.30 = (f32[1024]{0:T(1024)S(1)}, f32[1024]{0:T(1024)}, u32[]{:S(2)}) copy-start(f32[1024]{0:T(1024)} %param.21) | copy-start | bytes 12292
  44.9 47.0 %copy-start.31 = (f32[1024]{0:T(1024)S(1)}, f32[1024]{0:T(1024)}, u32[]{:S(2)}) copy-start(f32[1024]{0:T(1024)} %param.25) | copy-start | bytes 12292
  113.1 30.0 %copy-start.33 = (bf16[32,2,96,128]{3,2,1,0:T(8,128)(2,1)S(1)}, bf16[32,2,96,128]{3,2,1,0:T(8,128)(2,1)}, u32[]{:S(2)}) copy-start(bf16[32,2,96,128]{3,2,1,0:T(8,128)(2,1)} %get-tuple-element.55) | copy-start | bytes 4718596
  113.1 30.0 %copy-start.35 = (bf16[32,48,128]{2,1,0:T(8,128)(2,1)S(1)}, bf16[32,48,128]{2,1,0:T(8,128)(2,1)}, u32[]{:S(2)}) copy-start(bf16[32,48,128]{2,1,0:T(8,128)(2,1)} %get-tuple-element.56.qp_ref) | copy-start | bytes 1179652
  113.1 30.0 %copy-start.39 = (f32[64,3072]{1,0:T(8,128)S(1)}, f32[64,3072]{1,0:T(8,128)}, u32[]{:S(2)}) copy-start(f32[64,3072]{1,0:T(8,128)} %copy-done.38) | copy-start | bytes 2359300
  141.5 75.8 %collective-permute-start = (bf16[8,96,1024]{2,1,0:T(8,128)(2,1)}, bf16[8,96,1024]{2,1,0:T(8,128)(2,1)}, u32[]{:S(2)}, u32[]{:S(2)}) collective-permute-start(bf16[8,96,1024]{2,1,0:T(8,128)(2,1)} %get-tuple-element.81), channel_id=1, source_target_pairs={{0,1},{1,0},{2,3},{3,2},{4,5},{5,4},{6,7},{7,6},{8,9},{9,8},{10,11... | collective-permute-start | bytes 4718600 | tf_op jit(solution)/shard_map/ppermute | solution.py:1049
  142.0 75.2 %collective-permute-start.1 = (bf16[8,96,1024]{2,1,0:T(8,128)(2,1)}, bf16[8,96,1024]{2,1,0:T(8,128)(2,1)}, u32[]{:S(2)}, u32[]{:S(2)}) collective-permute-start(bf16[8,96,1024]{2,1,0:T(8,128)(2,1)} %get-tuple-element.83), channel_id=1, source_target_pairs={{0,4},{2,6},{4,0},{6,2},{8,12},{10,14},{12,8},{14,10},{16,20},{18,... | collective-permute-start | bytes 4718600 | tf_op jit(solution)/shard_map/ppermute | solution.py:1050
  142.6 74.7 %collective-permute-start.2 = (bf16[8,96,1024]{2,1,0:T(8,128)(2,1)}, bf16[8,96,1024]{2,1,0:T(8,128)(2,1)}, u32[]{:S(2)}, u32[]{:S(2)}) collective-permute-start(bf16[8,96,1024]{2,1,0:T(8,128)(2,1)} %get-tuple-element.85), channel_id=1, source_target_pairs={{0,8},{2,10},{4,12},{6,14},{8,0},{10,2},{12,4},{14,6},{16,24},{18,... | collective-permute-start | bytes 4718600 | tf_op jit(solution)/shard_map/ppermute | solution.py:1050
  143.1 69.0 %copy-start.3 = (bf16[1024,1024]{1,0:T(8,128)(2,1)S(1)}, bf16[1024,1024]{1,0:T(8,128)(2,1)}, u32[]{:S(2)}) copy-start(bf16[1024,1024]{1,0:T(8,128)(2,1)} %wk_ref.3) | copy-start | bytes 6291460
  181.3 1.6 copy-start.8
  183.7 1.9 copy-start.9
  186.6 25.6 %copy-start.1 = (bf16[1024,1024]{1,0:T(8,128)(2,1)S(1)}, bf16[1024,1024]{1,0:T(8,128)(2,1)}, u32[]{:S(2)}) copy-start(bf16[1024,1024]{1,0:T(8,128)(2,1)} %wq_ref.3) | copy-start | bytes 6291460
  186.6 25.6 %copy-start.21 = (f32[192,1024]{1,0:T(8,128)S(1)}, f32[192,1024]{1,0:T(8,128)}, u32[]{:S(2)}) copy-start(f32[192,1024]{1,0:T(8,128)} %copy-done.20) | copy-start | bytes 2359300
  186.6 25.6 %copy-start.28 = (f32[1024]{0:T(1024)S(1)}, f32[1024]{0:T(1024)}, u32[]{:S(2)}) copy-start(f32[1024]{0:T(1024)} %param.16) | copy-start | bytes 12292
  212.2 1.6 copy-start.5
  213.8 3.4 %copy-start.13 = (bf16[8,96,1024]{2,1,0:T(8,128)(2,1)S(1)}, bf16[8,96,1024]{2,1,0:T(8,128)(2,1)}, u32[]{:S(2)}) copy-start(bf16[8,96,1024]{2,1,0:T(8,128)(2,1)} %copy-done.12) | copy-start | bytes 4718596
  213.8 3.4 %copy-start.15 = (bf16[8,96,1024]{2,1,0:T(8,128)(2,1)S(1)}, bf16[8,96,1024]{2,1,0:T(8,128)(2,1)}, u32[]{:S(2)}) copy-start(bf16[8,96,1024]{2,1,0:T(8,128)(2,1)} %copy-done.14) | copy-start | bytes 4718596
  213.8 3.5 %copy-start.17 = (bf16[8,96,1024]{2,1,0:T(8,128)(2,1)S(1)}, bf16[8,96,1024]{2,1,0:T(8,128)(2,1)}, u32[]{:S(2)}) copy-start(bf16[8,96,1024]{2,1,0:T(8,128)(2,1)} %copy-done.16) | copy-start | bytes 4718596
  (19 other events, 20.2 us)

commit v3 on v2

--- a/solution.py
+++ b/solution.py
@@ -369,62 +369,6 @@
         a, b = x[:, p * 256 : p * 256 + 128], x[:, p * 256 + 128 : (p + 1) * 256]
         ref[0, :, p * 128 : (p + 1) * 128] = pair_low(a, b, low).astype(BF16)
         ref[1, :, p * 128 : (p + 1) * 128] = pair_high(a, b, low).astype(BF16)
-
-
-def pack_kernel(half, frames_ref, gain_ref, wq_ref, wk_ref, wv_ref, kv_ref, q_ref, halves_ref, act_ref):
-    @pl.when(pl.program_id(0) == 0)
-    def _():
-        x = frames_ref[...]
-        r = lax.rsqrt(jnp.mean(x * x, axis=-1, keepdims=True) + EPSILON)
-        normed = x * r * gain_ref[...]
-        act_ref[...] = normed.astype(BF16)
-        store_halves(halves_ref, normed)
-
-    act = act_ref[...]
-    q = nn_dot(act, wq_ref[...]).astype(BF16).astype(F32) * 0.125
-    k = nn_dot(act, wk_ref[...])
-    v = nn_dot(act, wv_ref[...])
-    rows = q.shape[0]
-    low = low_lanes((rows, 128))
-    low_h = low_lanes((half // 2, 128))
-    for p in range(q.shape[1] // 128):
-        at = slice(p * 128, (p + 1) * 128)
-        k2, v2, q2 = k[:, at], v[:, at], q[:, at]
-        kv_a = jnp.where(low, k2, pltpu.roll(v2, 64, 1)).astype(BF16)
-        kv_b = jnp.where(low, pltpu.roll(k2, 64, 1), v2).astype(BF16)
-        for s in range(2):
-            span = slice(s * half, (s + 1) * half)
-            kv_ref[2 * p, s] = kv_a[span]
-            kv_ref[2 * p + 1, s] = kv_b[span]
-            top = q2[s * half : s * half + half // 2]
-            bot = q2[s * half + half // 2 : (s + 1) * half]
-            q_ref[2 * p, s] = jnp.where(low_h, top, pltpu.roll(bot, 64, 1)).astype(BF16)
-            q_ref[2 * p + 1, s] = jnp.where(low_h, pltpu.roll(top, 64, 1), bot).astype(BF16)
-
-
-def project_and_pack(frames, gain, w_query, w_key, w_value):
-    rows, width = frames.shape
-    heads, half, step = width // 64, rows // 2, 256
-    w_spec = pl.BlockSpec((width, step), lambda i: (0, i))
-    whole = lambda i: (0, 0)
-    return pl.pallas_call(
-        functools.partial(pack_kernel, half),
-        grid=(width // step,),
-        in_specs=[pl.BlockSpec((rows, width), whole), pl.BlockSpec((1, width), whole), w_spec, w_spec, w_spec],
-        out_specs=[
-            pl.BlockSpec((step // 64, 2, half, 128), lambda i: (i, 0, 0, 0)),
-            pl.BlockSpec((step // 64, 2, half // 2, 128), lambda i: (i, 0, 0, 0)),
-            pl.BlockSpec((2, rows, width // 2), lambda i: (0, 0, 0)),
-        ],
-        out_shape=[
-            jax.ShapeDtypeStruct((heads, 2, half, 128), BF16),
-            jax.ShapeDtypeStruct((heads, 2, half // 2, 128), BF16),
-            jax.ShapeDtypeStruct((2, rows, width // 2), BF16),
-        ],
-        scratch_shapes=[pltpu.VMEM((rows, width), BF16)],
-        compiler_params=pltpu.CompilerParams(vmem_limit_bytes=40 << 20),
-        name="project_and_pack",
-    )(frames, gain.reshape(1, width), w_query, w_key, w_value)
 
 
 def block_bounds(len_ref, items, qpos, first, last, key_block):
@@ -777,7 +721,7 @@
             pltpu.VMEM((rows, width), BF16),
             pltpu.VMEM((rows, width), F32),
         ],
-        compiler_params=pltpu.CompilerParams(vmem_limit_bytes=40 << 20),
+        compiler_params=pltpu.CompilerParams(vmem_limit_bytes=28 << 20),
         name="feed",
     )(
         blocks, frames, cotangent, w_out, gain.reshape(1, width), w_up, b_up.reshape(1, ff), w_down,
@@ -785,61 +729,16 @@
     )
 
 
-def input_grad_kernel(
-    dkv_ref, dq_ref, frames_ref, grad_mid_ref, gain_ref, wq_ref, wk_ref, wv_ref, gain2_grad_ref, b_up_grad_ref,
-    b_down_grad_ref, grads_ref, out_ref, small_ref,
-):
-    rows, width = frames_ref.shape
-    quarter = rows // 4
-    low_q, low_h = low_lanes((quarter, 128)), low_lanes((2 * quarter, 128))
-    for zy in range(8):
-        for s in range(2):
-            j = (zy * 2 + s) * 2
-            first = 2 * s * quarter
-            a, b = dq_ref[j].astype(F32), dq_ref[j + 1].astype(F32)
-            at = slice(zy * 128, (zy + 1) * 128)
-            grads_ref[first : first + quarter, at] = pair_low(a, b, low_q).astype(BF16)
-            grads_ref[first + quarter : first + 2 * quarter, at] = pair_high(a, b, low_q).astype(BF16)
-            a, b = dkv_ref[j].astype(F32), dkv_ref[j + 1].astype(F32)
-            at = slice(width + zy * 128, width + (zy + 1) * 128)
-            grads_ref[first : first + 2 * quarter, at] = pair_low(a, b, low_h).astype(BF16)
-            at = slice(2 * width + zy * 128, 2 * width + (zy + 1) * 128)
-            grads_ref[first : first + 2 * quarter, at] = pair_high(a, b, low_h).astype(BF16)
-    g = nt_dot(grads_ref[:, :width], wq_ref[...])
-    g += nt_dot(grads_ref[:, width : 2 * width], wk_ref[...])
-    g += nt_dot(grads_ref[:, 2 * width :], wv_ref[...])
-    x = frames_ref[...]
-    r = lax.rsqrt(jnp.mean(x * x, axis=-1, keepdims=True) + EPSILON)
-    n = x * r
-    gain_grad = jnp.sum(g * n, axis=0, keepdims=True)
-    small_ref[...] = jnp.zeros_like(small_ref)
-    for d in range(small_ref.shape[0]):
-        at = slice(d // 4 * 128, (d // 4 + 1) * 128)
-        small_ref[d, 0:1] = gain_grad[:, at]
-        small_ref[d, 1:2] = gain2_grad_ref[:, at]
-        small_ref[d, 2:3] = b_down_grad_ref[:, at]
-        small_ref[d, 3:4] = b_up_grad_ref[:, d * 128 : (d + 1) * 128]
-    g = g * gain_ref[...]
-    out_ref[...] = grad_mid_ref[...] + r * (g - n * jnp.mean(g * n, axis=-1, keepdims=True))
-
-
-def input_grad(dkv, dq, frames, grad_mid, gain, w_query, w_key, w_value, gain2_grad, b_up_grad, b_down_grad):
-    rows, width = frames.shape
-    shape = jax.ShapeDtypeStruct
-    return pl.pallas_call(
-        input_grad_kernel,
-        in_specs=[pl.BlockSpec(memory_space=pltpu.VMEM)] * 11,
-        out_specs=[pl.BlockSpec(memory_space=pltpu.VMEM)] * 3,
-        out_shape=[shape((rows, 3 * width), BF16), shape((rows, width), F32), shape((32, 8, 128), F32)],
-        compiler_params=pltpu.CompilerParams(vmem_limit_bytes=24 << 20),
-        name="input_grad",
-    )(
-        dkv, dq, frames, grad_mid, gain.reshape(1, width), w_query, w_key, w_value, gain2_grad, b_up_grad, b_down_grad
-    )
-
-
 MESH = pl.DeviceIdType.MESH
 ALL = ("blk", "grp")
+
+
+def in_hbm(*arrays):
+    return [pltpu.with_memory_space_constraint(x, pltpu.HBM) for x in arrays]
+
+
+def in_vmem(*arrays):
+    return [pltpu.with_memory_space_constraint(x, pltpu.VMEM) for x in arrays]
 
 
 def place(index):
@@ -855,6 +754,10 @@
     return lax.axis_index("blk") * 2 + lax.axis_index("grp")
 
 
+def sibling_of(core):
+    return {"blk": lax.axis_index("blk") + 1 - 2 * core, "grp": lax.axis_index("grp")}
+
+
 def greet_all(me, n):
     barrier = pltpu.get_barrier_semaphore()
 
@@ -871,65 +774,119 @@
     )
 
 
-def to_heads_kernel(n, kv_in, q_in, kv_out, q_out, send, recv, local, pair):
+def to_heads_kernel(
+    n, gain, frames_in, wq_in, wk_in, wv_in, kv_out, q_out, halves,
+    frames, act, wq, wk, wv, kv_own, q_own, send, recv, local, pair,
+):
     me = own_index()
     head, core = head_of(me)
+    rows, width = frames.shape
+    half = rows // 2
+    weights = [
+        pltpu.make_async_copy(src, dst, local.at[k])
+        for k, (src, dst) in enumerate(((frames_in, frames), (wq_in, wq), (wk_in, wk), (wv_in, wv)))
+    ]
+    for copy in weights:
+        copy.start()
     greet_all(me, n)
-
-    def copies(i, src):
-        other = lax.rem(me + i, n)
+    weights[0].wait()
+    x = frames[...]
+    r = lax.rsqrt(jnp.mean(x * x, axis=-1, keepdims=True) + EPSILON)
+    normed = x * r * gain[...]
+    act[...] = normed.astype(BF16)
+    store_halves(halves, normed)
+    for copy in weights[1:]:
+        copy.wait()
+
+    def copies(other, src):
         h, c = head_of(other)
         kv_at = core if src is not me else c
         return (
-            remote(kv_in.at[h, c], kv_out.at[src, kv_at], send.at[0, i], recv.at[0, src], place(other)),
-            remote(q_in.at[h, c], q_out.at[src], send.at[1, i], recv.at[1, src], place(other)),
+            remote(kv_own.at[h, c], kv_out.at[src, kv_at], send.at[0, other], recv.at[0, src], place(other)),
+            remote(q_own.at[h, c], q_out.at[src], send.at[1, other], recv.at[1, src], place(other)),
         )
+
+    low = low_lanes((rows, 128))
+    low_h = low_lanes((half // 2, 128))
+    groups = width // 256
+
+    @pl.loop(0, groups)
+    def _(i):
+        group = lax.rem(lax.div(me, n // groups) + 1 + i, groups)
+        columns = pl.ds(pl.multiple_of(group * 256, 256), 256)
+        q = nn_dot(act[...], wq[:, columns]).astype(BF16).astype(F32) * 0.125
+        k = nn_dot(act[...], wk[:, columns])
+        v = nn_dot(act[...], wv[:, columns])
+        for p in range(2):
+            at = slice(p * 128, (p + 1) * 128)
+            k2, v2, q2 = k[:, at], v[:, at], q[:, at]
+            kv_a = pair_low(k2, v2, low).astype(BF16)
+            kv_b = pair_high(k2, v2, low).astype(BF16)
+            h = group * 4 + 2 * p
+            for s in range(2):
+                span = slice(s * half, (s + 1) * half)
+                kv_own[h, s] = kv_a[span]
+                kv_own[h + 1, s] = kv_b[span]
+                top = q2[s * half : s * half + half // 2]
+                bot = q2[s * half + half // 2 : (s + 1) * half]
+                q_own[h, s] = pair_low(top, bot, low_h).astype(BF16)
+                q_own[h + 1, s] = pair_high(top, bot, low_h).astype(BF16)
+
+        @pl.loop(0, n // groups)
+        def _(j):
+            other = group * (n // groups) + j
+
+            @pl.when(other != me)
+            def _():
+                for copy in copies(other, me):
+                    copy.start()
+
+    kv_out[me, core] = kv_own[head, core]
+    q_out[me] = q_own[head, core]
 
     @pl.loop(1, n)
     def _(i):
-        for copy in copies(i, me):
-            copy.start()
-
-    own = (
-        pltpu.make_async_copy(kv_in.at[head, core], kv_out.at[me, core], local.at[0]),
-        pltpu.make_async_copy(q_in.at[head, core], q_out.at[me], local.at[1]),
-    )
-    for copy in own:
-        copy.start()
-    for copy in own:
-        copy.wait()
-
-    @pl.loop(1, n)
-    def _(i):
-        for copy in copies(i, lax.rem(me + i, n)):
+        other = lax.rem(me + i, n)
+        for copy in copies(other, other):
             copy.wait()
 
-    sibling = {"blk": lax.axis_index("blk") + 1 - 2 * core, "grp": lax.axis_index("grp")}
-    swap = remote(kv_out.at[:, core], kv_out.at[:, core], pair.at[0], pair.at[1], sibling)
+    swap = remote(kv_out.at[:, core], kv_out.at[:, core], pair.at[0], pair.at[1], sibling_of(core))
     swap.start()
     swap.wait()
 
 
-def to_heads(kv, q, n):
-    half = kv.shape[2]
-    anywhere = pl.BlockSpec(memory_space=pl.ANY)
+def to_heads(frames, gain, w_query, w_key, w_value, n):
+    rows, width = frames.shape
+    half = rows // 2
+    vmem = pl.BlockSpec(memory_space=pltpu.VMEM)
+    hbm = pl.BlockSpec(memory_space=pltpu.HBM)
     return pl.pallas_call(
         functools.partial(to_heads_kernel, n),
-        in_specs=[anywhere] * 2,
-        out_specs=[anywhere] * 2,
+        in_specs=[vmem] + [hbm] * 4,
+        out_specs=[vmem] * 3,
         out_shape=[
             jax.ShapeDtypeStruct((n, 2, half, 128), BF16),
             jax.ShapeDtypeStruct((n, half // 2, 128), BF16),
+            jax.ShapeDtypeStruct((2, rows, width // 2), BF16),
         ],
         scratch_shapes=[
+            pltpu.VMEM((rows, width), F32),
+            pltpu.VMEM((rows, width), BF16),
+            pltpu.VMEM((width, width), BF16),
+            pltpu.VMEM((width, width), BF16),
+            pltpu.VMEM((width, width), BF16),
+            pltpu.VMEM((width // 64, 2, half, 128), BF16),
+            pltpu.VMEM((width // 64, 2, half // 2, 128), BF16),
             pltpu.SemaphoreType.DMA((2, n)),
             pltpu.SemaphoreType.DMA((2, n)),
-            pltpu.SemaphoreType.DMA((2,)),
+            pltpu.SemaphoreType.DMA((4,)),
             pltpu.SemaphoreType.DMA((2,)),
         ],
-        compiler_params=pltpu.CompilerParams(collective_id=0, has_side_effects=True),
+        compiler_params=pltpu.CompilerParams(
+            collective_id=0, has_side_effects=True, vmem_limit_bytes=16 << 20
+        ),
         name="to_heads",
-    )(kv, q)
+    )(gain.reshape(1, width), *in_hbm(frames, w_query, w_key, w_value))
 
 
 def exchange_kernel(n, x_in, x_out, send, recv, local):
@@ -954,91 +911,20 @@
 
 
 def exchange(x, n, collective_id):
-    anywhere = pl.BlockSpec(memory_space=pl.ANY)
+    vmem = pl.BlockSpec(memory_space=pltpu.VMEM)
     return pl.pallas_call(
         functools.partial(exchange_kernel, n),
-        in_specs=[anywhere],
-        out_specs=anywhere,
+        in_specs=[vmem],
+        out_specs=vmem,
         out_shape=jax.ShapeDtypeStruct(x.shape, x.dtype),
         scratch_shapes=[
             pltpu.SemaphoreType.DMA((n,)),
             pltpu.SemaphoreType.DMA((n,)),
             pltpu.SemaphoreType.DMA,
         ],
-        compiler_params=pltpu.CompilerParams(collective_id=collective_id, has_side_effects=True),
+        compiler_params=pltpu.CompilerParams(collective_id=collective_id, has_side_effects=True, vmem_limit_bytes=8 << 20),
         name="exchange",
     )(x)
-
-
-def from_heads_kernel(n, dkv_in, dq_in, dkv_out, dq_out, theirs, total, send, recv, local, pair):
-    me = own_index()
-    head, core = head_of(me)
-    greet_all(me, n)
-    sibling = {"blk": lax.axis_index("blk") + 1 - 2 * core, "grp": lax.axis_index("grp")}
-    swap = remote(dkv_in.at[:, 1 - core], theirs, pair.at[0], pair.at[1], sibling)
-    swap.start()
-
-    def dq_copy(i, src):
-        other = lax.rem(me + i, n)
-        return remote(dq_in.at[other], dq_out.at[src], send.at[1, i], recv.at[1, src], place(other))
-
-    def dkv_copy(i, src):
-        other = lax.rem(me + i, n)
-        return remote(total.at[other], dkv_out.at[src], send.at[0, i], recv.at[0, src], place(other))
-
-    @pl.loop(1, n)
-    def _(i):
-        dq_copy(i, me).start()
-
-    own_q = pltpu.make_async_copy(dq_in.at[me], dq_out.at[me], local.at[1])
-    own_q.start()
-    swap.wait()
-
-    def add(j):
-        total[j] = (dkv_in[j, core] + theirs[j]).astype(BF16)
-
-    @pl.loop(1, n)
-    def _(i):
-        add(lax.rem(me + i, n))
-        dkv_copy(i, me).start()
-
-    add(me)
-    own = pltpu.make_async_copy(total.at[me], dkv_out.at[me], local.at[0])
-    own.start()
-    own.wait()
-    own_q.wait()
-
-    @pl.loop(1, n)
-    def _(i):
-        src = lax.rem(me + i, n)
-        dkv_copy(i, src).wait()
-        dq_copy(i, src).wait()
-
-
-def from_heads(dkv, dq, n):
-    half = dkv.shape[2]
-    anywhere = pl.BlockSpec(memory_space=pl.ANY)
-    return pl.pallas_call(
-        functools.partial(from_heads_kernel, n),
-        in_specs=[pl.BlockSpec(memory_space=pltpu.VMEM), anywhere],
-        out_specs=[anywhere] * 2,
-        out_shape=[
-            jax.ShapeDtypeStruct((n, half, 128), BF16),
-            jax.ShapeDtypeStruct(dq.shape, BF16),
-        ],
-        scratch_shapes=[
-            pltpu.VMEM((n, half, 128), F32),
-            pltpu.VMEM((n, half, 128), BF16),
-            pltpu.SemaphoreType.DMA((2, n)),
-            pltpu.SemaphoreType.DMA((2, n)),
-            pltpu.SemaphoreType.DMA((2,)),
-            pltpu.SemaphoreType.DMA((2,)),
-        ],
-        compiler_params=pltpu.CompilerParams(
-            collective_id=1, has_side_effects=True, vmem_limit_bytes=24 << 20
-        ),
-        name="from_heads",
-    )(dkv, dq)
 
 
 BITS = {"core": 1, "y": 2, "z0": 4, "z1": 8}
@@ -1054,10 +940,6 @@
     if axis == "x":
         return lax.axis_index("grp")
     return lax.rem(lax.div(lax.axis_index("blk"), BITS[axis]), 2)
-
-
-def sibling_of(core):
-    return {"blk": lax.axis_index("blk") + 1 - 2 * core, "grp": lax.axis_index("grp")}
 
 
 def across(axis):
@@ -1074,8 +956,8 @@
 
 def share_kernel(
     n, blocks_in, hidden, grad_before, act2, mixed, low, attn,
-    blocks_out, keep_a, send_a, keep_b, send_b, keep_c, send_c,
-    hidden2, before2, act2_2, mixed2, low2, attn2, tile, send, recv, local, pair_send, pair_recv,
+    blocks_out, keep_a_out, send_a_out, keep_b_out, send_b_out, keep_c_out, send_c_out,
+    keep_a, send_a, keep_b, send_b, keep_c, send_c, hidden2, before2, act2_2, mixed2, low2, attn2, tile, send, recv, local, out, pair_send, pair_recv,
 ):
     me = own_index()
     head, core = head_of(me)
@@ -1127,6 +1009,12 @@
         def _():
             away[at, row : row + value.shape[0]] = value
 
+    flushes = []
+
+    def flush(src, dst):
+        flushes.append(pltpu.make_async_copy(src, dst, out.at[len(flushes)]))
+        flushes[-1].start()
+
     pairs[0].wait()
     pairs[1].wait()
 
@@ -1152,31 +1040,42 @@
             else:
                 put(keep_c, send_c, z_mine, z0, (z1 * 2 + y) * 2 + x, row, value)
 
+    flush(keep_a, keep_a_out)
+    flush(send_a, send_a_out)
     pairs[2].wait()
     pairs[3].wait()
     for slab in range(3):
         spread_rows(act2_2, before2, slab, True, 32 * slab)
+    flush(keep_b, keep_b_out)
+    flush(send_b, send_b_out)
     spread_rows(act2_2, before2, 3, False, 32)
     pairs[4].wait()
     pairs[5].wait()
     spread_rows(mixed2, attn2, 0, False, 64)
+    flush(keep_c, keep_c_out)
+    flush(send_c, send_c_out)
     own.wait()
 
     @pl.loop(1, n)
     def _(i):
         copy_with(i, lax.rem(me + i, n)).wait()
 
+    for copy in flushes:
+        copy.wait()
+
 
 def share(blocks, hidden, grad_before, act2, mixed, low, attn, n):
     rows, width = low.shape
     vmem = pl.BlockSpec(memory_space=pltpu.VMEM)
+    hbm = pl.BlockSpec(memory_space=pltpu.HBM)
     shape = jax.ShapeDtypeStruct
     return pl.pallas_call(
         functools.partial(share_kernel, n),
         in_specs=[vmem] * 7,
-        out_specs=[vmem] * 7,
-        out_shape=[shape(blocks.shape, BF16)] + [shape((8, 96, width), BF16)] * 6,
+        out_specs=[vmem] + [hbm] * 6,
+        out_shape=[shape(blocks.shape, BF16)] + [pltpu.HBM((8, 96, width), BF16)] * 6,
         scratch_shapes=[
+            *[pltpu.VMEM((8, 96, width), BF16)] * 6,
             pltpu.VMEM((2 * rows, hidden.shape[2]), BF16),
             pltpu.VMEM((2 * rows, grad_before.shape[1]), BF16),
             pltpu.VMEM((2 * rows, width // 2), BF16),
@@ -1189,9 +1088,10 @@
             pltpu.SemaphoreType.DMA,
             pltpu.SemaphoreType.DMA((6,)),
             pltpu.SemaphoreType.DMA((6,)),
+            pltpu.SemaphoreType.DMA((6,)),
         ],
         compiler_params=pltpu.CompilerParams(
-            collective_id=3, has_side_effects=True, vmem_limit_bytes=40 << 20
+            collective_id=3, has_side_effects=True, vmem_limit_bytes=26 << 20
         ),
         name="share",
     )(blocks, hidden, grad_before, act2, mixed, low, attn)
@@ -1236,27 +1136,68 @@
         return self.kept[...].astype(F32) + self.landing[self.stage - 1][...].astype(F32)
 
 
-def gather_kernel(
-    n, act1, qkv, keep_a, got_a, keep_b, got_b, keep_c, got_c, small_in,
-    q_out, k_out, v_out, o_out, up_out, down_out, small_out,
+def finish_kernel(
+    n, dkv_in, dq_in, gain, gain2_grad, b_up_grad, b_down_grad, act1, frames_in, grad_mid_in, wq_in, wk_in, wv_in,
+    keep_a, got_a, keep_b, got_b, keep_c, got_c,
+    frames_out, q_out, k_out, v_out, o_out, up_out, down_out, small_out,
+    theirs, total, dkv_all, dq_all, frames, grad_mid, wq, wk, wv, small_in, new_a, new_b, new_c,
     act1_2, qkv2, sum_a, sum_b, sum_c, sum_q, sum_k, sum_v,
     a2, a3, a4, b2, b3, b4, c2, c3, c4,
     q1, q2, q3, q4, k1, k2, k3, k4, v1, v2, v3, v4, small_all,
-    send, recv, small_send, small_recv, pair_send, pair_recv,
+    send, recv, dq_send, dq_recv, dkv_send, dkv_recv, small_send, small_recv, pair_send, pair_recv, local,
 ):
     me = own_index()
     head, core = head_of(me)
-    rows, width = qkv.shape[0], qkv.shape[1] // 3
+    rows, width = frames.shape
+    quarter = rows // 4
+    sums = [sum_a, sum_b, sum_c, sum_q, sum_k, sum_v]
+    news = [new_a, new_b, new_c]
+    fetches = [
+        pltpu.make_async_copy(src, dst, local.at[k])
+        for k, (src, dst) in enumerate(
+            (
+                (keep_a, sum_a), (got_a, new_a), (keep_b, sum_b), (got_b, new_b), (keep_c, sum_c), (got_c, new_c),
+                (wq_in, wq), (wk_in, wk), (wv_in, wv), (frames_in, frames), (grad_mid_in, grad_mid),
+            )
+        )
+    ]
+    for copy in fetches:
+        copy.start()
     greet_all(me, n)
     sibling = sibling_of(core)
-    theirs = pl.ds(rows, rows)
-    pairs = [
-        remote(act1.at[1 - core], act1_2.at[theirs], pair_send.at[0], pair_recv.at[0], sibling),
-        remote(qkv, qkv2.at[theirs], pair_send.at[1], pair_recv.at[1], sibling),
-    ]
-    for copy in pairs:
-        copy.start()
-    sums = [sum_a, sum_b, sum_c, sum_q, sum_k, sum_v]
+    swap = remote(dkv_in.at[:, 1 - core], theirs, pair_send.at[0], pair_recv.at[0], sibling)
+    swap.start()
+    act1_copy = remote(act1.at[1 - core], act1_2.at[pl.ds(rows, rows)], pair_send.at[1], pair_recv.at[1], sibling)
+
+    def to_all(src_ref, dst_ref, sends, recvs):
+        def copy_with(i, src):
+            other = lax.rem(me + i, n)
+            return remote(src_ref.at[other], dst_ref.at[src], sends.at[i], recvs.at[src], place(other))
+
+        return copy_with
+
+    dq_copy = to_all(dq_in, dq_all, dq_send, dq_recv)
+    dkv_copy = to_all(total, dkv_all, dkv_send, dkv_recv)
+    small_copy = to_all(small_in, small_all, small_send, small_recv)
+
+    @pl.loop(1, n)
+    def _(i):
+        dq_copy(i, me).start()
+
+    swap.wait()
+
+    def add(j):
+        return (dkv_in[j, core] + theirs[j]).astype(BF16)
+
+    @pl.loop(1, n)
+    def _(i):
+        other = lax.rem(me + i, n)
+        total[other] = add(other)
+        dkv_copy(i, me).start()
+
+    dkv_all[me] = add(me)
+    dq_all[me] = dq_in[me]
+    act1_copy.start()
     dims = [("z1", "z0", "y"), ("z1", "z0", "x"), ("z1", "y", "x")] + [("z1", "z0", "y", "x")] * 3
     orders = [
         ("y", "z0", "z1"), ("z0", "x", "z1"), ("x", "y", "z1"),
@@ -1264,44 +1205,90 @@
     ]
     landings = [(a2, a3, a4), (b2, b3, b4), (c2, c3, c4), (q1, q2, q3, q4), (k1, k2, k3, k4), (v1, v2, v3, v4)]
     parts = [
-        Part(total, names, order, landing, send.at[k], recv.at[k])
-        for k, (total, names, order, landing) in enumerate(zip(sums, dims, orders, landings))
+        Part(whole, names, order, landing, send.at[k], recv.at[k])
+        for k, (whole, names, order, landing) in enumerate(zip(sums, dims, orders, landings))
     ]
-    for part, total, keep, got in zip(parts, sums, (keep_a, keep_b, keep_c), (got_a, got_b, got_c)):
+    for k in range(3):
+        whole, new = sums[k], news[k]
+        fetches[2 * k].wait()
+        fetches[2 * k + 1].wait()
 
         @pl.loop(0, 8)
         def _(k):
             at = (lax.div(k, 4), lax.rem(lax.div(k, 2), 2), lax.rem(k, 2))
-            total[at] = (keep[k].astype(F32) + got[k].astype(F32)).astype(BF16)
-
-        part.start()
-
-    def small_copy(i, src):
-        other = lax.rem(me + i, n)
-        return remote(small_in.at[other], small_all.at[src], small_send.at[i], small_recv.at[src], place(other))
+            whole[at] = (whole[at].astype(F32) + new[at].astype(F32)).astype(BF16)
+
+        parts[k].start()
+
+    act1_own = pltpu.make_async_copy(act1.at[core], act1_2.at[pl.ds(0, rows)], local.at[11])
+    act1_own.start()
 
     @pl.loop(1, n)
     def _(i):
-        small_copy(i, me).start()
-
-    act1_2[:rows] = act1[core]
-    qkv2[:rows] = qkv[...]
-    for copy in pairs:
+        src = lax.rem(me + i, n)
+        dq_copy(i, src).wait()
+        dkv_copy(i, src).wait()
+
+    for part in parts[:3]:
+        part.finish()
+        part.start()
+    low_q, low_h = low_lanes((quarter, 128)), low_lanes((2 * quarter, 128))
+    for zy in range(8):
+        for s in range(2):
+            j = (zy * 2 + s) * 2
+            first = 2 * s * quarter
+            a, b = dq_all[j].astype(F32), dq_all[j + 1].astype(F32)
+            at = slice(zy * 128, (zy + 1) * 128)
+            qkv2[first : first + quarter, at] = pair_low(a, b, low_q).astype(BF16)
+            qkv2[first + quarter : first + 2 * quarter, at] = pair_high(a, b, low_q).astype(BF16)
+            a, b = dkv_all[j].astype(F32), dkv_all[j + 1].astype(F32)
+            at = slice(width + zy * 128, width + (zy + 1) * 128)
+            qkv2[first : first + 2 * quarter, at] = pair_low(a, b, low_h).astype(BF16)
+            at = slice(2 * width + zy * 128, 2 * width + (zy + 1) * 128)
+            qkv2[first : first + 2 * quarter, at] = pair_high(a, b, low_h).astype(BF16)
+    pair = remote(qkv2.at[pl.ds(0, rows)], qkv2.at[pl.ds(rows, rows)], pair_send.at[2], pair_recv.at[2], sibling)
+    pair.start()
+
+    for copy in fetches[6:]:
         copy.wait()
+    g = nt_dot(qkv2[:rows, :width], wq[...])
+    g += nt_dot(qkv2[:rows, width : 2 * width], wk[...])
+    g += nt_dot(qkv2[:rows, 2 * width :], wv[...])
+    act1_copy.wait()
+    act1_own.wait()
+    pair.wait()
     for k in range(3):
         value = tn_dot(act1_2[...], qkv2[:, k * width : (k + 1) * width]).astype(BF16)
         for j in range(16):
             sums[3 + k][j // 8, j // 4 % 2, j // 2 % 2, j % 2] = value[j * 32 : (j + 1) * 32]
         parts[3 + k].start()
-
-    for turn in range(2):
-        for part in parts:
-            part.finish()
-            part.start()
-    for part in parts[3:]:
+    for part in parts[:3]:
         part.finish()
         part.start()
+
+    x = frames[...]
+    r = lax.rsqrt(jnp.mean(x * x, axis=-1, keepdims=True) + EPSILON)
+    norm = x * r
+    gain_grad = jnp.sum(g * norm, axis=0, keepdims=True)
+    small_in[...] = jnp.zeros_like(small_in)
+    for d in range(n):
+        at = slice(d // 4 * 128, (d // 4 + 1) * 128)
+        small_in[d, 0:1] = gain_grad[:, at]
+        small_in[d, 1:2] = gain2_grad[:, at]
+        small_in[d, 2:3] = b_down_grad[:, at]
+        small_in[d, 3:4] = b_up_grad[:, d * 128 : (d + 1) * 128]
+
+    @pl.loop(1, n)
+    def _(i):
+        small_copy(i, me).start()
+
+    g = g * gain[...]
+    frames_out[...] = grad_mid[...] + r * (g - norm * jnp.mean(g * norm, axis=-1, keepdims=True))
     small_all[me] = small_in[me]
+
+    for part in parts[3:] * 3:
+        part.finish()
+        part.start()
 
     @pl.loop(1, n)
     def _(i):
@@ -1321,36 +1308,56 @@
     v_out[...] = parts[5].last()
 
 
-def gather(act1, qkv, keeps, gots, small, n):
-    rows, width = qkv.shape[0], qkv.shape[1] // 3
+def finish(dkv, dq, act1, frames, grad_mid, gain, gain2_grad, b_up_grad, b_down_grad, weights, keeps, gots, n):
+    rows, width = frames.shape
+    parts = [x.reshape(2, 2, 2, *x.shape[1:]) for pair in zip(keeps, gots) for x in pair]
+    half = dkv.shape[2]
     vmem = pl.BlockSpec(memory_space=pltpu.VMEM)
+    hbm = pl.BlockSpec(memory_space=pltpu.HBM)
     shape = jax.ShapeDtypeStruct
     thin, wide = (32, width), (96, width)
     buffers = [pltpu.VMEM((2, 2, 2, *wide), BF16)] * 3 + [pltpu.VMEM((2, 2, 2, 2, *thin), BF16)] * 3
     buffers += [pltpu.VMEM((2,) * k + wide, BF16) for k in (2, 1, 0)] * 3
     buffers += [pltpu.VMEM((2,) * k + thin, BF16) for k in (3, 2, 1, 0)] * 3
+    over_devices = [pltpu.SemaphoreType.DMA((n,))] * 6
     return pl.pallas_call(
-        functools.partial(gather_kernel, n),
-        in_specs=[vmem] * 9,
-        out_specs=[vmem] * 7,
-        out_shape=[shape(thin, F32)] * 4 + [shape((32, 4 * width), F32), shape((128, width), F32), shape((8, 128), F32)],
+        functools.partial(finish_kernel, n),
+        in_specs=[vmem] * 6 + [hbm] * 12,
+        out_specs=[vmem] * 8,
+        out_shape=[shape((rows, width), F32)]
+        + [shape(thin, F32)] * 4
+        + [shape((32, 4 * width), F32), shape((128, width), F32), shape((8, 128), F32)],
         scratch_shapes=[
+            pltpu.VMEM((n, half, 128), F32),
+            pltpu.VMEM((n, half, 128), BF16),
+            pltpu.VMEM((n, half, 128), BF16),
+            pltpu.VMEM((n, half // 2, 128), BF16),
+            pltpu.VMEM((rows, width), F32),
+            pltpu.VMEM((rows, width), F32),
+            pltpu.VMEM((width, width), BF16),
+            pltpu.VMEM((width, width), BF16),
+            pltpu.VMEM((width, width), BF16),
+            pltpu.VMEM((n, 8, 128), F32),
+            *[pltpu.VMEM((2, 2, 2, *wide), BF16)] * 3,
             pltpu.VMEM((2 * rows, width // 2), BF16),
             pltpu.VMEM((2 * rows, 3 * width), BF16),
             *buffers,
             pltpu.VMEM((n, 8, 128), F32),
             pltpu.SemaphoreType.DMA((6, 4)),
             pltpu.SemaphoreType.DMA((6, 4)),
-            pltpu.SemaphoreType.DMA((n,)),
-            pltpu.SemaphoreType.DMA((n,)),
-            pltpu.SemaphoreType.DMA((2,)),
-            pltpu.SemaphoreType.DMA((2,)),
+            *over_devices,
+            pltpu.SemaphoreType.DMA((3,)),
+            pltpu.SemaphoreType.DMA((3,)),
+            pltpu.SemaphoreType.DMA((12,)),
         ],
         compiler_params=pltpu.CompilerParams(
-            collective_id=4, has_side_effects=True, vmem_limit_bytes=40 << 20
+            collective_id=4, has_side_effects=True, vmem_limit_bytes=42 << 20
         ),
-        name="gather",
-    )(act1, qkv, keeps[0], gots[0], keeps[1], gots[1], keeps[2], gots[2], small)
+        name="finish",
+    )(
+        *in_vmem(dkv, dq), gain.reshape(1, width), gain2_grad, b_up_grad, b_down_grad,
+        *in_hbm(act1, frames, grad_mid, *weights, *parts),
+    )
 
 
 def shards_heads(
@@ -1362,8 +1369,7 @@
     core_word = bit_of("core").astype(jnp.int32).reshape(1)
     qpos = jnp.asarray(packed_positions(n, half))
 
-    kv_blocks, q_blocks, act1 = project_and_pack(frames, norm1_gain, w_query, w_key, w_value)
-    kv, q = to_heads(kv_blocks, q_blocks, n)
+    kv, q, act1 = to_heads(frames, norm1_gain, w_query, w_key, w_value, n)
     kv_rows = kv.reshape(n * rows, 128)
     out_t, lse, out_blocks = mix(lengths, core_word, kv_rows, q, qpos)
     mixed_blocks = exchange(out_blocks, n, 2)
@@ -1377,13 +1383,9 @@
     gots = [flipped(part, axis) for part, axis in zip(parts[1::2], ("x", "y", "z0"))]
     dkv, dq = mix_back(lengths, core_word, kv_rows, q, grad_blocks, qpos, out_t, lse)
 
-    dkv_blocks, dq_blocks = from_heads(dkv.reshape(n, 2, half, 128), dq, n)
-    qkv, frames_grad, small = input_grad(
-        dkv_blocks, dq_blocks, frames, grad_middle, norm1_gain, w_query, w_key, w_value,
-        norm2_gain_grad, b_up_grad, b_down_grad,
-    )
-    w_query_grad, w_key_grad, w_value_grad, w_out_grad, w_up_grad, w_down_grad, small = gather(
-        act1, qkv, keeps, gots, small, n
+    frames_grad, w_query_grad, w_key_grad, w_value_grad, w_out_grad, w_up_grad, w_down_grad, small = finish(
+        dkv.reshape(n, 2, half, 128), dq, act1, frames, grad_middle, norm1_gain, norm2_gain_grad, b_up_grad,
+        b_down_grad, (w_query, w_key, w_value), keeps, gots, n,
     )
     part = width // n
     turn = lax.rem(own_index(), 128 // part) * part

time: 309 us -> 257 us (0.83); the launches traced: 313 us -> 257 us
  Pallas kernels: 278 us -> 241 us
  local copies, waits for them, and re-layouts: 32.2 us -> 9.75 us
  waiting for transfers between devices: 0.01 us -> 3.18 us
    pallas_call x6 -> x3, Pallas kernels: 172 us -> 147 us  [the longest x1 97.8 us: finish(): pl.pallas_call(functools.partial(finish_kernel, n), in_specs=[vmem] * 6 +...]
    unnamed x86 -> x47, local copies, waits for them, and re-layouts: 31.1 us -> 8.64 us
    pallas_call x1, Pallas kernels: 38.1 us -> 32.5 us  [mix_back(): pl.pallas_call(functools.partial(back_kernel, lengths.shape[0], chunks, k...]
    pallas_call x1, Pallas kernels: 26.1 us -> 22.3 us  [mix(): pl.pallas_call(functools.partial(mix_kernel, lengths.shape[0], chunks, ke...]
  transfers between devices with their start and end apart: 3 -> 3, of which waited for: 0 -> 3; matrix products, arithmetic and copies ran while one was open for 0% -> 0% of each run, Pallas kernels for 21% -> 13%
where the time goes in v3:
time: 257 us
  Pallas kernels  241 us (94%)
  local copies, waits for them, and re-layouts  9.75 us (4%)
  waiting for transfers between devices  3.18 us (1%)
    pallas_call x1, Pallas kernels, finish(): pl.pallas_call(functools.partial(finish_kernel, n), in_specs=[vmem] * 6 +...  97.8 us
    pallas_call x1, Pallas kernels, mix_back(): pl.pallas_call(functools.partial(back_kernel, lengths.shape[0], chunks, k...  32.5 us
    pallas_call x1, Pallas kernels, to_heads(): pl.pallas_call(functools.partial(to_heads_kernel, n), in_specs=[vmem] + [...  30.5 us
    pallas_call x1, Pallas kernels, share(): pl.pallas_call(functools.partial(share_kernel, n), in_specs=[vmem] * 7, o...  22.4 us
    pallas_call x1, Pallas kernels, mix(): pl.pallas_call(functools.partial(mix_kernel, lengths.shape[0], chunks, ke...  22.3 us
    pallas_call x1, Pallas kernels, exchange(): pl.pallas_call(functools.partial(exchange_kernel, n), in_specs=[vmem], ou...  19.1 us
    pallas_call x1, Pallas kernels, feed(): pl.pallas_call(feed_kernel, grid=(steps,), in_specs=[fixed(*blocks.shape)...  16.2 us
    unnamed x47, local copies, waits for them, and re-layouts  8.64 us
  transfers between devices with their start and end apart: 3, of which 3 were waited for; matrix products, arithmetic and copies ran while one was open for 0% of the time, Pallas kernels for 13%

profile of v3, /device:TPU:0, one launch (start us, length us, event | category | flops | bytes accessed | tf_op | source)
XLA Modules:
  0.0 256.6 jit_solution(12663553519420875379)
XLA Ops:
  0.7 0.7 copy-done.5
  1.3 30.5 %to_heads.1 = (bf16[32,2,96,128]{3,2,1,0:T(8,128)(2,1)S(1)}, bf16[32,48,128]{2,1,0:T(8,128)(2,1)S(1)}, bf16[2,192,512]{2,1,0:T(8,128)(2,1)S(1)}) custom-call(f32[1,1024]{1,0:T(1,128)S(1)} %bitcast.26, f32[192,1024]{1,0:T(8,128)} %frames_in.3, bf16[1024,1024]{1,0:T(8,128)(2,1)} %wq_in.3, bf16[1024,1024]{1,0:T(8,128)(2,1)} %wk_in.3, bf16[1024,1024]{1,0:T(8,128)(2,1)} %wv_in.3), custom_call_target="tpu_custom_call" | custom-call | tf_op jit(solution)/shard_map/to_heads/pallas_call | solution.py:863
  31.9 0.7 copy-done.4
  32.7 22.3 %mix.1 = (f32[64,3072]{1,0:T(8,128)S(1)}, f32[1,3072]{1,0:T(1,128)S(1)}, bf16[32,48,128]{2,1,0:T(8,128)(2,1)S(1)}) custom-call(s32[12]{0:T(128)S(1)} %copy-done.14, s32[1]{0:T(128)} %bitcast.core_ref, bf16[6144,128]{1,0:T(8,128)(2,1)S(1)} %bitcast.31, bf16[32,48,128]{2,1,0:T(8,128)(2,1)S(1)} %get-tuple-element.48.qp_ref, s32[1,3072]{1,0:T(1,128)S(1)} %copy-done.15), custom_call_target="tpu_custom_call" | custom-call | flops 24999999488 | bytes 8388608 | tf_op jit(solution)/shard_map/mix/pallas_call | solution.py:465
  55.0 19.1 %exchange.1.blocks_ref = bf16[32,48,128]{2,1,0:T(8,128)(2,1)S(1)} custom-call(bf16[32,48,128]{2,1,0:T(8,128)(2,1)S(1)} %get-tuple-element.49.x_in), custom_call_target="tpu_custom_call" | custom-call | tf_op jit(solution)/shard_map/exchange/pallas_call | solution.py:915
  74.3 16.2 %feed.1 = (f32[192,1024]{1,0:T(8,128)}, f32[192,1024]{1,0:T(8,128)S(1)}, bf16[32,48,128]{2,1,0:T(8,128)(2,1)S(1)}, bf16[2,192,2048]{2,1,0:T(8,128)(2,1)S(1)}, bf...) custom-call(bf16[32,48,128]{2,1,0:T(8,128)(2,1)S(1)} %exchange.1.blo, ...), custom_call_target="tpu_custom_call" | custom-call | tf_op jit(solution)/shard_map/feed/pallas_call | solution.py:677
  90.5 22.4 %share.1 = (bf16[32,48,128]{2,1,0:T(8,128)(2,1)S(1)}, bf16[8,96,1024]{2,1,0:T(8,128)(2,1)}, bf16[8,96,1024]{2,1,0:T(8,128)(2,1)}, bf16[8,96,1024]{2,1,0:T(8,128)...) custom-call(bf16[32,48,128]{2,1,0:T(8,128)(2,1)S(1)} %get-tuple-element.51.blocks_in, ...), custom_call_target="tpu_custom_call" | custom-call | tf_op jit(solution)/shard_map/share/pallas_call | solution.py:1072
  113.0 0.6 collective-permute-start
  113.6 0.6 collective-permute-start.1
  114.2 0.7 collective-permute-start.2
  114.9 32.5 %mix_back.1 = (f32[6144,128]{1,0:T(8,128)S(1)}, bf16[32,48,128]{2,1,0:T(8,128)(2,1)S(1)}) custom-call(s32[12]{0:T(128)S(1)} %copy-done.14, s32[1]{0:T(128)} %bitcast.core_ref, bf16[6144,128]{1,0:T(8,128)(2,1)S(1)} %bitcast.32, bf16[32,48,128]{2,1,0:T(8,128)(2,1)S(1)} %get-tuple-element.48.qp_ref, bf16[32,48,128]{2,1,0:T(8,128)(2,1)S(1)} %get-tuple-element.58.dp_ref, ...), custom_call_target="tpu_custom_call" | custom-call | flops 40000000000 | bytes 8388608 | tf_op jit(solution)/shard_map/mix_back/pallas_call | solution.py:564
  147.4 2.6 %collective-permute-done = bf16[8,96,1024]{2,1,0:T(8,128)(2,1)} collective-permute-done((bf16[8,96,1024]{2,1,0:T(8,128)(2,1)}, bf16[8,96,1024]{2,1,0:T(8,128)(2,1)}, u32[]{:S(2)}, u32[]{:S(2)}) %collective-permute-start) | collective-permute-done | bytes 1572896 | tf_op jit(solution)/shard_map/ppermute | solution.py:935
  150.6 0.7 copy-done.6
  151.3 0.7 copy-done.9
  152.0 0.7 copy-done.11
  152.7 97.8 %finish.1 = (f32[192,1024]{1,0:T(8,128)S(1)}, f32[32,1024]{1,0:T(8,128)S(1)}, f32[32,1024]{1,0:T(8,128)S(1)}, f32[32,1024]{1,0:T(8,128)S(1)}, f32[32,1024]{1,0:T...) custom-call(f32[32,2,96,128]{3,2,1,0:T(8,128)S(1)} %bitcast.25, ...), custom_call_target="tpu_custom_call" | custom-call | tf_op jit(solution)/shard_map/finish/pallas_call | solution.py:1323
  251.0 0.5 slice_bitcast_fusion
  251.6 0.9 copy.33
  252.4 0.7 copy.34
  253.1 0.7 copy.35
  253.7 0.7 copy.36
  254.4 0.7 copy.37
  255.1 0.8 copy.38
  255.9 0.8 copy.39
  (41 shorter events, 1.3 us)
Async XLA Ops:
  0.6 0.7 copy-start.5
  1.3 31.3 %copy-start.14 = (s32[12]{0:T(128)S(1)}, s32[12]{0:T(128)}, u32[]{:S(2)}) copy-start(s32[12]{0:T(128)} %len_ref.3) | copy-start | bytes 148
  1.3 31.3 %copy-start.15 = (s32[1,3072]{1,0:T(1,128)S(1)}, s32[1,3072]{1,0:T(1,128)}, u32[]{:S(2)}) copy-start(s32[1,3072]{1,0:T(1,128)} %constant.26.clone.qpos_ref) | copy-start | bytes 36868
  31.9 0.7 copy-start.4
  32.6 41.6 %slice-start = ((s8[8388608]{0:T(1024)(128)(4,1)}), s8[4194304]{0:T(1024)(128)(4,1)S(1)}, s32[]{:S(2)}) async-start(s8[8388608]{0:T(1024)(128)(4,1)} %bitcast.21), calls=%async_computation | async-start | bytes 8388608
  32.6 41.6 %slice-start.2 = ((s8[8388608]{0:T(1024)(128)(4,1)}), s8[4194304]{0:T(1024)(128)(4,1)S(1)}, s32[]{:S(2)}) async-start(s8[8388608]{0:T(1024)(128)(4,1)} %bitcast.23), calls=%async_computation.2 | async-start | bytes 8388608
  32.6 41.6 %slice-start.1 = ((s8[8388608]{0:T(1024)(128)(4,1)}), s8[4194304]{0:T(1024)(128)(4,1)S(1)}, s32[]{:S(2)}) async-start(s8[8388608]{0:T(1024)(128)(4,1)} %bitcast.21), calls=%async_computation.1 | async-start | bytes 8388608
  32.6 41.6 %slice-start.3 = ((s8[8388608]{0:T(1024)(128)(4,1)}), s8[4194304]{0:T(1024)(128)(4,1)S(1)}, s32[]{:S(2)}) async-start(s8[8388608]{0:T(1024)(128)(4,1)} %bitcast.23), calls=%async_computation.3 | async-start | bytes 8388608
  32.6 41.6 %copy-start = (f32[192,1024]{1,0:T(8,128)S(1)}, f32[192,1024]{1,0:T(8,128)}, u32[]{:S(2)}) copy-start(f32[192,1024]{1,0:T(8,128)} %frames_in.3) | copy-start | bytes 2359300
  32.7 41.6 %copy-start.1 = (bf16[1024,1024]{1,0:T(8,128)(2,1)S(1)}, bf16[1024,1024]{1,0:T(8,128)(2,1)}, u32[]{:S(2)}) copy-start(bf16[1024,1024]{1,0:T(8,128)(2,1)} %w_out_ref.1) | copy-start | bytes 6291460
  32.7 41.6 %copy-start.2 = (f32[192,1024]{1,0:T(8,128)S(1)}, f32[192,1024]{1,0:T(8,128)}, u32[]{:S(2)}) copy-start(f32[192,1024]{1,0:T(8,128)} %cot_ref.1) | copy-start | bytes 2359300
  32.7 41.6 %copy-start.7 = (f32[4096]{0:T(1024)S(1)}, f32[4096]{0:T(1024)}, u32[]{:S(2)}) copy-start(f32[4096]{0:T(1024)} %param.23) | copy-start | bytes 49156
  32.7 41.6 %copy-start.12 = (f32[1024]{0:T(1024)S(1)}, f32[1024]{0:T(1024)}, u32[]{:S(2)}) copy-start(f32[1024]{0:T(1024)} %param.21) | copy-start | bytes 12292
  32.7 41.6 %copy-start.13 = (f32[1024]{0:T(1024)S(1)}, f32[1024]{0:T(1024)}, u32[]{:S(2)}) copy-start(f32[1024]{0:T(1024)} %param.25) | copy-start | bytes 12292
  90.5 22.4 %copy-start.3 = (f32[192,1024]{1,0:T(8,128)}, f32[192,1024]{1,0:T(8,128)S(1)}, u32[]{:S(2)}) copy-start(f32[192,1024]{1,0:T(8,128)S(1)} %get-tuple-element.67.grad_mid_in) | copy-start | bytes 2359300
  90.5 22.4 %copy-start.8 = (f32[1,1024]{1,0:T(1,128)}, f32[1,1024]{1,0:T(1,128)S(1)}, u32[]{:S(2)}) copy-start(f32[1,1024]{1,0:T(1,128)S(1)} %get-tuple-element.63.gain2_grad) | copy-start | bytes 12292
  90.5 22.4 %copy-start.10 = (f32[1,1024]{1,0:T(1,128)}, f32[1,1024]{1,0:T(1,128)S(1)}, u32[]{:S(2)}) copy-start(f32[1,1024]{1,0:T(1,128)S(1)} %get-tuple-element.65.b_down_grad) | copy-start | bytes 12292
  113.0 37.0 %collective-permute-start = (bf16[8,96,1024]{2,1,0:T(8,128)(2,1)}, bf16[8,96,1024]{2,1,0:T(8,128)(2,1)}, u32[]{:S(2)}, u32[]{:S(2)}) collective-permute-start(bf16[8,96,1024]{2,1,0:T(8,128)(2,1)} %get-tuple-element.69), channel_id=1, source_target_pairs={{0,1},{1,0},{2,3},{3,2},{4,5},{5,4},{6,7},{7,6},{8,9},{9,8},{10,11... | collective-permute-start | bytes 4718600 | tf_op jit(solution)/shard_map/ppermute | solution.py:935
  113.6 36.7 %collective-permute-start.1 = (bf16[8,96,1024]{2,1,0:T(8,128)(2,1)}, bf16[8,96,1024]{2,1,0:T(8,128)(2,1)}, u32[]{:S(2)}, u32[]{:S(2)}) collective-permute-start(bf16[8,96,1024]{2,1,0:T(8,128)(2,1)} %get-tuple-element.71), channel_id=1, source_target_pairs={{0,4},{2,6},{4,0},{6,2},{8,12},{10,14},{12,8},{14,10},{16,20},{18,... | collective-permute-start | bytes 4718600 | tf_op jit(solution)/shard_map/ppermute | solution.py:936
  114.2 36.4 %collective-permute-start.2 = (bf16[8,96,1024]{2,1,0:T(8,128)(2,1)}, bf16[8,96,1024]{2,1,0:T(8,128)(2,1)}, u32[]{:S(2)}, u32[]{:S(2)}) collective-permute-start(bf16[8,96,1024]{2,1,0:T(8,128)(2,1)} %get-tuple-element.73), channel_id=1, source_target_pairs={{0,8},{2,10},{4,12},{6,14},{8,0},{10,2},{12,4},{14,6},{16,24},{18,... | collective-permute-start | bytes 4718600 | tf_op jit(solution)/shard_map/ppermute | solution.py:936
  150.6 0.7 copy-start.6
  151.3 0.7 copy-start.9
  152.0 0.7 copy-start.11

commit v4 on v3

--- a/solution.py
+++ b/solution.py
@@ -490,7 +490,7 @@
             jax.ShapeDtypeStruct((1, n_src * half), F32),
             jax.ShapeDtypeStruct((n_src, quarter, 128), BF16),
         ],
-        compiler_params=pltpu.CompilerParams(vmem_limit_bytes=32 << 20),
+        compiler_params=pltpu.CompilerParams(vmem_limit_bytes=22 << 20),
         cost_estimate=pl.CostEstimate(flops=25_000_000_000, bytes_accessed=8 << 20, transcendentals=0),
         name="mix",
     )(lengths, core, kv, qp, qpos)
@@ -585,7 +585,7 @@
             jax.ShapeDtypeStruct((total, 128), F32),
             jax.ShapeDtypeStruct((n_src, quarter, 128), BF16),
         ],
-        compiler_params=pltpu.CompilerParams(vmem_limit_bytes=32 << 20),
+        compiler_params=pltpu.CompilerParams(vmem_limit_bytes=22 << 20),
         cost_estimate=pl.CostEstimate(flops=40_000_000_000, bytes_accessed=8 << 20, transcendentals=0),
         name="mix_back",
     )(lengths, core, kv, qp, dp, qpos, out_t, lse)
@@ -775,8 +775,8 @@
 
 
 def to_heads_kernel(
-    n, gain, frames_in, wq_in, wk_in, wv_in, kv_out, q_out, halves,
-    frames, act, wq, wk, wv, kv_own, q_own, send, recv, local, pair,
+    n, gain_in, frames_in, wq_in, wk_in, wv_in, kv_out, q_out, halves_out,
+    gain, frames, act, halves, wq, wk, wv, kv_own, q_own, send, recv, local, pair,
 ):
     me = own_index()
     head, core = head_of(me)
@@ -784,18 +784,22 @@
     half = rows // 2
     weights = [
         pltpu.make_async_copy(src, dst, local.at[k])
-        for k, (src, dst) in enumerate(((frames_in, frames), (wq_in, wq), (wk_in, wk), (wv_in, wv)))
+        for k, (src, dst) in enumerate(
+            ((gain_in, gain), (frames_in, frames), (wq_in, wq), (wk_in, wk), (wv_in, wv), (halves, halves_out))
+        )
     ]
-    for copy in weights:
+    for copy in weights[:5]:
         copy.start()
     greet_all(me, n)
     weights[0].wait()
+    weights[1].wait()
     x = frames[...]
     r = lax.rsqrt(jnp.mean(x * x, axis=-1, keepdims=True) + EPSILON)
     normed = x * r * gain[...]
     act[...] = normed.astype(BF16)
     store_halves(halves, normed)
-    for copy in weights[1:]:
+    weights[5].start()
+    for copy in weights[2:5]:
         copy.wait()
 
     def copies(other, src):
@@ -844,15 +848,25 @@
     kv_out[me, core] = kv_own[head, core]
     q_out[me] = q_own[head, core]
 
-    @pl.loop(1, n)
-    def _(i):
-        other = lax.rem(me + i, n)
-        for copy in copies(other, other):
-            copy.wait()
-
-    swap = remote(kv_out.at[:, core], kv_out.at[:, core], pair.at[0], pair.at[1], sibling_of(core))
-    swap.start()
-    swap.wait()
+    plane = n // groups
+    swaps = []
+    for t in range(groups):
+        first = pl.multiple_of(lax.rem(lax.div(me, plane) + groups - 1 - t, groups) * plane, plane)
+
+        @pl.loop(0, plane)
+        def _(j):
+            @pl.when(first + j != me)
+            def _():
+                for copy in copies(first + j, first + j):
+                    copy.wait()
+
+        at = pl.ds(first, plane)
+        swap = remote(kv_out.at[at, core], kv_out.at[at, core], pair.at[0, t], pair.at[1, t], sibling_of(core))
+        swap.start()
+        swaps.append(swap)
+    weights[5].wait()
+    for swap in swaps:
+        swap.wait()
 
 
 def to_heads(frames, gain, w_query, w_key, w_value, n):
@@ -862,16 +876,18 @@
     hbm = pl.BlockSpec(memory_space=pltpu.HBM)
     return pl.pallas_call(
         functools.partial(to_heads_kernel, n),
-        in_specs=[vmem] + [hbm] * 4,
-        out_specs=[vmem] * 3,
+        in_specs=[hbm] * 5,
+        out_specs=[vmem, vmem, hbm],
         out_shape=[
             jax.ShapeDtypeStruct((n, 2, half, 128), BF16),
             jax.ShapeDtypeStruct((n, half // 2, 128), BF16),
-            jax.ShapeDtypeStruct((2, rows, width // 2), BF16),
+            pltpu.HBM((2, rows, width // 2), BF16),
         ],
         scratch_shapes=[
+            pltpu.VMEM((1, width), F32),
             pltpu.VMEM((rows, width), F32),
             pltpu.VMEM((rows, width), BF16),
+            pltpu.VMEM((2, rows, width // 2), BF16),
             pltpu.VMEM((width, width), BF16),
             pltpu.VMEM((width, width), BF16),
             pltpu.VMEM((width, width), BF16),
@@ -879,14 +895,14 @@
             pltpu.VMEM((width // 64, 2, half // 2, 128), BF16),
             pltpu.SemaphoreType.DMA((2, n)),
             pltpu.SemaphoreType.DMA((2, n)),
-            pltpu.SemaphoreType.DMA((4,)),
-            pltpu.SemaphoreType.DMA((2,)),
+            pltpu.SemaphoreType.DMA((6,)),
+            pltpu.SemaphoreType.DMA((2, 4)),
         ],
         compiler_params=pltpu.CompilerParams(
             collective_id=0, has_side_effects=True, vmem_limit_bytes=16 << 20
         ),
         name="to_heads",
-    )(gain.reshape(1, width), *in_hbm(frames, w_query, w_key, w_value))
+    )(*in_hbm(gain.reshape(1, width), frames, w_query, w_key, w_value))
 
 
 def exchange_kernel(n, x_in, x_out, send, recv, local):
@@ -916,7 +932,7 @@
         functools.partial(exchange_kernel, n),
         in_specs=[vmem],
         out_specs=vmem,
-        out_shape=jax.ShapeDtypeStruct(x.shape, x.dtype),
+        out_shape=pltpu.VMEM(x.shape, x.dtype),
         scratch_shapes=[
             pltpu.SemaphoreType.DMA((n,)),
             pltpu.SemaphoreType.DMA((n,)),
@@ -924,7 +940,7 @@
         ],
         compiler_params=pltpu.CompilerParams(collective_id=collective_id, has_side_effects=True, vmem_limit_bytes=8 << 20),
         name="exchange",
-    )(x)
+    )(*in_vmem(x))
 
 
 BITS = {"core": 1, "y": 2, "z0": 4, "z1": 8}
@@ -1073,7 +1089,7 @@
         functools.partial(share_kernel, n),
         in_specs=[vmem] * 7,
         out_specs=[vmem] + [hbm] * 6,
-        out_shape=[shape(blocks.shape, BF16)] + [pltpu.HBM((8, 96, width), BF16)] * 6,
+        out_shape=[pltpu.VMEM(blocks.shape, BF16)] + [pltpu.HBM((8, 96, width), BF16)] * 6,
         scratch_shapes=[
             *[pltpu.VMEM((8, 96, width), BF16)] * 6,
             pltpu.VMEM((2 * rows, hidden.shape[2]), BF16),
@@ -1137,14 +1153,14 @@
 
 
 def finish_kernel(
-    n, dkv_in, dq_in, gain, gain2_grad, b_up_grad, b_down_grad, act1, frames_in, grad_mid_in, wq_in, wk_in, wv_in,
-    keep_a, got_a, keep_b, got_b, keep_c, got_c,
+    n, dkv_in, dq_in, gain2_grad, b_up_grad, b_down_grad,
+    gain_in, act1, frames_in, grad_mid_in, wq_in, wk_in, wv_in, keep_a, keep_b, keep_c, got_a, got_b, got_c,
     frames_out, q_out, k_out, v_out, o_out, up_out, down_out, small_out,
-    theirs, total, dkv_all, dq_all, frames, grad_mid, wq, wk, wv, small_in, new_a, new_b, new_c,
+    theirs, total, dkv_all, dq_all, gain, frames, grad_mid, wq, wk, wv, small_in, new_a, new_b, new_c,
     act1_2, qkv2, sum_a, sum_b, sum_c, sum_q, sum_k, sum_v,
     a2, a3, a4, b2, b3, b4, c2, c3, c4,
     q1, q2, q3, q4, k1, k2, k3, k4, v1, v2, v3, v4, small_all,
-    send, recv, dq_send, dq_recv, dkv_send, dkv_recv, small_send, small_recv, pair_send, pair_recv, local,
+    early_send, early_recv, send, recv, dq_send, dq_recv, dkv_send, dkv_recv, small_send, small_recv, pair_send, pair_recv, local,
 ):
     me = own_index()
     head, core = head_of(me)
@@ -1157,7 +1173,7 @@
         for k, (src, dst) in enumerate(
             (
                 (keep_a, sum_a), (got_a, new_a), (keep_b, sum_b), (got_b, new_b), (keep_c, sum_c), (got_c, new_c),
-                (wq_in, wq), (wk_in, wk), (wv_in, wv), (frames_in, frames), (grad_mid_in, grad_mid),
+                (wq_in, wq), (wk_in, wk), (wv_in, wv), (gain_in, gain), (frames_in, frames), (grad_mid_in, grad_mid),
             )
         )
     ]
@@ -1198,40 +1214,64 @@
     dkv_all[me] = add(me)
     dq_all[me] = dq_in[me]
     act1_copy.start()
-    dims = [("z1", "z0", "y"), ("z1", "z0", "x"), ("z1", "y", "x")] + [("z1", "z0", "y", "x")] * 3
-    orders = [
-        ("y", "z0", "z1"), ("z0", "x", "z1"), ("x", "y", "z1"),
-        ("x", "y", "z0", "z1"), ("y", "z0", "x", "z1"), ("z0", "x", "y", "z1"),
-    ]
-    landings = [(a2, a3, a4), (b2, b3, b4), (c2, c3, c4), (q1, q2, q3, q4), (k1, k2, k3, k4), (v1, v2, v3, v4)]
-    parts = [
-        Part(whole, names, order, landing, send.at[k], recv.at[k])
-        for k, (whole, names, order, landing) in enumerate(zip(sums, dims, orders, landings))
-    ]
-    for k in range(3):
-        whole, new = sums[k], news[k]
-        fetches[2 * k].wait()
-        fetches[2 * k + 1].wait()
-
-        @pl.loop(0, 8)
-        def _(k):
-            at = (lax.div(k, 4), lax.rem(lax.div(k, 2), 2), lax.rem(k, 2))
-            whole[at] = (whole[at].astype(F32) + new[at].astype(F32)).astype(BF16)
-
-        parts[k].start()
-
-    act1_own = pltpu.make_async_copy(act1.at[core], act1_2.at[pl.ds(0, rows)], local.at[11])
+    order = ("x", "y", "z0", "z1"), ("y", "z0", "x", "z1"), ("z0", "x", "y", "z1")
+    landings = (q1, q2, q3, q4), (k1, k2, k3, k4), (v1, v2, v3, v4)
+    late = [Part(sums[3 + k], ("z1", "z0", "y", "x"), order[k], landings[k], send.at[k], recv.at[k]) for k in range(3)]
+    dims = ("z1", "z0", "y"), ("z1", "z0", "x"), ("z1", "y", "x")
+    order = ("y", "z0", "z1"), ("z0", "x", "z1"), ("x", "y", "z1")
+    landings = (a2, a3, a4), (b2, b3, b4), (c2, c3, c4)
+    waves = []
+    for u in range(3):
+        band = slice(32 * u, 32 * u + 32)
+        wave = []
+        for k in range(3):
+            wave.append(
+                Part(
+                    sums[k].at[:, :, :, band],
+                    dims[k],
+                    order[k],
+                    [ref.at[(slice(None),) * lead + (band,)] for lead, ref in zip((2, 1, 0), landings[k])],
+                    early_send.at[u, k],
+                    early_recv.at[u, k],
+                )
+            )
+        waves.append(wave)
+
+    for u, wave in enumerate(waves):
+        for k, part in enumerate(wave):
+            whole, new = sums[k], news[k]
+            if u == 0:
+                fetches[2 * k].wait()
+                fetches[2 * k + 1].wait()
+
+            @pl.loop(0, 8)
+            def _(j):
+                at = (lax.div(j, 4), lax.rem(lax.div(j, 2), 2), lax.rem(j, 2), slice(32 * u, 32 * u + 32))
+                whole[at] = (whole[at].astype(F32) + new[at].astype(F32)).astype(BF16)
+
+            part.start()
+
+    def advance(parts):
+        for part in parts:
+            part.finish()
+            part.start()
+
+    act1_own = pltpu.make_async_copy(act1.at[core], act1_2.at[pl.ds(0, rows)], local.at[12])
     act1_own.start()
 
     @pl.loop(1, n)
     def _(i):
-        src = lax.rem(me + i, n)
-        dq_copy(i, src).wait()
-        dkv_copy(i, src).wait()
-
-    for part in parts[:3]:
-        part.finish()
-        part.start()
+        dq_copy(i, lax.rem(me + i, n)).wait()
+
+    advance(waves[0])
+    advance(waves[1])
+
+    @pl.loop(1, n)
+    def _(i):
+        dkv_copy(i, lax.rem(me + i, n)).wait()
+
+    advance(waves[0])
+    advance(waves[2])
     low_q, low_h = low_lanes((quarter, 128)), low_lanes((2 * quarter, 128))
     for zy in range(8):
         for s in range(2):
@@ -1248,6 +1288,7 @@
             qkv2[first : first + 2 * quarter, at] = pair_high(a, b, low_h).astype(BF16)
     pair = remote(qkv2.at[pl.ds(0, rows)], qkv2.at[pl.ds(rows, rows)], pair_send.at[2], pair_recv.at[2], sibling)
     pair.start()
+    advance(waves[1])
 
     for copy in fetches[6:]:
         copy.wait()
@@ -1261,10 +1302,9 @@
         value = tn_dot(act1_2[...], qkv2[:, k * width : (k + 1) * width]).astype(BF16)
         for j in range(16):
             sums[3 + k][j // 8, j // 4 % 2, j // 2 % 2, j % 2] = value[j * 32 : (j + 1) * 32]
-        parts[3 + k].start()
-    for part in parts[:3]:
-        part.finish()
-        part.start()
+        late[k].start()
+
+    advance(waves[2])
 
     x = frames[...]
     r = lax.rsqrt(jnp.mean(x * x, axis=-1, keepdims=True) + EPSILON)
@@ -1286,31 +1326,27 @@
     frames_out[...] = grad_mid[...] + r * (g - norm * jnp.mean(g * norm, axis=-1, keepdims=True))
     small_all[me] = small_in[me]
 
-    for part in parts[3:] * 3:
-        part.finish()
-        part.start()
+    advance(late * 3)
 
     @pl.loop(1, n)
     def _(i):
         small_copy(i, lax.rem(me + i, n)).wait()
 
     small_out[...] = jnp.sum(small_all[...], axis=0)
-    down_out[:96] = parts[0].last()
-    value = parts[1].last()
-    for slab in range(3):
-        up_out[:, slab * 1024 : (slab + 1) * 1024] = value[slab * 32 : (slab + 1) * 32]
-    value = parts[2].last()
-    down_out[96:] = value[:32]
-    up_out[:, 3072:] = value[32:64]
-    o_out[...] = value[64:]
-    q_out[...] = parts[3].last()
-    k_out[...] = parts[4].last()
-    v_out[...] = parts[5].last()
+    for u, wave in enumerate(waves):
+        down_out[32 * u : 32 * u + 32] = wave[0].last()
+        up_out[:, 1024 * u : 1024 * u + 1024] = wave[1].last()
+    down_out[96:] = waves[0][2].last()
+    up_out[:, 3072:] = waves[1][2].last()
+    o_out[...] = waves[2][2].last()
+    q_out[...] = late[0].last()
+    k_out[...] = late[1].last()
+    v_out[...] = late[2].last()
 
 
 def finish(dkv, dq, act1, frames, grad_mid, gain, gain2_grad, b_up_grad, b_down_grad, weights, keeps, gots, n):
     rows, width = frames.shape
-    parts = [x.reshape(2, 2, 2, *x.shape[1:]) for pair in zip(keeps, gots) for x in pair]
+    keeps, gots = [[x.reshape(2, 2, 2, *x.shape[1:]) for x in xs] for xs in (keeps, gots)]
     half = dkv.shape[2]
     vmem = pl.BlockSpec(memory_space=pltpu.VMEM)
     hbm = pl.BlockSpec(memory_space=pltpu.HBM)
@@ -1322,16 +1358,17 @@
     over_devices = [pltpu.SemaphoreType.DMA((n,))] * 6
     return pl.pallas_call(
         functools.partial(finish_kernel, n),
-        in_specs=[vmem] * 6 + [hbm] * 12,
+        in_specs=[vmem] * 5 + [hbm] * 13,
         out_specs=[vmem] * 8,
-        out_shape=[shape((rows, width), F32)]
-        + [shape(thin, F32)] * 4
-        + [shape((32, 4 * width), F32), shape((128, width), F32), shape((8, 128), F32)],
+        out_shape=[pltpu.VMEM((rows, width), F32)]
+        + [pltpu.VMEM(thin, F32)] * 4
+        + [pltpu.VMEM((32, 4 * width), F32), pltpu.VMEM((128, width), F32), shape((8, 128), F32)],
         scratch_shapes=[
             pltpu.VMEM((n, half, 128), F32),
             pltpu.VMEM((n, half, 128), BF16),
             pltpu.VMEM((n, half, 128), BF16),
             pltpu.VMEM((n, half // 2, 128), BF16),
+            pltpu.VMEM((1, width), F32),
             pltpu.VMEM((rows, width), F32),
             pltpu.VMEM((rows, width), F32),
             pltpu.VMEM((width, width), BF16),
@@ -1343,21 +1380,45 @@
             pltpu.VMEM((2 * rows, 3 * width), BF16),
             *buffers,
             pltpu.VMEM((n, 8, 128), F32),
-            pltpu.SemaphoreType.DMA((6, 4)),
-            pltpu.SemaphoreType.DMA((6, 4)),
+            pltpu.SemaphoreType.DMA((3, 3, 3)),
+            pltpu.SemaphoreType.DMA((3, 3, 3)),
+            pltpu.SemaphoreType.DMA((3, 4)),
+            pltpu.SemaphoreType.DMA((3, 4)),
             *over_devices,
             pltpu.SemaphoreType.DMA((3,)),
             pltpu.SemaphoreType.DMA((3,)),
-            pltpu.SemaphoreType.DMA((12,)),
+            pltpu.SemaphoreType.DMA((13,)),
         ],
         compiler_params=pltpu.CompilerParams(
-            collective_id=4, has_side_effects=True, vmem_limit_bytes=42 << 20
+            collective_id=4, has_side_effects=True, vmem_limit_bytes=40 << 20
         ),
         name="finish",
     )(
-        *in_vmem(dkv, dq), gain.reshape(1, width), gain2_grad, b_up_grad, b_down_grad,
-        *in_hbm(act1, frames, grad_mid, *weights, *parts),
-    )
+        *in_vmem(dkv, dq), gain2_grad, b_up_grad, b_down_grad,
+        *in_hbm(gain.reshape(1, width), act1, frames, grad_mid, *weights, *keeps, *gots),
+    )
+
+
+def emit_kernel(n, *refs):
+    sems = refs[-1]
+    copies = [pltpu.make_async_copy(refs[k], refs[n + k], sems.at[k]) for k in range(n)]
+    for copy in copies:
+        copy.start()
+    for copy in copies:
+        copy.wait()
+
+
+def emit(*arrays):
+    n = len(arrays)
+    return pl.pallas_call(
+        functools.partial(emit_kernel, n),
+        in_specs=[pl.BlockSpec(memory_space=pltpu.VMEM)] * n,
+        out_specs=[pl.BlockSpec(memory_space=pltpu.HBM)] * n,
+        out_shape=[pltpu.HBM(x.shape, x.dtype) for x in arrays],
+        scratch_shapes=[pltpu.SemaphoreType.DMA((n,))],
+        compiler_params=pltpu.CompilerParams(vmem_limit_bytes=8 << 20),
+        name="emit",
+    )(*in_vmem(*arrays))
 
 
 def shards_heads(
@@ -1377,15 +1438,19 @@
         layer_out, grad_middle, grad_blocks, hidden, grad_before, act2, mixed, grad_low, grad_attn,
         norm2_gain_grad, b_up_grad, b_down_grad,
     ) = feed(mixed_blocks, frames, cotangent, w_out, norm2_gain, w_up, b_up, w_down, b_down)
-
     grad_blocks, *parts = share(grad_blocks, hidden, grad_before, act2, mixed, grad_low, grad_attn, n)
     keeps = parts[0::2]
     gots = [flipped(part, axis) for part, axis in zip(parts[1::2], ("x", "y", "z0"))]
-    dkv, dq = mix_back(lengths, core_word, kv_rows, q, grad_blocks, qpos, out_t, lse)
+    dkv, dq = mix_back(lengths, core_word, kv_rows, q, *in_vmem(grad_blocks), qpos, out_t, lse)
 
     frames_grad, w_query_grad, w_key_grad, w_value_grad, w_out_grad, w_up_grad, w_down_grad, small = finish(
         dkv.reshape(n, 2, half, 128), dq, act1, frames, grad_middle, norm1_gain, norm2_gain_grad, b_up_grad,
         b_down_grad, (w_query, w_key, w_value), keeps, gots, n,
+    )
+    (
+        layer_out, frames_grad, w_query_grad, w_key_grad, w_value_grad, w_out_grad, w_up_grad, w_down_grad
+    ) = emit(
+        layer_out, frames_grad, w_query_grad, w_key_grad, w_value_grad, w_out_grad, w_up_grad, w_down_grad
     )
     part = width // n
     turn = lax.rem(own_index(), 128 // part) * part

time: 257 us -> 252 us (0.981)
  local copies, waits for them, and re-layouts: 9.75 us -> 3.43 us
    unnamed x47 -> x34, local copies, waits for them, and re-layouts: 8.64 us -> 2.32 us
    pallas_call x2 -> x3, Pallas kernels: 128 us -> 130 us  [the longest x1 97.8 us: finish(): pl.pallas_call(functools.partial(finish_kernel, n), in_specs=[vmem] * 5 +...]
where the time goes in v4:
time: 252 us
  Pallas kernels  243 us (96%)
  local copies, waits for them, and re-layouts  3.43 us (1%)
  waiting for transfers between devices  3.1 us (1%)
    pallas_call x1, Pallas kernels, finish(): pl.pallas_call(functools.partial(finish_kernel, n), in_specs=[vmem] * 5 +...  97.8 us
    pallas_call x1, Pallas kernels, mix_back(): pl.pallas_call(functools.partial(back_kernel, lengths.shape[0], chunks, k...  32.6 us
    pallas_call x1, Pallas kernels, to_heads(): pl.pallas_call(functools.partial(to_heads_kernel, n), in_specs=[hbm] * 5,...  30.7 us
    pallas_call x1, Pallas kernels, share(): pl.pallas_call(functools.partial(share_kernel, n), in_specs=[vmem] * 7, o...  22.3 us
    pallas_call x1, Pallas kernels, mix(): pl.pallas_call(functools.partial(mix_kernel, lengths.shape[0], chunks, ke...  22.3 us
    pallas_call x1, Pallas kernels, exchange(): pl.pallas_call(functools.partial(exchange_kernel, n), in_specs=[vmem], ou...  18.6 us
    pallas_call x1, Pallas kernels, feed(): pl.pallas_call(feed_kernel, grid=(steps,), in_specs=[fixed(*blocks.shape)...  16.4 us
  transfers between devices with their start and end apart: 3, of which 3 were waited for; matrix products, arithmetic and copies ran while one was open for 0% of the time, Pallas kernels for 13%

profile of v4, /device:TPU:0, one launch (start us, length us, event | category | flops | bytes accessed | tf_op | source)
XLA Modules:
  0.0 252.1 jit_solution(3275837043170784243)
XLA Ops:
  0.7 0.0 copy-start.14
  0.7 30.7 %to_heads.1 = (bf16[32,2,96,128]{3,2,1,0:T(8,128)(2,1)S(1)}, bf16[32,48,128]{2,1,0:T(8,128)(2,1)S(1)}, bf16[2,192,512]{2,1,0:T(8,128)(2,1)}) custom-call(f32[1,1024]{1,0:T(1,128)} %bitcast.32, f32[192,1024]{1,0:T(8,128)} %frames_in.3, bf16[1024,1024]{1,0:T(8,128)(2,1)} %wq_in.3, bf16[1024,1024]{1,0:T(8,128)(2,1)} %wk_in.3, bf16[1024,1024]{1,0:T(8,128)(2,1)} %wv_in.3), custom_call_target="tpu_custom_call" | custom-call | tf_op jit(solution)/shard_map/to_heads/pallas_call | solution.py:877
  31.4 0.0 slice-start
  31.4 0.0 copy-start
  31.4 0.0 copy-start.1
  31.5 22.3 %mix.1 = (f32[64,3072]{1,0:T(8,128)S(1)}, f32[1,3072]{1,0:T(1,128)S(1)}, bf16[32,48,128]{2,1,0:T(8,128)(2,1)S(1)}) custom-call(s32[12]{0:T(128)S(1)} %copy-done.13, s32[1]{0:T(128)} %bitcast.core_ref, bf16[6144,128]{1,0:T(8,128)(2,1)S(1)} %bitcast.27, bf16[32,48,128]{2,1,0:T(8,128)(2,1)S(1)} %get-tuple-element.56.qp_ref, s32[1,3072]{1,0:T(1,128)S(1)} %copy-done.14), custom_call_target="tpu_custom_call" | custom-call | flops 24999999488 | bytes 8388608 | tf_op jit(solution)/shard_map/mix/pallas_call | solution.py:465
  53.8 18.6 %exchange.1.blocks_ref = bf16[32,48,128]{2,1,0:T(8,128)(2,1)S(1)} custom-call(bf16[32,48,128]{2,1,0:T(8,128)(2,1)S(1)} %get-tuple-element.57.x_in), custom_call_target="tpu_custom_call" | custom-call | tf_op jit(solution)/shard_map/exchange/pallas_call | solution.py:931
  72.5 16.4 %feed.1 = (f32[192,1024]{1,0:T(8,128)S(1)}, f32[192,1024]{1,0:T(8,128)S(1)}, bf16[32,48,128]{2,1,0:T(8,128)(2,1)S(1)}, bf16[2,192,2048]{2,1,0:T(8,128)(2,1)S(1)}...) custom-call(bf16[32,48,128]{2,1,0:T(8,128)(2,1)S(1)} %exchange.1.blo, ...), custom_call_target="tpu_custom_call" | custom-call | tf_op jit(solution)/shard_map/feed/pallas_call | solution.py:677
  89.0 0.9 copy-done.3
  89.8 22.3 %share.1 = (bf16[32,48,128]{2,1,0:T(8,128)(2,1)S(1)}, bf16[8,96,1024]{2,1,0:T(8,128)(2,1)}, bf16[8,96,1024]{2,1,0:T(8,128)(2,1)}, bf16[8,96,1024]{2,1,0:T(8,128)...) custom-call(bf16[32,48,128]{2,1,0:T(8,128)(2,1)S(1)} %get-tuple-element.59.blocks_in, ...), custom_call_target="tpu_custom_call" | custom-call | tf_op jit(solution)/shard_map/share/pallas_call | solution.py:1088
  112.2 0.6 collective-permute-start
  112.8 0.6 collective-permute-start.1
  113.4 0.7 collective-permute-start.2
  114.1 32.6 %mix_back.1 = (f32[6144,128]{1,0:T(8,128)S(1)}, bf16[32,48,128]{2,1,0:T(8,128)(2,1)S(1)}) custom-call(s32[12]{0:T(128)S(1)} %copy-done.13, s32[1]{0:T(128)} %bitcast.core_ref, bf16[6144,128]{1,0:T(8,128)(2,1)S(1)} %bitcast.28, bf16[32,48,128]{2,1,0:T(8,128)(2,1)S(1)} %get-tuple-element.56.qp_ref, bf16[32,48,128]{2,1,0:T(8,128)(2,1)S(1)} %get-tuple-element.66.dp_ref, ...), custom_call_target="tpu_custom_call" | custom-call | flops 40000000000 | bytes 8388608 | tf_op jit(solution)/shard_map/mix_back/pallas_call | solution.py:564
  146.7 2.5 collective-permute-done
  149.3 0.2 collective-permute-done.1
  149.5 0.4 collective-permute-done.2
  149.9 0.7 copy-done.8
  150.5 0.7 copy-done.10
  151.2 97.8 %finish.1 = (f32[192,1024]{1,0:T(8,128)S(1)}, f32[32,1024]{1,0:T(8,128)S(1)}, f32[32,1024]{1,0:T(8,128)S(1)}, f32[32,1024]{1,0:T(8,128)S(1)}, f32[32,1024]{1,0:T...) custom-call(f32[32,2,96,128]{3,2,1,0:T(8,128)S(1)} %bitcast.23, ...), custom_call_target="tpu_custom_call" | custom-call | tf_op jit(solution)/shard_map/finish/pallas_call | solution.py:1359
  249.1 0.5 slice_bitcast_fusion.1
  249.6 0.1 constant_dynamic-slice_fusion
  249.7 0.5 slice_bitcast_fusion
  250.2 1.7 emit.1
  (28 shorter events, 0.1 us)
Async XLA Ops:
  0.6 30.7 %copy-start.13 = (s32[12]{0:T(128)S(1)}, s32[12]{0:T(128)}, u32[]{:S(2)}) copy-start(s32[12]{0:T(128)} %len_ref.3) | copy-start | bytes 148
  0.7 30.7 %copy-start.14 = (s32[1,3072]{1,0:T(1,128)S(1)}, s32[1,3072]{1,0:T(1,128)}, u32[]{:S(2)}) copy-start(s32[1,3072]{1,0:T(1,128)} %constant.26.clone.qpos_ref) | copy-start | bytes 36868
  31.4 41.1 %slice-start = ((s8[8388608]{0:T(1024)(128)(4,1)}), s8[4194304]{0:T(1024)(128)(4,1)S(1)}, s32[]{:S(2)}) async-start(s8[8388608]{0:T(1024)(128)(4,1)} %bitcast.21), calls=%async_computation | async-start | bytes 8388608
  31.4 41.1 %slice-start.1 = ((s8[8388608]{0:T(1024)(128)(4,1)}), s8[4194304]{0:T(1024)(128)(4,1)S(1)}, s32[]{:S(2)}) async-start(s8[8388608]{0:T(1024)(128)(4,1)} %bitcast.21), calls=%async_computation.1 | async-start | bytes 8388608
  31.4 41.1 %copy-start = (f32[192,1024]{1,0:T(8,128)S(1)}, f32[192,1024]{1,0:T(8,128)}, u32[]{:S(2)}) copy-start(f32[192,1024]{1,0:T(8,128)} %frames_in.3) | copy-start | bytes 2359300
  31.4 41.1 %copy-start.1 = (bf16[1024,1024]{1,0:T(8,128)(2,1)S(1)}, bf16[1024,1024]{1,0:T(8,128)(2,1)}, u32[]{:S(2)}) copy-start(bf16[1024,1024]{1,0:T(8,128)(2,1)} %w_out_ref.1) | copy-start | bytes 6291460
  31.4 41.1 %copy-start.2 = (f32[192,1024]{1,0:T(8,128)S(1)}, f32[192,1024]{1,0:T(8,128)}, u32[]{:S(2)}) copy-start(f32[192,1024]{1,0:T(8,128)} %cot_ref.1) | copy-start | bytes 2359300
  31.4 41.1 %copy-start.6 = (f32[4096]{0:T(1024)S(1)}, f32[4096]{0:T(1024)}, u32[]{:S(2)}) copy-start(f32[4096]{0:T(1024)} %param.23) | copy-start | bytes 49156
  31.4 41.1 %copy-start.11 = (f32[1024]{0:T(1024)S(1)}, f32[1024]{0:T(1024)}, u32[]{:S(2)}) copy-start(f32[1024]{0:T(1024)} %param.21) | copy-start | bytes 12292
  31.5 41.1 %copy-start.12 = (f32[1024]{0:T(1024)S(1)}, f32[1024]{0:T(1024)}, u32[]{:S(2)}) copy-start(f32[1024]{0:T(1024)} %param.25) | copy-start | bytes 12292
  88.9 0.9 copy-start.3
  89.8 22.4 %copy-start.4 = (f32[192,1024]{1,0:T(8,128)}, f32[192,1024]{1,0:T(8,128)S(1)}, u32[]{:S(2)}) copy-start(f32[192,1024]{1,0:T(8,128)S(1)} %get-tuple-element.58.refs_0_) | copy-start | bytes 2359300
  89.8 22.4 %copy-start.7 = (f32[1,1024]{1,0:T(1,128)}, f32[1,1024]{1,0:T(1,128)S(1)}, u32[]{:S(2)}) copy-start(f32[1,1024]{1,0:T(1,128)S(1)} %get-tuple-element.71.gain2_grad) | copy-start | bytes 12292
  89.8 22.4 %copy-start.9 = (f32[1,1024]{1,0:T(1,128)}, f32[1,1024]{1,0:T(1,128)S(1)}, u32[]{:S(2)}) copy-start(f32[1,1024]{1,0:T(1,128)S(1)} %get-tuple-element.73.b_down_grad) | copy-start | bytes 12292
  112.2 37.0 %collective-permute-start = (bf16[8,96,1024]{2,1,0:T(8,128)(2,1)}, bf16[8,96,1024]{2,1,0:T(8,128)(2,1)}, u32[]{:S(2)}, u32[]{:S(2)}) collective-permute-start(bf16[8,96,1024]{2,1,0:T(8,128)(2,1)} %get-tuple-element.79), channel_id=1, source_target_pairs={{0,1},{1,0},{2,3},{3,2},{4,5},{5,4},{6,7},{7,6},{8,9},{9,8},{10,11... | collective-permute-start | bytes 4718600 | tf_op jit(solution)/shard_map/ppermute | solution.py:951
  112.8 36.7 %collective-permute-start.1 = (bf16[8,96,1024]{2,1,0:T(8,128)(2,1)}, bf16[8,96,1024]{2,1,0:T(8,128)(2,1)}, u32[]{:S(2)}, u32[]{:S(2)}) collective-permute-start(bf16[8,96,1024]{2,1,0:T(8,128)(2,1)} %get-tuple-element.80), channel_id=1, source_target_pairs={{0,4},{2,6},{4,0},{6,2},{8,12},{10,14},{12,8},{14,10},{16,20},{18,... | collective-permute-start | bytes 4718600 | tf_op jit(solution)/shard_map/ppermute | solution.py:952
  113.4 36.4 %collective-permute-start.2 = (bf16[8,96,1024]{2,1,0:T(8,128)(2,1)}, bf16[8,96,1024]{2,1,0:T(8,128)(2,1)}, u32[]{:S(2)}, u32[]{:S(2)}) collective-permute-start(bf16[8,96,1024]{2,1,0:T(8,128)(2,1)} %get-tuple-element.81), channel_id=1, source_target_pairs={{0,8},{2,10},{4,12},{6,14},{8,0},{10,2},{12,4},{14,6},{16,24},{18,... | collective-permute-start | bytes 4718600 | tf_op jit(solution)/shard_map/ppermute | solution.py:952
  149.9 0.7 copy-start.8
  150.5 0.7 copy-start.10
  151.2 99.0 %copy-start.5 = (f32[192,1024]{1,0:T(8,128)S(1)}, f32[192,1024]{1,0:T(8,128)}, u32[]{:S(2)}) copy-start(f32[192,1024]{1,0:T(8,128)} %copy-done.4) | copy-start | bytes 2359300

commit v5 on v4

--- a/solution.py
+++ b/solution.py
@@ -776,7 +776,7 @@
 
 def to_heads_kernel(
     n, gain_in, frames_in, wq_in, wk_in, wv_in, kv_out, q_out, halves_out,
-    gain, frames, act, halves, wq, wk, wv, kv_own, q_own, send, recv, local, pair,
+    gain, frames, act, halves, wq, wk, wv, kv_own, q_own, send, recv, local, fetched, pair,
 ):
     me = own_index()
     head, core = head_of(me)
@@ -785,11 +785,29 @@
     weights = [
         pltpu.make_async_copy(src, dst, local.at[k])
         for k, (src, dst) in enumerate(
-            ((gain_in, gain), (frames_in, frames), (wq_in, wq), (wk_in, wk), (wv_in, wv), (halves, halves_out))
+            ((gain_in, gain), (frames_in, frames), (halves, halves_out))
         )
     ]
-    for copy in weights[:5]:
+    groups = width // 256
+
+    def group_at(i):
+        return lax.rem(lax.div(me, n // groups) + 1 + i, groups)
+
+    def fetch(group):
+        columns = pl.ds(pl.multiple_of(group * 256, 256), 256)
+        return [
+            pltpu.make_async_copy(src.at[:, columns], dst.at[:, columns], fetched.at[k, group])
+            for k, (src, dst) in enumerate(((wq_in, wq), (wk_in, wk), (wv_in, wv)))
+        ]
+
+    for copy in weights[:2]:
         copy.start()
+
+    @pl.loop(0, groups)
+    def _(i):
+        for copy in fetch(group_at(i)):
+            copy.start()
+
     greet_all(me, n)
     weights[0].wait()
     weights[1].wait()
@@ -798,9 +816,7 @@
     normed = x * r * gain[...]
     act[...] = normed.astype(BF16)
     store_halves(halves, normed)
-    weights[5].start()
-    for copy in weights[2:5]:
-        copy.wait()
+    weights[2].start()
 
     def copies(other, src):
         h, c = head_of(other)
@@ -812,11 +828,12 @@
 
     low = low_lanes((rows, 128))
     low_h = low_lanes((half // 2, 128))
-    groups = width // 256
 
     @pl.loop(0, groups)
     def _(i):
-        group = lax.rem(lax.div(me, n // groups) + 1 + i, groups)
+        group = group_at(i)
+        for copy in fetch(group):
+            copy.wait()
         columns = pl.ds(pl.multiple_of(group * 256, 256), 256)
         q = nn_dot(act[...], wq[:, columns]).astype(BF16).astype(F32) * 0.125
         k = nn_dot(act[...], wk[:, columns])
@@ -864,7 +881,7 @@
         swap = remote(kv_out.at[at, core], kv_out.at[at, core], pair.at[0, t], pair.at[1, t], sibling_of(core))
         swap.start()
         swaps.append(swap)
-    weights[5].wait()
+    weights[2].wait()
     for swap in swaps:
         swap.wait()
 
@@ -895,7 +912,8 @@
             pltpu.VMEM((width // 64, 2, half // 2, 128), BF16),
             pltpu.SemaphoreType.DMA((2, n)),
             pltpu.SemaphoreType.DMA((2, n)),
-            pltpu.SemaphoreType.DMA((6,)),
+            pltpu.SemaphoreType.DMA((3,)),
+            pltpu.SemaphoreType.DMA((3, 4)),
             pltpu.SemaphoreType.DMA((2, 4)),
         ],
         compiler_params=pltpu.CompilerParams(
@@ -1214,11 +1232,15 @@
     dkv_all[me] = add(me)
     dq_all[me] = dq_in[me]
     act1_copy.start()
-    order = ("x", "y", "z0", "z1"), ("y", "z0", "x", "z1"), ("z0", "x", "y", "z1")
+    order = ("x", "y", "z0", "z1"), ("y", "x", "z0", "z1"), ("z0", "x", "y", "z1")
     landings = (q1, q2, q3, q4), (k1, k2, k3, k4), (v1, v2, v3, v4)
     late = [Part(sums[3 + k], ("z1", "z0", "y", "x"), order[k], landings[k], send.at[k], recv.at[k]) for k in range(3)]
     dims = ("z1", "z0", "y"), ("z1", "z0", "x"), ("z1", "y", "x")
-    order = ("y", "z0", "z1"), ("z0", "x", "z1"), ("x", "y", "z1")
+    order = (
+        (("y", "z0", "z1"),) * 3,
+        (("x", "z0", "z1"), ("x", "z0", "z1"), ("z0", "x", "z1")),
+        (("y", "x", "z1"), ("x", "y", "z1"), ("x", "y", "z1")),
+    )
     landings = (a2, a3, a4), (b2, b3, b4), (c2, c3, c4)
     waves = []
     for u in range(3):
@@ -1229,7 +1251,7 @@
                 Part(
                     sums[k].at[:, :, :, band],
                     dims[k],
-                    order[k],
+                    order[k][u],
                     [ref.at[(slice(None),) * lead + (band,)] for lead, ref in zip((2, 1, 0), landings[k])],
                     early_send.at[u, k],
                     early_recv.at[u, k],
@@ -1272,6 +1294,12 @@
 
     advance(waves[0])
     advance(waves[2])
+    def pair_with(k):
+        columns = slice(k * width, (k + 1) * width)
+        own, other = qkv2.at[pl.ds(0, rows), columns], qkv2.at[pl.ds(rows, rows), columns]
+        return remote(own, other, pair_send.at[2 + k], pair_recv.at[2 + k], sibling)
+
+    pairs = [pair_with(k) for k in range(3)]
     low_q, low_h = low_lanes((quarter, 128)), low_lanes((2 * quarter, 128))
     for zy in range(8):
         for s in range(2):
@@ -1281,29 +1309,33 @@
             at = slice(zy * 128, (zy + 1) * 128)
             qkv2[first : first + quarter, at] = pair_low(a, b, low_q).astype(BF16)
             qkv2[first + quarter : first + 2 * quarter, at] = pair_high(a, b, low_q).astype(BF16)
+    pairs[0].start()
+    for zy in range(8):
+        for s in range(2):
+            j = (zy * 2 + s) * 2
+            first = 2 * s * quarter
             a, b = dkv_all[j].astype(F32), dkv_all[j + 1].astype(F32)
             at = slice(width + zy * 128, width + (zy + 1) * 128)
             qkv2[first : first + 2 * quarter, at] = pair_low(a, b, low_h).astype(BF16)
             at = slice(2 * width + zy * 128, 2 * width + (zy + 1) * 128)
             qkv2[first : first + 2 * quarter, at] = pair_high(a, b, low_h).astype(BF16)
-    pair = remote(qkv2.at[pl.ds(0, rows)], qkv2.at[pl.ds(rows, rows)], pair_send.at[2], pair_recv.at[2], sibling)
-    pair.start()
+    pairs[1].start()
+    pairs[2].start()
     advance(waves[1])
+    act1_copy.wait()
+    act1_own.wait()
+    for k in range(3):
+        pairs[k].wait()
+        value = tn_dot(act1_2[...], qkv2[:, k * width : (k + 1) * width]).astype(BF16)
+        for j in range(16):
+            sums[3 + k][j // 8, j // 4 % 2, j // 2 % 2, j % 2] = value[j * 32 : (j + 1) * 32]
+        late[k].start()
 
     for copy in fetches[6:]:
         copy.wait()
     g = nt_dot(qkv2[:rows, :width], wq[...])
     g += nt_dot(qkv2[:rows, width : 2 * width], wk[...])
     g += nt_dot(qkv2[:rows, 2 * width :], wv[...])
-    act1_copy.wait()
-    act1_own.wait()
-    pair.wait()
-    for k in range(3):
-        value = tn_dot(act1_2[...], qkv2[:, k * width : (k + 1) * width]).astype(BF16)
-        for j in range(16):
-            sums[3 + k][j // 8, j // 4 % 2, j // 2 % 2, j % 2] = value[j * 32 : (j + 1) * 32]
-        late[k].start()
-
     advance(waves[2])
 
     x = frames[...]
@@ -1385,8 +1417,8 @@
             pltpu.SemaphoreType.DMA((3, 4)),
             pltpu.SemaphoreType.DMA((3, 4)),
             *over_devices,
-            pltpu.SemaphoreType.DMA((3,)),
-            pltpu.SemaphoreType.DMA((3,)),
+            pltpu.SemaphoreType.DMA((5,)),
+            pltpu.SemaphoreType.DMA((5,)),
             pltpu.SemaphoreType.DMA((13,)),
         ],
         compiler_params=pltpu.CompilerParams(

time: 252 us -> 244 us (0.968)
  Pallas kernels: 243 us -> 234 us
    pallas_call x1, Pallas kernels: 97.8 us -> 89.5 us  [finish(): pl.pallas_call(functools.partial(finish_kernel, n), in_specs=[vmem] * 5 +...]
where the time goes in v5:
time: 244 us
  Pallas kernels  234 us (96%)
  local copies, waits for them, and re-layouts  3.43 us (1%)
  waiting for transfers between devices  3.19 us (1%)
    pallas_call x1, Pallas kernels, finish(): pl.pallas_call(functools.partial(finish_kernel, n), in_specs=[vmem] * 5 +...  89.5 us
    pallas_call x1, Pallas kernels, mix_back(): pl.pallas_call(functools.partial(back_kernel, lengths.shape[0], chunks, k...  32.5 us
    pallas_call x1, Pallas kernels, to_heads(): pl.pallas_call(functools.partial(to_heads_kernel, n), in_specs=[hbm] * 5,...  30.8 us
    pallas_call x1, Pallas kernels, share(): pl.pallas_call(functools.partial(share_kernel, n), in_specs=[vmem] * 7, o...  22.4 us
    pallas_call x1, Pallas kernels, mix(): pl.pallas_call(functools.partial(mix_kernel, lengths.shape[0], chunks, ke...  22.2 us
    pallas_call x1, Pallas kernels, exchange(): pl.pallas_call(functools.partial(exchange_kernel, n), in_specs=[vmem], ou...  18.6 us
    pallas_call x1, Pallas kernels, feed(): pl.pallas_call(feed_kernel, grid=(steps,), in_specs=[fixed(*blocks.shape)...  16.4 us
  transfers between devices with their start and end apart: 3, of which 3 were waited for; matrix products, arithmetic and copies ran while one was open for 0% of the time, Pallas kernels for 13%

profile of v5, /device:TPU:0, one launch (start us, length us, event | category | flops | bytes accessed | tf_op | source)
XLA Modules:
  0.0 243.8 jit_solution(418805688644135949)
XLA Ops:
  0.7 0.0 copy-start.14
  0.7 30.8 %to_heads.1 = (bf16[32,2,96,128]{3,2,1,0:T(8,128)(2,1)S(1)}, bf16[32,48,128]{2,1,0:T(8,128)(2,1)S(1)}, bf16[2,192,512]{2,1,0:T(8,128)(2,1)}) custom-call(f32[1,1024]{1,0:T(1,128)} %bitcast.32, f32[192,1024]{1,0:T(8,128)} %frames_in.3, bf16[1024,1024]{1,0:T(8,128)(2,1)} %wq_in.3, bf16[1024,1024]{1,0:T(8,128)(2,1)} %wk_in.3, bf16[1024,1024]{1,0:T(8,128)(2,1)} %wv_in.3), custom_call_target="tpu_custom_call" | custom-call | tf_op jit(solution)/shard_map/to_heads/pallas_call | solution.py:894
  31.5 0.0 slice-start
  31.6 0.0 copy-start.2
  31.6 0.0 copy-start.6
  31.6 22.2 %mix.1 = (f32[64,3072]{1,0:T(8,128)S(1)}, f32[1,3072]{1,0:T(1,128)S(1)}, bf16[32,48,128]{2,1,0:T(8,128)(2,1)S(1)}) custom-call(s32[12]{0:T(128)S(1)} %copy-done.13, s32[1]{0:T(128)} %bitcast.core_ref, bf16[6144,128]{1,0:T(8,128)(2,1)S(1)} %bitcast.27, bf16[32,48,128]{2,1,0:T(8,128)(2,1)S(1)} %get-tuple-element.56.qp_ref, s32[1,3072]{1,0:T(1,128)S(1)} %copy-done.14), custom_call_target="tpu_custom_call" | custom-call | flops 24999999488 | bytes 8388608 | tf_op jit(solution)/shard_map/mix/pallas_call | solution.py:465
  53.8 18.6 %exchange.1.blocks_ref = bf16[32,48,128]{2,1,0:T(8,128)(2,1)S(1)} custom-call(bf16[32,48,128]{2,1,0:T(8,128)(2,1)S(1)} %get-tuple-element.57.x_in), custom_call_target="tpu_custom_call" | custom-call | tf_op jit(solution)/shard_map/exchange/pallas_call | solution.py:949
  72.5 16.4 %feed.1 = (f32[192,1024]{1,0:T(8,128)S(1)}, f32[192,1024]{1,0:T(8,128)S(1)}, bf16[32,48,128]{2,1,0:T(8,128)(2,1)S(1)}, bf16[2,192,2048]{2,1,0:T(8,128)(2,1)S(1)}...) custom-call(bf16[32,48,128]{2,1,0:T(8,128)(2,1)S(1)} %exchange.1.blo, ...), custom_call_target="tpu_custom_call" | custom-call | tf_op jit(solution)/shard_map/feed/pallas_call | solution.py:677
  89.0 0.9 copy-done.3
  89.8 22.4 %share.1 = (bf16[32,48,128]{2,1,0:T(8,128)(2,1)S(1)}, bf16[8,96,1024]{2,1,0:T(8,128)(2,1)}, bf16[8,96,1024]{2,1,0:T(8,128)(2,1)}, bf16[8,96,1024]{2,1,0:T(8,128)...) custom-call(bf16[32,48,128]{2,1,0:T(8,128)(2,1)S(1)} %get-tuple-element.59.blocks_in, ...), custom_call_target="tpu_custom_call" | custom-call | tf_op jit(solution)/shard_map/share/pallas_call | solution.py:1106
  112.2 0.6 collective-permute-start
  112.8 0.6 collective-permute-start.1
  113.5 0.7 collective-permute-start.2
  114.1 32.5 %mix_back.1 = (f32[6144,128]{1,0:T(8,128)S(1)}, bf16[32,48,128]{2,1,0:T(8,128)(2,1)S(1)}) custom-call(s32[12]{0:T(128)S(1)} %copy-done.13, s32[1]{0:T(128)} %bitcast.core_ref, bf16[6144,128]{1,0:T(8,128)(2,1)S(1)} %bitcast.28, bf16[32,48,128]{2,1,0:T(8,128)(2,1)S(1)} %get-tuple-element.56.qp_ref, bf16[32,48,128]{2,1,0:T(8,128)(2,1)S(1)} %get-tuple-element.66.dp_ref, ...), custom_call_target="tpu_custom_call" | custom-call | flops 40000000000 | bytes 8388608 | tf_op jit(solution)/shard_map/mix_back/pallas_call | solution.py:564
  146.7 2.6 %collective-permute-done = bf16[8,96,1024]{2,1,0:T(8,128)(2,1)} collective-permute-done((bf16[8,96,1024]{2,1,0:T(8,128)(2,1)}, bf16[8,96,1024]{2,1,0:T(8,128)(2,1)}, u32[]{:S(2)}, u32[]{:S(2)}) %collective-permute-start) | collective-permute-done | bytes 1572896 | tf_op jit(solution)/shard_map/ppermute | solution.py:969
  149.3 0.2 collective-permute-done.1
  149.5 0.4 collective-permute-done.2
  149.9 0.7 copy-done.8
  150.6 0.7 copy-done.10
  151.2 89.5 %finish.1 = (f32[192,1024]{1,0:T(8,128)S(1)}, f32[32,1024]{1,0:T(8,128)S(1)}, f32[32,1024]{1,0:T(8,128)S(1)}, f32[32,1024]{1,0:T(8,128)S(1)}, f32[32,1024]{1,0:T...) custom-call(f32[32,2,96,128]{3,2,1,0:T(8,128)S(1)} %bitcast.23, ...), custom_call_target="tpu_custom_call" | custom-call | tf_op jit(solution)/shard_map/finish/pallas_call | solution.py:1391
  240.8 0.5 slice_bitcast_fusion.1
  241.3 0.1 constant_dynamic-slice_fusion
  241.4 0.5 slice_bitcast_fusion
  241.9 1.7 emit.1
  (28 shorter events, 0.1 us)
Async XLA Ops:
  0.6 30.9 %copy-start.13 = (s32[12]{0:T(128)S(1)}, s32[12]{0:T(128)}, u32[]{:S(2)}) copy-start(s32[12]{0:T(128)} %len_ref.3) | copy-start | bytes 148
  0.7 30.9 %copy-start.14 = (s32[1,3072]{1,0:T(1,128)S(1)}, s32[1,3072]{1,0:T(1,128)}, u32[]{:S(2)}) copy-start(s32[1,3072]{1,0:T(1,128)} %constant.26.clone.qpos_ref) | copy-start | bytes 36868
  31.5 40.9 %slice-start = ((s8[8388608]{0:T(1024)(128)(4,1)}), s8[4194304]{0:T(1024)(128)(4,1)S(1)}, s32[]{:S(2)}) async-start(s8[8388608]{0:T(1024)(128)(4,1)} %bitcast.21), calls=%async_computation | async-start | bytes 8388608
  31.5 40.9 %slice-start.1 = ((s8[8388608]{0:T(1024)(128)(4,1)}), s8[4194304]{0:T(1024)(128)(4,1)S(1)}, s32[]{:S(2)}) async-start(s8[8388608]{0:T(1024)(128)(4,1)} %bitcast.21), calls=%async_computation.1 | async-start | bytes 8388608
  31.5 40.9 %copy-start = (f32[192,1024]{1,0:T(8,128)S(1)}, f32[192,1024]{1,0:T(8,128)}, u32[]{:S(2)}) copy-start(f32[192,1024]{1,0:T(8,128)} %frames_in.3) | copy-start | bytes 2359300
  31.6 40.9 %copy-start.1 = (bf16[1024,1024]{1,0:T(8,128)(2,1)S(1)}, bf16[1024,1024]{1,0:T(8,128)(2,1)}, u32[]{:S(2)}) copy-start(bf16[1024,1024]{1,0:T(8,128)(2,1)} %w_out_ref.1) | copy-start | bytes 6291460
  31.6 40.9 %copy-start.2 = (f32[192,1024]{1,0:T(8,128)S(1)}, f32[192,1024]{1,0:T(8,128)}, u32[]{:S(2)}) copy-start(f32[192,1024]{1,0:T(8,128)} %cot_ref.1) | copy-start | bytes 2359300
  31.6 40.9 %copy-start.6 = (f32[4096]{0:T(1024)S(1)}, f32[4096]{0:T(1024)}, u32[]{:S(2)}) copy-start(f32[4096]{0:T(1024)} %param.23) | copy-start | bytes 49156
  31.6 40.9 %copy-start.11 = (f32[1024]{0:T(1024)S(1)}, f32[1024]{0:T(1024)}, u32[]{:S(2)}) copy-start(f32[1024]{0:T(1024)} %param.21) | copy-start | bytes 12292
  31.6 40.9 %copy-start.12 = (f32[1024]{0:T(1024)S(1)}, f32[1024]{0:T(1024)}, u32[]{:S(2)}) copy-start(f32[1024]{0:T(1024)} %param.25) | copy-start | bytes 12292
  88.9 0.9 copy-start.3
  89.8 22.4 %copy-start.4 = (f32[192,1024]{1,0:T(8,128)}, f32[192,1024]{1,0:T(8,128)S(1)}, u32[]{:S(2)}) copy-start(f32[192,1024]{1,0:T(8,128)S(1)} %get-tuple-element.58.refs_0_) | copy-start | bytes 2359300
  89.8 22.4 %copy-start.7 = (f32[1,1024]{1,0:T(1,128)}, f32[1,1024]{1,0:T(1,128)S(1)}, u32[]{:S(2)}) copy-start(f32[1,1024]{1,0:T(1,128)S(1)} %get-tuple-element.71.gain2_grad) | copy-start | bytes 12292
  89.8 22.4 %copy-start.9 = (f32[1,1024]{1,0:T(1,128)}, f32[1,1024]{1,0:T(1,128)S(1)}, u32[]{:S(2)}) copy-start(f32[1,1024]{1,0:T(1,128)S(1)} %get-tuple-element.73.b_down_grad) | copy-start | bytes 12292
  112.2 37.0 %collective-permute-start = (bf16[8,96,1024]{2,1,0:T(8,128)(2,1)}, bf16[8,96,1024]{2,1,0:T(8,128)(2,1)}, u32[]{:S(2)}, u32[]{:S(2)}) collective-permute-start(bf16[8,96,1024]{2,1,0:T(8,128)(2,1)} %get-tuple-element.79), channel_id=1, source_target_pairs={{0,1},{1,0},{2,3},{3,2},{4,5},{5,4},{6,7},{7,6},{8,9},{9,8},{10,11... | collective-permute-start | bytes 4718600 | tf_op jit(solution)/shard_map/ppermute | solution.py:969
  112.8 36.7 %collective-permute-start.1 = (bf16[8,96,1024]{2,1,0:T(8,128)(2,1)}, bf16[8,96,1024]{2,1,0:T(8,128)(2,1)}, u32[]{:S(2)}, u32[]{:S(2)}) collective-permute-start(bf16[8,96,1024]{2,1,0:T(8,128)(2,1)} %get-tuple-element.80), channel_id=1, source_target_pairs={{0,4},{2,6},{4,0},{6,2},{8,12},{10,14},{12,8},{14,10},{16,20},{18,... | collective-permute-start | bytes 4718600 | tf_op jit(solution)/shard_map/ppermute | solution.py:970
  113.5 36.4 %collective-permute-start.2 = (bf16[8,96,1024]{2,1,0:T(8,128)(2,1)}, bf16[8,96,1024]{2,1,0:T(8,128)(2,1)}, u32[]{:S(2)}, u32[]{:S(2)}) collective-permute-start(bf16[8,96,1024]{2,1,0:T(8,128)(2,1)} %get-tuple-element.81), channel_id=1, source_target_pairs={{0,8},{2,10},{4,12},{6,14},{8,0},{10,2},{12,4},{14,6},{16,24},{18,... | collective-permute-start | bytes 4718600 | tf_op jit(solution)/shard_map/ppermute | solution.py:970
  149.9 0.7 copy-start.8
  150.6 0.7 copy-start.10
  151.2 90.7 %copy-start.5 = (f32[192,1024]{1,0:T(8,128)S(1)}, f32[192,1024]{1,0:T(8,128)}, u32[]{:S(2)}) copy-start(f32[192,1024]{1,0:T(8,128)} %copy-done.4) | copy-start | bytes 2359300

commit v6 on v5

--- a/solution.py
+++ b/solution.py
@@ -704,7 +704,7 @@
         ],
         out_shape=[
             shape((rows, width), F32),
-            shape((rows, width), F32),
+            pltpu.HBM((rows, width), F32),
             shape(blocks.shape, BF16),
             shape((2, rows, ff // 2), BF16),
             shape((rows, ff), BF16),
@@ -712,9 +712,9 @@
             shape((2, rows, width // 2), BF16),
             shape((rows, width), BF16),
             shape((rows, width), BF16),
-            shape((1, width), F32),
-            shape((1, ff), F32),
-            shape((1, width), F32),
+            pltpu.VMEM((1, width), F32),
+            pltpu.VMEM((1, ff), F32),
+            pltpu.VMEM((1, width), F32),
         ],
         scratch_shapes=[
             pltpu.VMEM((rows, width), F32),
@@ -1171,10 +1171,10 @@
 
 
 def finish_kernel(
-    n, dkv_in, dq_in, gain2_grad, b_up_grad, b_down_grad,
-    gain_in, act1, frames_in, grad_mid_in, wq_in, wk_in, wv_in, keep_a, keep_b, keep_c, got_a, got_b, got_c,
+    n, dkv_in, dq_in, gain2_grad, b_up_grad, b_down_grad, got_a, got_b, got_c,
+    gain_in, act1, frames_in, grad_mid_in, wq_in, wk_in, wv_in, keep_a, keep_b, keep_c,
     frames_out, q_out, k_out, v_out, o_out, up_out, down_out, small_out,
-    theirs, total, dkv_all, dq_all, gain, frames, grad_mid, wq, wk, wv, small_in, new_a, new_b, new_c,
+    theirs, total, dkv_all, dq_all, gain, frames, grad_mid, wq, wk, wv, small_in,
     act1_2, qkv2, sum_a, sum_b, sum_c, sum_q, sum_k, sum_v,
     a2, a3, a4, b2, b3, b4, c2, c3, c4,
     q1, q2, q3, q4, k1, k2, k3, k4, v1, v2, v3, v4, small_all,
@@ -1185,12 +1185,12 @@
     rows, width = frames.shape
     quarter = rows // 4
     sums = [sum_a, sum_b, sum_c, sum_q, sum_k, sum_v]
-    news = [new_a, new_b, new_c]
+    news = [got_a, got_b, got_c]
     fetches = [
         pltpu.make_async_copy(src, dst, local.at[k])
         for k, (src, dst) in enumerate(
             (
-                (keep_a, sum_a), (got_a, new_a), (keep_b, sum_b), (got_b, new_b), (keep_c, sum_c), (got_c, new_c),
+                (keep_a, sum_a), (keep_b, sum_b), (keep_c, sum_c),
                 (wq_in, wq), (wk_in, wk), (wv_in, wv), (gain_in, gain), (frames_in, frames), (grad_mid_in, grad_mid),
             )
         )
@@ -1239,7 +1239,7 @@
     order = (
         (("y", "z0", "z1"),) * 3,
         (("x", "z0", "z1"), ("x", "z0", "z1"), ("z0", "x", "z1")),
-        (("y", "x", "z1"), ("x", "y", "z1"), ("x", "y", "z1")),
+        (("x", "y", "z1"), ("y", "x", "z1"), ("x", "y", "z1")),
     )
     landings = (a2, a3, a4), (b2, b3, b4), (c2, c3, c4)
     waves = []
@@ -1263,8 +1263,7 @@
         for k, part in enumerate(wave):
             whole, new = sums[k], news[k]
             if u == 0:
-                fetches[2 * k].wait()
-                fetches[2 * k + 1].wait()
+                fetches[k].wait()
 
             @pl.loop(0, 8)
             def _(j):
@@ -1278,7 +1277,7 @@
             part.finish()
             part.start()
 
-    act1_own = pltpu.make_async_copy(act1.at[core], act1_2.at[pl.ds(0, rows)], local.at[12])
+    act1_own = pltpu.make_async_copy(act1.at[core], act1_2.at[pl.ds(0, rows)], local.at[9])
     act1_own.start()
 
     @pl.loop(1, n)
@@ -1331,7 +1330,7 @@
             sums[3 + k][j // 8, j // 4 % 2, j // 2 % 2, j % 2] = value[j * 32 : (j + 1) * 32]
         late[k].start()
 
-    for copy in fetches[6:]:
+    for copy in fetches[3:]:
         copy.wait()
     g = nt_dot(qkv2[:rows, :width], wq[...])
     g += nt_dot(qkv2[:rows, width : 2 * width], wk[...])
@@ -1364,7 +1363,9 @@
     def _(i):
         small_copy(i, lax.rem(me + i, n)).wait()
 
-    small_out[...] = jnp.sum(small_all[...], axis=0)
+    part = width // n
+    small_out[...] = pltpu.roll(jnp.sum(small_all[...], axis=0), lax.rem(128 - lax.rem(me, 128 // part) * part, 128), 1)
+    small_out[3:4] = jnp.sum(small_all[:, 3:4], axis=0)
     for u, wave in enumerate(waves):
         down_out[32 * u : 32 * u + 32] = wave[0].last()
         up_out[:, 1024 * u : 1024 * u + 1024] = wave[1].last()
@@ -1390,11 +1391,11 @@
     over_devices = [pltpu.SemaphoreType.DMA((n,))] * 6
     return pl.pallas_call(
         functools.partial(finish_kernel, n),
-        in_specs=[vmem] * 5 + [hbm] * 13,
+        in_specs=[vmem] * 8 + [hbm] * 10,
         out_specs=[vmem] * 8,
         out_shape=[pltpu.VMEM((rows, width), F32)]
         + [pltpu.VMEM(thin, F32)] * 4
-        + [pltpu.VMEM((32, 4 * width), F32), pltpu.VMEM((128, width), F32), shape((8, 128), F32)],
+        + [pltpu.VMEM((32, 4 * width), F32), pltpu.VMEM((128, width), F32), pltpu.VMEM((8, 128), F32)],
         scratch_shapes=[
             pltpu.VMEM((n, half, 128), F32),
             pltpu.VMEM((n, half, 128), BF16),
@@ -1407,7 +1408,6 @@
             pltpu.VMEM((width, width), BF16),
             pltpu.VMEM((width, width), BF16),
             pltpu.VMEM((n, 8, 128), F32),
-            *[pltpu.VMEM((2, 2, 2, *wide), BF16)] * 3,
             pltpu.VMEM((2 * rows, width // 2), BF16),
             pltpu.VMEM((2 * rows, 3 * width), BF16),
             *buffers,
@@ -1419,38 +1419,42 @@
             *over_devices,
             pltpu.SemaphoreType.DMA((5,)),
             pltpu.SemaphoreType.DMA((5,)),
-            pltpu.SemaphoreType.DMA((13,)),
+            pltpu.SemaphoreType.DMA((10,)),
         ],
         compiler_params=pltpu.CompilerParams(
-            collective_id=4, has_side_effects=True, vmem_limit_bytes=40 << 20
+            collective_id=4, has_side_effects=True, vmem_limit_bytes=36 << 20
         ),
         name="finish",
     )(
-        *in_vmem(dkv, dq), gain2_grad, b_up_grad, b_down_grad,
-        *in_hbm(gain.reshape(1, width), act1, frames, grad_mid, *weights, *keeps, *gots),
-    )
-
-
-def emit_kernel(n, *refs):
+        *in_vmem(dkv, dq, gain2_grad, b_up_grad, b_down_grad, *gots),
+        *in_hbm(gain.reshape(1, width), act1, frames, grad_mid, *weights, *keeps),
+    )
+
+
+def emit_kernel(n, small, *refs):
     sems = refs[-1]
     copies = [pltpu.make_async_copy(refs[k], refs[n + k], sems.at[k]) for k in range(n)]
     for copy in copies:
         copy.start()
+    for row, out in enumerate(refs[2 * n : -1]):
+        out[...] = small[row : row + 1, : out.shape[1]]
     for copy in copies:
         copy.wait()
 
 
-def emit(*arrays):
+def emit(small, widths, *arrays):
     n = len(arrays)
+    vmem = pl.BlockSpec(memory_space=pltpu.VMEM)
     return pl.pallas_call(
         functools.partial(emit_kernel, n),
-        in_specs=[pl.BlockSpec(memory_space=pltpu.VMEM)] * n,
-        out_specs=[pl.BlockSpec(memory_space=pltpu.HBM)] * n,
-        out_shape=[pltpu.HBM(x.shape, x.dtype) for x in arrays],
+        in_specs=[vmem] * (n + 1),
+        out_specs=[pl.BlockSpec(memory_space=pltpu.HBM)] * n + [vmem] * len(widths),
+        out_shape=[pltpu.HBM(x.shape, x.dtype) for x in arrays]
+        + [jax.ShapeDtypeStruct((1, width), F32) for width in widths],
         scratch_shapes=[pltpu.SemaphoreType.DMA((n,))],
         compiler_params=pltpu.CompilerParams(vmem_limit_bytes=8 << 20),
         name="emit",
-    )(*in_vmem(*arrays))
+    )(*in_vmem(small, *arrays))
 
 
 def shards_heads(
@@ -1479,27 +1483,26 @@
         dkv.reshape(n, 2, half, 128), dq, act1, frames, grad_middle, norm1_gain, norm2_gain_grad, b_up_grad,
         b_down_grad, (w_query, w_key, w_value), keeps, gots, n,
     )
+    part = width // n
     (
-        layer_out, frames_grad, w_query_grad, w_key_grad, w_value_grad, w_out_grad, w_up_grad, w_down_grad
+        layer_out, frames_grad, w_query_grad, w_key_grad, w_value_grad, w_out_grad, w_up_grad, w_down_grad, *vectors
     ) = emit(
-        layer_out, frames_grad, w_query_grad, w_key_grad, w_value_grad, w_out_grad, w_up_grad, w_down_grad
-    )
-    part = width // n
-    turn = lax.rem(own_index(), 128 // part) * part
-    vectors = lax.dynamic_slice(small, (0, turn), (3, part))
+        small, (part, part, part, b_up.shape[0] // n),
+        layer_out, frames_grad, w_query_grad, w_key_grad, w_value_grad, w_out_grad, w_up_grad, w_down_grad,
+    )
     return (
         layer_out,
         frames_grad,
-        vectors[0],
+        vectors[0].reshape(-1),
         w_query_grad,
         w_key_grad,
         w_value_grad,
         w_out_grad,
-        vectors[1],
+        vectors[1].reshape(-1),
         w_up_grad,
-        small[3],
+        vectors[3].reshape(-1),
         w_down_grad,
-        vectors[2],
+        vectors[2].reshape(-1),
     )
 
 

time: 244 us -> 240 us (0.984)
  local copies, waits for them, and re-layouts: 3.43 us -> 0.07 us
  transfers between devices with their start and end apart: 3 -> 3, of which waited for: 3 -> 3; matrix products, arithmetic and copies ran while one was open for 0% -> 0% of each run, Pallas kernels for 13% -> 14%
where the time goes in v6:
time: 240 us; the launch traced here: 239 us
  Pallas kernels  233 us (97%)
  waiting for transfers between devices  3.18 us (1%)
    pallas_call x1, Pallas kernels, finish(): pl.pallas_call(functools.partial(finish_kernel, n), in_specs=[vmem] * 8 +...  88.3 us
    pallas_call x1, Pallas kernels, mix_back(): pl.pallas_call(functools.partial(back_kernel, lengths.shape[0], chunks, k...  32.5 us
    pallas_call x1, Pallas kernels, to_heads(): pl.pallas_call(functools.partial(to_heads_kernel, n), in_specs=[hbm] * 5,...  30.8 us
    pallas_call x1, Pallas kernels, share(): pl.pallas_call(functools.partial(share_kernel, n), in_specs=[vmem] * 7, o...  22.5 us
    pallas_call x1, Pallas kernels, mix(): pl.pallas_call(functools.partial(mix_kernel, lengths.shape[0], chunks, ke...  22.2 us
    pallas_call x1, Pallas kernels, exchange(): pl.pallas_call(functools.partial(exchange_kernel, n), in_specs=[vmem], ou...  18.6 us
    pallas_call x1, Pallas kernels, feed(): pl.pallas_call(feed_kernel, grid=(steps,), in_specs=[fixed(*blocks.shape)...  16.2 us
  transfers between devices with their start and end apart: 3, of which 3 were waited for; matrix products, arithmetic and copies ran while one was open for 0% of the time, Pallas kernels for 14%

profile of v6, /device:TPU:0, one launch (start us, length us, event | category | flops | bytes accessed | tf_op | source)
XLA Modules:
  0.0 239.4 jit_solution(2631618761449378749)
XLA Ops:
  0.7 0.0 copy-start.7
  0.7 30.8 %to_heads.1 = (bf16[32,2,96,128]{3,2,1,0:T(8,128)(2,1)S(1)}, bf16[32,48,128]{2,1,0:T(8,128)(2,1)S(1)}, bf16[2,192,512]{2,1,0:T(8,128)(2,1)}) custom-call(f32[1,1024]{1,0:T(1,128)} %bitcast.33, f32[192,1024]{1,0:T(8,128)} %frames_in.3, bf16[1024,1024]{1,0:T(8,128)(2,1)} %wq_in.3, bf16[1024,1024]{1,0:T(8,128)(2,1)} %wk_in.3, bf16[1024,1024]{1,0:T(8,128)(2,1)} %wv_in.3), custom_call_target="tpu_custom_call" | custom-call | tf_op jit(solution)/shard_map/to_heads/pallas_call | solution.py:894
  31.5 0.0 slice-start
  31.5 0.0 slice-start.2
  31.6 0.0 slice-start.3
  31.6 0.0 copy-start
  31.6 0.0 copy-start.1
  31.6 0.0 copy-start.2
  31.6 0.0 copy-start.3
  31.6 0.0 copy-start.4
  31.6 0.0 copy-start.5
  31.6 22.2 %mix.1 = (f32[64,3072]{1,0:T(8,128)S(1)}, f32[1,3072]{1,0:T(1,128)S(1)}, bf16[32,48,128]{2,1,0:T(8,128)(2,1)S(1)}) custom-call(s32[12]{0:T(128)S(1)} %copy-done.6, s32[1]{0:T(128)} %bitcast.core_ref, bf16[6144,128]{1,0:T(8,128)(2,1)S(1)} %bitcast.28, bf16[32,48,128]{2,1,0:T(8,128)(2,1)S(1)} %get-tuple-element.60.qp_ref, s32[1,3072]{1,0:T(1,128)S(1)} %copy-done.7), custom_call_target="tpu_custom_call" | custom-call | flops 24999999488 | bytes 8388608 | tf_op jit(solution)/shard_map/mix/pallas_call | solution.py:465
  53.8 18.6 %exchange.1.blocks_ref = bf16[32,48,128]{2,1,0:T(8,128)(2,1)S(1)} custom-call(bf16[32,48,128]{2,1,0:T(8,128)(2,1)S(1)} %get-tuple-element.61.x_in), custom_call_target="tpu_custom_call" | custom-call | tf_op jit(solution)/shard_map/exchange/pallas_call | solution.py:949
  72.6 16.2 %feed.1 = (f32[192,1024]{1,0:T(8,128)S(1)}, f32[192,1024]{1,0:T(8,128)}, bf16[32,48,128]{2,1,0:T(8,128)(2,1)S(1)}, bf16[2,192,2048]{2,1,0:T(8,128)(2,1)S(1)}, bf...) custom-call(bf16[32,48,128]{2,1,0:T(8,128)(2,1)S(1)} %exchange.1.blo, ...), custom_call_target="tpu_custom_call" | custom-call | tf_op jit(solution)/shard_map/feed/pallas_call | solution.py:677
  88.7 22.5 %share.1 = (bf16[32,48,128]{2,1,0:T(8,128)(2,1)S(1)}, bf16[8,96,1024]{2,1,0:T(8,128)(2,1)}, bf16[8,96,1024]{2,1,0:T(8,128)(2,1)}, bf16[8,96,1024]{2,1,0:T(8,128)...) custom-call(bf16[32,48,128]{2,1,0:T(8,128)(2,1)S(1)} %get-tuple-element.62.blocks_in, ...), custom_call_target="tpu_custom_call" | custom-call | tf_op jit(solution)/shard_map/share/pallas_call | solution.py:1106
  111.3 0.6 collective-permute-start
  111.9 0.6 collective-permute-start.1
  112.4 0.6 collective-permute-start.2
  113.0 32.5 %mix_back.1 = (f32[6144,128]{1,0:T(8,128)S(1)}, bf16[32,48,128]{2,1,0:T(8,128)(2,1)S(1)}) custom-call(s32[12]{0:T(128)S(1)} %copy-done.6, s32[1]{0:T(128)} %bitcast.core_ref, bf16[6144,128]{1,0:T(8,128)(2,1)S(1)} %bitcast.29, bf16[32,48,128]{2,1,0:T(8,128)(2,1)S(1)} %get-tuple-element.60.qp_ref, bf16[32,48,128]{2,1,0:T(8,128)(2,1)S(1)} %get-tuple-element.69.dp_ref, ...), custom_call_target="tpu_custom_call" | custom-call | flops 40000000000 | bytes 8388608 | tf_op jit(solution)/shard_map/mix_back/pallas_call | solution.py:564
  145.6 2.7 %collective-permute-done = bf16[8,96,1024]{2,1,0:T(8,128)(2,1)S(1)} collective-permute-done((bf16[8,96,1024]{2,1,0:T(8,128)(2,1)}, bf16[8,96,1024]{2,1,0:T(8,128)(2,1)S(1)}, u32[]{:S(2)}, u32[]{:S(2)}) %collective-permute-start) | collective-permute-done | bytes 1572896 | tf_op jit(solution)/shard_map/ppermute | solution.py:969
  148.2 0.2 collective-permute-done.1
  148.5 0.3 collective-permute-done.2
  148.7 88.3 %finish.1 = (f32[192,1024]{1,0:T(8,128)S(1)}, f32[32,1024]{1,0:T(8,128)S(1)}, f32[32,1024]{1,0:T(8,128)S(1)}, f32[32,1024]{1,0:T(8,128)S(1)}, f32[32,1024]{1,0:T...) custom-call(f32[32,2,96,128]{3,2,1,0:T(8,128)S(1)} %bitcast.21, ...), custom_call_target="tpu_custom_call" | custom-call | tf_op jit(solution)/shard_map/finish/pallas_call | solution.py:1392
  237.0 2.3 emit.1
  (16 shorter events, 0.0 us)
Async XLA Ops:
  0.6 30.9 %copy-start.6 = (s32[12]{0:T(128)S(1)}, s32[12]{0:T(128)}, u32[]{:S(2)}) copy-start(s32[12]{0:T(128)} %len_ref.3) | copy-start | bytes 148
  0.7 30.9 %copy-start.7 = (s32[1,3072]{1,0:T(1,128)S(1)}, s32[1,3072]{1,0:T(1,128)}, u32[]{:S(2)}) copy-start(s32[1,3072]{1,0:T(1,128)} %constant.14.clone.qpos_ref) | copy-start | bytes 36868
  31.5 40.9 %slice-start = ((s8[8388608]{0:T(1024)(128)(4,1)}), s8[4194304]{0:T(1024)(128)(4,1)S(1)}, s32[]{:S(2)}) async-start(s8[8388608]{0:T(1024)(128)(4,1)} %bitcast.17), calls=%async_computation | async-start | bytes 8388608
  31.5 40.9 %slice-start.2 = ((s8[8388608]{0:T(1024)(128)(4,1)}), s8[4194304]{0:T(1024)(128)(4,1)S(1)}, s32[]{:S(2)}) async-start(s8[8388608]{0:T(1024)(128)(4,1)} %bitcast.19), calls=%async_computation.2 | async-start | bytes 8388608
  31.5 40.9 %slice-start.1 = ((s8[8388608]{0:T(1024)(128)(4,1)}), s8[4194304]{0:T(1024)(128)(4,1)S(1)}, s32[]{:S(2)}) async-start(s8[8388608]{0:T(1024)(128)(4,1)} %bitcast.17), calls=%async_computation.1 | async-start | bytes 8388608
  31.6 40.9 %slice-start.3 = ((s8[8388608]{0:T(1024)(128)(4,1)}), s8[4194304]{0:T(1024)(128)(4,1)S(1)}, s32[]{:S(2)}) async-start(s8[8388608]{0:T(1024)(128)(4,1)} %bitcast.19), calls=%async_computation.3 | async-start | bytes 8388608
  31.6 40.9 %copy-start = (f32[192,1024]{1,0:T(8,128)S(1)}, f32[192,1024]{1,0:T(8,128)}, u32[]{:S(2)}) copy-start(f32[192,1024]{1,0:T(8,128)} %frames_in.3) | copy-start | bytes 2359300
  31.6 40.9 %copy-start.1 = (bf16[1024,1024]{1,0:T(8,128)(2,1)S(1)}, bf16[1024,1024]{1,0:T(8,128)(2,1)}, u32[]{:S(2)}) copy-start(bf16[1024,1024]{1,0:T(8,128)(2,1)} %w_out_ref.1) | copy-start | bytes 6291460
  31.6 40.9 %copy-start.2 = (f32[192,1024]{1,0:T(8,128)S(1)}, f32[192,1024]{1,0:T(8,128)}, u32[]{:S(2)}) copy-start(f32[192,1024]{1,0:T(8,128)} %cot_ref.1) | copy-start | bytes 2359300
  31.6 40.9 %copy-start.3 = (f32[4096]{0:T(1024)S(1)}, f32[4096]{0:T(1024)}, u32[]{:S(2)}) copy-start(f32[4096]{0:T(1024)} %param.23) | copy-start | bytes 49156
  31.6 40.9 %copy-start.4 = (f32[1024]{0:T(1024)S(1)}, f32[1024]{0:T(1024)}, u32[]{:S(2)}) copy-start(f32[1024]{0:T(1024)} %param.21) | copy-start | bytes 12292
  31.6 40.9 %copy-start.5 = (f32[1024]{0:T(1024)S(1)}, f32[1024]{0:T(1024)}, u32[]{:S(2)}) copy-start(f32[1024]{0:T(1024)} %param.25) | copy-start | bytes 12292
  111.3 36.9 %collective-permute-start = (bf16[8,96,1024]{2,1,0:T(8,128)(2,1)}, bf16[8,96,1024]{2,1,0:T(8,128)(2,1)S(1)}, u32[]{:S(2)}, u32[]{:S(2)}) collective-permute-start(bf16[8,96,1024]{2,1,0:T(8,128)(2,1)} %get-tuple-element.77), channel_id=1, source_target_pairs={{0,1},{1,0},{2,3},{3,2},{4,5},{5,4},{6,7},{7,6},{8,9},{9,8},{10,11... | collective-permute-start | bytes 4718600 | tf_op jit(solution)/shard_map/ppermute | solution.py:969
  111.9 36.6 %collective-permute-start.1 = (bf16[8,96,1024]{2,1,0:T(8,128)(2,1)}, bf16[8,96,1024]{2,1,0:T(8,128)(2,1)S(1)}, u32[]{:S(2)}, u32[]{:S(2)}) collective-permute-start(bf16[8,96,1024]{2,1,0:T(8,128)(2,1)} %get-tuple-element.78), channel_id=1, source_target_pairs={{0,4},{2,6},{4,0},{6,2},{8,12},{10,14},{12,8},{14,10},{16,20},{18,... | collective-permute-start | bytes 4718600 | tf_op jit(solution)/shard_map/ppermute | solution.py:970
  112.4 36.3 %collective-permute-start.2 = (bf16[8,96,1024]{2,1,0:T(8,128)(2,1)}, bf16[8,96,1024]{2,1,0:T(8,128)(2,1)S(1)}, u32[]{:S(2)}, u32[]{:S(2)}) collective-permute-start(bf16[8,96,1024]{2,1,0:T(8,128)(2,1)} %get-tuple-element.79), channel_id=1, source_target_pairs={{0,8},{2,10},{4,12},{6,14},{8,0},{10,2},{12,4},{14,6},{16,24},{18,... | collective-permute-start | bytes 4718600 | tf_op jit(solution)/shard_map/ppermute | solution.py:970

commit v7 on v6

--- a/solution.py
+++ b/solution.py
@@ -754,6 +754,27 @@
     return lax.axis_index("blk") * 2 + lax.axis_index("grp")
 
 
+def plane_at(z, turn):
+    high = lax.rem(lax.div(z, 2) + jnp.where(turn < 2, 1, 0), 2)
+    low = lax.rem(z + jnp.where((turn == 1) | (turn == 2), 1, 0), 2)
+    return high * 2 + low
+
+
+def peer_at(i, n):
+    me, plane = own_index(), n // 4
+    return plane_at(lax.div(me, plane), lax.div(i, plane)) * plane + lax.rem(me + i, plane)
+
+
+def each_peer(n, body):
+    @pl.loop(0, n)
+    def _(i):
+        other = peer_at(i, n)
+
+        @pl.when(other != own_index())
+        def _():
+            body(i, other)
+
+
 def sibling_of(core):
     return {"blk": lax.axis_index("blk") + 1 - 2 * core, "grp": lax.axis_index("grp")}
 
@@ -791,7 +812,7 @@
     groups = width // 256
 
     def group_at(i):
-        return lax.rem(lax.div(me, n // groups) + 1 + i, groups)
+        return plane_at(lax.div(me, n // groups), i)
 
     def fetch(group):
         columns = pl.ds(pl.multiple_of(group * 256, 256), 256)
@@ -868,7 +889,7 @@
     plane = n // groups
     swaps = []
     for t in range(groups):
-        first = pl.multiple_of(lax.rem(lax.div(me, plane) + groups - 1 - t, groups) * plane, plane)
+        first = pl.multiple_of(group_at(t) * plane, plane)
 
         @pl.loop(0, plane)
         def _(j):
@@ -928,20 +949,16 @@
     greet_all(me, n)
 
     def copy_with(i, src):
-        other = lax.rem(me + i, n)
+        other = peer_at(i, n)
         return remote(x_in.at[other], x_out.at[src], send.at[i], recv.at[src], place(other))
 
-    @pl.loop(1, n)
-    def _(i):
-        copy_with(i, me).start()
+    each_peer(n, lambda i, other: copy_with(i, me).start())
 
     own = pltpu.make_async_copy(x_in.at[me], x_out.at[me], local)
     own.start()
     own.wait()
 
-    @pl.loop(1, n)
-    def _(i):
-        copy_with(i, lax.rem(me + i, n)).wait()
+    each_peer(n, lambda i, other: copy_with(i, other).wait())
 
 
 def exchange(x, n, collective_id):
@@ -1016,12 +1033,10 @@
         copy.start()
 
     def copy_with(i, src):
-        other = lax.rem(me + i, n)
+        other = peer_at(i, n)
         return remote(blocks_in.at[other], blocks_out.at[src], send.at[i], recv.at[src], place(other))
 
-    @pl.loop(1, n)
-    def _(i):
-        copy_with(i, me).start()
+    each_peer(n, lambda i, other: copy_with(i, me).start())
 
     own = pltpu.make_async_copy(blocks_in.at[me], blocks_out.at[me], local)
     own.start()
@@ -1090,9 +1105,7 @@
     flush(send_c, send_c_out)
     own.wait()
 
-    @pl.loop(1, n)
-    def _(i):
-        copy_with(i, lax.rem(me + i, n)).wait()
+    each_peer(n, lambda i, other: copy_with(i, other).wait())
 
     for copy in flushes:
         copy.wait()
@@ -1205,7 +1218,7 @@
 
     def to_all(src_ref, dst_ref, sends, recvs):
         def copy_with(i, src):
-            other = lax.rem(me + i, n)
+            other = peer_at(i, n)
             return remote(src_ref.at[other], dst_ref.at[src], sends.at[i], recvs.at[src], place(other))
 
         return copy_with
@@ -1214,20 +1227,18 @@
     dkv_copy = to_all(total, dkv_all, dkv_send, dkv_recv)
     small_copy = to_all(small_in, small_all, small_send, small_recv)
 
-    @pl.loop(1, n)
-    def _(i):
-        dq_copy(i, me).start()
+    each_peer(n, lambda i, other: dq_copy(i, me).start())
 
     swap.wait()
 
     def add(j):
         return (dkv_in[j, core] + theirs[j]).astype(BF16)
 
-    @pl.loop(1, n)
-    def _(i):
-        other = lax.rem(me + i, n)
+    def add_and_send(i, other):
         total[other] = add(other)
         dkv_copy(i, me).start()
+
+    each_peer(n, add_and_send)
 
     dkv_all[me] = add(me)
     dq_all[me] = dq_in[me]
@@ -1280,16 +1291,12 @@
     act1_own = pltpu.make_async_copy(act1.at[core], act1_2.at[pl.ds(0, rows)], local.at[9])
     act1_own.start()
 
-    @pl.loop(1, n)
-    def _(i):
-        dq_copy(i, lax.rem(me + i, n)).wait()
+    each_peer(n, lambda i, other: dq_copy(i, other).wait())
 
     advance(waves[0])
     advance(waves[1])
 
-    @pl.loop(1, n)
-    def _(i):
-        dkv_copy(i, lax.rem(me + i, n)).wait()
+    each_peer(n, lambda i, other: dkv_copy(i, other).wait())
 
     advance(waves[0])
     advance(waves[2])
@@ -1349,9 +1356,7 @@
         small_in[d, 2:3] = b_down_grad[:, at]
         small_in[d, 3:4] = b_up_grad[:, d * 128 : (d + 1) * 128]
 
-    @pl.loop(1, n)
-    def _(i):
-        small_copy(i, me).start()
+    each_peer(n, lambda i, other: small_copy(i, me).start())
 
     g = g * gain[...]
     frames_out[...] = grad_mid[...] + r * (g - norm * jnp.mean(g * norm, axis=-1, keepdims=True))
@@ -1359,9 +1364,7 @@
 
     advance(late * 3)
 
-    @pl.loop(1, n)
-    def _(i):
-        small_copy(i, lax.rem(me + i, n)).wait()
+    each_peer(n, lambda i, other: small_copy(i, other).wait())
 
     part = width // n
     small_out[...] = pltpu.roll(jnp.sum(small_all[...], axis=0), lax.rem(128 - lax.rem(me, 128 // part) * part, 128), 1)

time: 240 us -> 242 us (level); the launches traced: 239 us -> 245 us
  Pallas kernels: 233 us -> 242 us
  waiting for transfers between devices: 3.18 us -> 0.01 us
    pallas_call x1, Pallas kernels: 32.5 us -> 38.3 us  [mix_back(): pl.pallas_call(functools.partial(back_kernel, lengths.shape[0], chunks, k...]
    pallas_call x1, Pallas kernels: 22.2 us -> 26.1 us  [mix(): pl.pallas_call(functools.partial(mix_kernel, lengths.shape[0], chunks, ke...]
    pallas_call x1, Pallas kernels: 22.5 us -> 19.6 us  [share(): pl.pallas_call(functools.partial(share_kernel, n), in_specs=[vmem] * 7, o...]
    ppermute x1, waiting for transfers between devices: 2.65 us -> 0.01 us  [flipped(): return lax.ppermute(x, 'grp', [(0, 1), (1, 0)])]
  transfers between devices with their start and end apart: 3 -> 3, of which waited for: 3 -> 0; matrix products, arithmetic and copies ran while one was open for 0% -> 0% of each run, Pallas kernels for 14% -> 16%
where the time goes in v7:
time: 242 us; the launch traced here: 245 us
  Pallas kernels  242 us (100%)
    pallas_call x1, Pallas kernels, finish(): pl.pallas_call(functools.partial(finish_kernel, n), in_specs=[vmem] * 8 +...  88.6 us
    pallas_call x1, Pallas kernels, mix_back(): pl.pallas_call(functools.partial(back_kernel, lengths.shape[0], chunks, k...  38.3 us
    pallas_call x1, Pallas kernels, to_heads(): pl.pallas_call(functools.partial(to_heads_kernel, n), in_specs=[hbm] * 5,...  30.3 us
    pallas_call x1, Pallas kernels, mix(): pl.pallas_call(functools.partial(mix_kernel, lengths.shape[0], chunks, ke...  26.1 us
    pallas_call x1, Pallas kernels, exchange(): pl.pallas_call(functools.partial(exchange_kernel, n), in_specs=[vmem], ou...  20.6 us
    pallas_call x1, Pallas kernels, share(): pl.pallas_call(functools.partial(share_kernel, n), in_specs=[vmem] * 7, o...  19.6 us
    pallas_call x1, Pallas kernels, feed(): pl.pallas_call(feed_kernel, grid=(steps,), in_specs=[fixed(*blocks.shape)...  16.2 us
  transfers between devices with their start and end apart: 3, of which 0 were waited for; matrix products, arithmetic and copies ran while one was open for 0% of the time, Pallas kernels for 16%

profile of v7, /device:TPU:0, one launch (start us, length us, event | category | flops | bytes accessed | tf_op | source)
XLA Modules:
  0.0 245.3 jit_solution(16526955954909666102)
XLA Ops:
  0.7 0.0 copy-start.7
  0.7 30.3 %to_heads.1 = (bf16[32,2,96,128]{3,2,1,0:T(8,128)(2,1)S(1)}, bf16[32,48,128]{2,1,0:T(8,128)(2,1)S(1)}, bf16[2,192,512]{2,1,0:T(8,128)(2,1)}) custom-call(f32[1,1024]{1,0:T(1,128)} %bitcast.33, f32[192,1024]{1,0:T(8,128)} %frames_in.3, bf16[1024,1024]{1,0:T(8,128)(2,1)} %wq_in.3, bf16[1024,1024]{1,0:T(8,128)(2,1)} %wk_in.3, bf16[1024,1024]{1,0:T(8,128)(2,1)} %wv_in.3), custom_call_target="tpu_custom_call" | custom-call | tf_op jit(solution)/shard_map/to_heads/pallas_call | solution.py:915
  31.0 0.0 slice-start
  31.0 0.0 slice-start.2
  31.0 0.0 slice-start.1
  31.0 0.0 slice-start.3
  31.0 0.0 copy-start
  31.0 0.0 copy-start.1
  31.1 0.0 copy-start.2
  31.1 0.0 copy-start.3
  31.1 0.0 copy-start.4
  31.1 0.0 copy-start.5
  31.1 26.1 %mix.1 = (f32[64,3072]{1,0:T(8,128)S(1)}, f32[1,3072]{1,0:T(1,128)S(1)}, bf16[32,48,128]{2,1,0:T(8,128)(2,1)S(1)}) custom-call(s32[12]{0:T(128)S(1)} %copy-done.6, s32[1]{0:T(128)} %bitcast.core_ref, bf16[6144,128]{1,0:T(8,128)(2,1)S(1)} %bitcast.28, bf16[32,48,128]{2,1,0:T(8,128)(2,1)S(1)} %get-tuple-element.60.qp_ref, s32[1,3072]{1,0:T(1,128)S(1)} %copy-done.7), custom_call_target="tpu_custom_call" | custom-call | flops 24999999488 | bytes 8388608 | tf_op jit(solution)/shard_map/mix/pallas_call | solution.py:465
  57.2 20.6 %exchange.1.blocks_ref = bf16[32,48,128]{2,1,0:T(8,128)(2,1)S(1)} custom-call(bf16[32,48,128]{2,1,0:T(8,128)(2,1)S(1)} %get-tuple-element.61.x_in), custom_call_target="tpu_custom_call" | custom-call | tf_op jit(solution)/shard_map/exchange/pallas_call | solution.py:966
  77.9 16.2 %feed.1 = (f32[192,1024]{1,0:T(8,128)S(1)}, f32[192,1024]{1,0:T(8,128)}, bf16[32,48,128]{2,1,0:T(8,128)(2,1)S(1)}, bf16[2,192,2048]{2,1,0:T(8,128)(2,1)S(1)}, bf...) custom-call(bf16[32,48,128]{2,1,0:T(8,128)(2,1)S(1)} %exchange.1.blo, ...), custom_call_target="tpu_custom_call" | custom-call | tf_op jit(solution)/shard_map/feed/pallas_call | solution.py:677
  94.1 19.6 %share.1 = (bf16[32,48,128]{2,1,0:T(8,128)(2,1)S(1)}, bf16[8,96,1024]{2,1,0:T(8,128)(2,1)}, bf16[8,96,1024]{2,1,0:T(8,128)(2,1)}, bf16[8,96,1024]{2,1,0:T(8,128)...) custom-call(bf16[32,48,128]{2,1,0:T(8,128)(2,1)S(1)} %get-tuple-element.62.blocks_in, ...), custom_call_target="tpu_custom_call" | custom-call | tf_op jit(solution)/shard_map/share/pallas_call | solution.py:1119
  113.7 0.6 collective-permute-start
  114.3 1.0 collective-permute-start.1
  115.3 0.7 collective-permute-start.2
  116.0 38.3 %mix_back.1 = (f32[6144,128]{1,0:T(8,128)S(1)}, bf16[32,48,128]{2,1,0:T(8,128)(2,1)S(1)}) custom-call(s32[12]{0:T(128)S(1)} %copy-done.6, s32[1]{0:T(128)} %bitcast.core_ref, bf16[6144,128]{1,0:T(8,128)(2,1)S(1)} %bitcast.29, bf16[32,48,128]{2,1,0:T(8,128)(2,1)S(1)} %get-tuple-element.60.qp_ref, bf16[32,48,128]{2,1,0:T(8,128)(2,1)S(1)} %get-tuple-element.69.dp_ref, ...), custom_call_target="tpu_custom_call" | custom-call | flops 40000000000 | bytes 8388608 | tf_op jit(solution)/shard_map/mix_back/pallas_call | solution.py:564
  154.2 0.0 collective-permute-done.1
  154.3 0.0 collective-permute-done.2
  154.3 88.6 %finish.1 = (f32[192,1024]{1,0:T(8,128)S(1)}, f32[32,1024]{1,0:T(8,128)S(1)}, f32[32,1024]{1,0:T(8,128)S(1)}, f32[32,1024]{1,0:T(8,128)S(1)}, f32[32,1024]{1,0:T...) custom-call(f32[32,2,96,128]{3,2,1,0:T(8,128)S(1)} %bitcast.21, ...), custom_call_target="tpu_custom_call" | custom-call | tf_op jit(solution)/shard_map/finish/pallas_call | solution.py:1395
  242.8 2.3 emit.1
  (16 shorter events, 0.0 us)
Async XLA Ops:
  0.6 30.3 %copy-start.6 = (s32[12]{0:T(128)S(1)}, s32[12]{0:T(128)}, u32[]{:S(2)}) copy-start(s32[12]{0:T(128)} %len_ref.3) | copy-start | bytes 148
  0.7 30.3 %copy-start.7 = (s32[1,3072]{1,0:T(1,128)S(1)}, s32[1,3072]{1,0:T(1,128)}, u32[]{:S(2)}) copy-start(s32[1,3072]{1,0:T(1,128)} %constant.14.clone.qpos_ref) | copy-start | bytes 36868
  31.0 46.9 %slice-start = ((s8[8388608]{0:T(1024)(128)(4,1)}), s8[4194304]{0:T(1024)(128)(4,1)S(1)}, s32[]{:S(2)}) async-start(s8[8388608]{0:T(1024)(128)(4,1)} %bitcast.17), calls=%async_computation | async-start | bytes 8388608
  31.0 46.9 %slice-start.2 = ((s8[8388608]{0:T(1024)(128)(4,1)}), s8[4194304]{0:T(1024)(128)(4,1)S(1)}, s32[]{:S(2)}) async-start(s8[8388608]{0:T(1024)(128)(4,1)} %bitcast.19), calls=%async_computation.2 | async-start | bytes 8388608
  31.0 46.8 %slice-start.1 = ((s8[8388608]{0:T(1024)(128)(4,1)}), s8[4194304]{0:T(1024)(128)(4,1)S(1)}, s32[]{:S(2)}) async-start(s8[8388608]{0:T(1024)(128)(4,1)} %bitcast.17), calls=%async_computation.1 | async-start | bytes 8388608
  31.0 46.8 %slice-start.3 = ((s8[8388608]{0:T(1024)(128)(4,1)}), s8[4194304]{0:T(1024)(128)(4,1)S(1)}, s32[]{:S(2)}) async-start(s8[8388608]{0:T(1024)(128)(4,1)} %bitcast.19), calls=%async_computation.3 | async-start | bytes 8388608
  31.0 46.8 %copy-start = (f32[192,1024]{1,0:T(8,128)S(1)}, f32[192,1024]{1,0:T(8,128)}, u32[]{:S(2)}) copy-start(f32[192,1024]{1,0:T(8,128)} %frames_in.3) | copy-start | bytes 2359300
  31.0 46.8 %copy-start.1 = (bf16[1024,1024]{1,0:T(8,128)(2,1)S(1)}, bf16[1024,1024]{1,0:T(8,128)(2,1)}, u32[]{:S(2)}) copy-start(bf16[1024,1024]{1,0:T(8,128)(2,1)} %w_out_ref.1) | copy-start | bytes 6291460
  31.1 46.8 %copy-start.2 = (f32[192,1024]{1,0:T(8,128)S(1)}, f32[192,1024]{1,0:T(8,128)}, u32[]{:S(2)}) copy-start(f32[192,1024]{1,0:T(8,128)} %cot_ref.1) | copy-start | bytes 2359300
  31.1 46.8 %copy-start.3 = (f32[4096]{0:T(1024)S(1)}, f32[4096]{0:T(1024)}, u32[]{:S(2)}) copy-start(f32[4096]{0:T(1024)} %param.23) | copy-start | bytes 49156
  31.1 46.8 %copy-start.4 = (f32[1024]{0:T(1024)S(1)}, f32[1024]{0:T(1024)}, u32[]{:S(2)}) copy-start(f32[1024]{0:T(1024)} %param.21) | copy-start | bytes 12292
  31.1 46.8 %copy-start.5 = (f32[1024]{0:T(1024)S(1)}, f32[1024]{0:T(1024)}, u32[]{:S(2)}) copy-start(f32[1024]{0:T(1024)} %param.25) | copy-start | bytes 12292
  113.7 40.5 %collective-permute-start = (bf16[8,96,1024]{2,1,0:T(8,128)(2,1)}, bf16[8,96,1024]{2,1,0:T(8,128)(2,1)S(1)}, u32[]{:S(2)}, u32[]{:S(2)}) collective-permute-start(bf16[8,96,1024]{2,1,0:T(8,128)(2,1)} %get-tuple-element.77), channel_id=1, source_target_pairs={{0,1},{1,0},{2,3},{3,2},{4,5},{5,4},{6,7},{7,6},{8,9},{9,8},{10,11... | collective-permute-start | bytes 4718600 | tf_op jit(solution)/shard_map/ppermute | solution.py:986
  114.3 39.9 %collective-permute-start.1 = (bf16[8,96,1024]{2,1,0:T(8,128)(2,1)}, bf16[8,96,1024]{2,1,0:T(8,128)(2,1)S(1)}, u32[]{:S(2)}, u32[]{:S(2)}) collective-permute-start(bf16[8,96,1024]{2,1,0:T(8,128)(2,1)} %get-tuple-element.78), channel_id=1, source_target_pairs={{0,4},{2,6},{4,0},{6,2},{8,12},{10,14},{12,8},{14,10},{16,20},{18,... | collective-permute-start | bytes 4718600 | tf_op jit(solution)/shard_map/ppermute | solution.py:987
  115.3 39.0 %collective-permute-start.2 = (bf16[8,96,1024]{2,1,0:T(8,128)(2,1)}, bf16[8,96,1024]{2,1,0:T(8,128)(2,1)S(1)}, u32[]{:S(2)}, u32[]{:S(2)}) collective-permute-start(bf16[8,96,1024]{2,1,0:T(8,128)(2,1)} %get-tuple-element.79), channel_id=1, source_target_pairs={{0,8},{2,10},{4,12},{6,14},{8,0},{10,2},{12,4},{14,6},{16,24},{18,... | collective-permute-start | bytes 4718600 | tf_op jit(solution)/shard_map/ppermute | solution.py:987

commit v8 on v7

--- a/solution.py
+++ b/solution.py
@@ -1293,13 +1293,6 @@
 
     each_peer(n, lambda i, other: dq_copy(i, other).wait())
 
-    advance(waves[0])
-    advance(waves[1])
-
-    each_peer(n, lambda i, other: dkv_copy(i, other).wait())
-
-    advance(waves[0])
-    advance(waves[2])
     def pair_with(k):
         columns = slice(k * width, (k + 1) * width)
         own, other = qkv2.at[pl.ds(0, rows), columns], qkv2.at[pl.ds(rows, rows), columns]
@@ -1316,6 +1309,23 @@
             qkv2[first : first + quarter, at] = pair_low(a, b, low_q).astype(BF16)
             qkv2[first + quarter : first + 2 * quarter, at] = pair_high(a, b, low_q).astype(BF16)
     pairs[0].start()
+    def product(k):
+        pairs[k].wait()
+        value = tn_dot(act1_2[...], qkv2[:, k * width : (k + 1) * width]).astype(BF16)
+        for j in range(16):
+            sums[3 + k][j // 8, j // 4 % 2, j // 2 % 2, j % 2] = value[j * 32 : (j + 1) * 32]
+        late[k].start()
+
+    advance(waves[0])
+    act1_copy.wait()
+    act1_own.wait()
+    product(0)
+    advance(waves[1])
+
+    each_peer(n, lambda i, other: dkv_copy(i, other).wait())
+
+    advance(waves[0])
+    advance(waves[2])
     for zy in range(8):
         for s in range(2):
             j = (zy * 2 + s) * 2
@@ -1328,15 +1338,8 @@
     pairs[1].start()
     pairs[2].start()
     advance(waves[1])
-    act1_copy.wait()
-    act1_own.wait()
-    for k in range(3):
-        pairs[k].wait()
-        value = tn_dot(act1_2[...], qkv2[:, k * width : (k + 1) * width]).astype(BF16)
-        for j in range(16):
-            sums[3 + k][j // 8, j // 4 % 2, j // 2 % 2, j % 2] = value[j * 32 : (j + 1) * 32]
-        late[k].start()
-
+    product(1)
+    product(2)
     for copy in fetches[3:]:
         copy.wait()
     g = nt_dot(qkv2[:rows, :width], wq[...])

time: 242 us -> 249 us (1.029)
  Pallas kernels: 242 us -> 249 us
    pallas_call x1, Pallas kernels: 88.6 us -> 95.5 us  [finish(): pl.pallas_call(functools.partial(finish_kernel, n), in_specs=[vmem] * 8 +...]
  transfers between devices with their start and end apart: 3 -> 3, of which waited for: 0 -> 0; matrix products, arithmetic and copies ran while one was open for 0% -> 0% of each run, Pallas kernels for 16% -> 15%
where the time goes in v8:
time: 249 us; the launch traced here: 252 us
  Pallas kernels  249 us (100%)
    pallas_call x1, Pallas kernels, finish(): pl.pallas_call(functools.partial(finish_kernel, n), in_specs=[vmem] * 8 +...  95.5 us
    pallas_call x1, Pallas kernels, mix_back(): pl.pallas_call(functools.partial(back_kernel, lengths.shape[0], chunks, k...  38.3 us
    pallas_call x1, Pallas kernels, to_heads(): pl.pallas_call(functools.partial(to_heads_kernel, n), in_specs=[hbm] * 5,...  30.3 us
    pallas_call x1, Pallas kernels, mix(): pl.pallas_call(functools.partial(mix_kernel, lengths.shape[0], chunks, ke...  26.1 us
    pallas_call x1, Pallas kernels, exchange(): pl.pallas_call(functools.partial(exchange_kernel, n), in_specs=[vmem], ou...  20.6 us
    pallas_call x1, Pallas kernels, share(): pl.pallas_call(functools.partial(share_kernel, n), in_specs=[vmem] * 7, o...  19.6 us
    pallas_call x1, Pallas kernels, feed(): pl.pallas_call(feed_kernel, grid=(steps,), in_specs=[fixed(*blocks.shape)...  16.2 us
  transfers between devices with their start and end apart: 3, of which 0 were waited for; matrix products, arithmetic and copies ran while one was open for 0% of the time, Pallas kernels for 15%

profile of v8, /device:TPU:0, one launch (start us, length us, event | category | flops | bytes accessed | tf_op | source)
XLA Modules:
  0.0 252.2 jit_solution(17770932553414715791)
XLA Ops:
  0.7 0.0 copy-start.7
  0.7 30.3 %to_heads.1 = (bf16[32,2,96,128]{3,2,1,0:T(8,128)(2,1)S(1)}, bf16[32,48,128]{2,1,0:T(8,128)(2,1)S(1)}, bf16[2,192,512]{2,1,0:T(8,128)(2,1)}) custom-call(f32[1,1024]{1,0:T(1,128)} %bitcast.33, f32[192,1024]{1,0:T(8,128)} %frames_in.3, bf16[1024,1024]{1,0:T(8,128)(2,1)} %wq_in.3, bf16[1024,1024]{1,0:T(8,128)(2,1)} %wk_in.3, bf16[1024,1024]{1,0:T(8,128)(2,1)} %wv_in.3), custom_call_target="tpu_custom_call" | custom-call | tf_op jit(solution)/shard_map/to_heads/pallas_call | solution.py:915
  31.0 0.0 slice-start
  31.0 0.0 slice-start.2
  31.0 0.0 slice-start.1
  31.0 0.0 slice-start.3
  31.0 0.0 copy-start
  31.0 0.0 copy-start.1
  31.1 0.0 copy-start.2
  31.1 0.0 copy-start.3
  31.1 0.0 copy-start.4
  31.1 0.0 copy-start.5
  31.1 26.1 %mix.1 = (f32[64,3072]{1,0:T(8,128)S(1)}, f32[1,3072]{1,0:T(1,128)S(1)}, bf16[32,48,128]{2,1,0:T(8,128)(2,1)S(1)}) custom-call(s32[12]{0:T(128)S(1)} %copy-done.6, s32[1]{0:T(128)} %bitcast.core_ref, bf16[6144,128]{1,0:T(8,128)(2,1)S(1)} %bitcast.28, bf16[32,48,128]{2,1,0:T(8,128)(2,1)S(1)} %get-tuple-element.60.qp_ref, s32[1,3072]{1,0:T(1,128)S(1)} %copy-done.7), custom_call_target="tpu_custom_call" | custom-call | flops 24999999488 | bytes 8388608 | tf_op jit(solution)/shard_map/mix/pallas_call | solution.py:465
  57.2 20.6 %exchange.1.blocks_ref = bf16[32,48,128]{2,1,0:T(8,128)(2,1)S(1)} custom-call(bf16[32,48,128]{2,1,0:T(8,128)(2,1)S(1)} %get-tuple-element.61.x_in), custom_call_target="tpu_custom_call" | custom-call | tf_op jit(solution)/shard_map/exchange/pallas_call | solution.py:966
  77.9 16.2 %feed.1 = (f32[192,1024]{1,0:T(8,128)S(1)}, f32[192,1024]{1,0:T(8,128)}, bf16[32,48,128]{2,1,0:T(8,128)(2,1)S(1)}, bf16[2,192,2048]{2,1,0:T(8,128)(2,1)S(1)}, bf...) custom-call(bf16[32,48,128]{2,1,0:T(8,128)(2,1)S(1)} %exchange.1.blo, ...), custom_call_target="tpu_custom_call" | custom-call | tf_op jit(solution)/shard_map/feed/pallas_call | solution.py:677
  94.1 19.6 %share.1 = (bf16[32,48,128]{2,1,0:T(8,128)(2,1)S(1)}, bf16[8,96,1024]{2,1,0:T(8,128)(2,1)}, bf16[8,96,1024]{2,1,0:T(8,128)(2,1)}, bf16[8,96,1024]{2,1,0:T(8,128)...) custom-call(bf16[32,48,128]{2,1,0:T(8,128)(2,1)S(1)} %get-tuple-element.62.blocks_in, ...), custom_call_target="tpu_custom_call" | custom-call | tf_op jit(solution)/shard_map/share/pallas_call | solution.py:1119
  113.7 0.6 collective-permute-start
  114.3 1.0 collective-permute-start.1
  115.3 0.7 collective-permute-start.2
  116.0 38.3 %mix_back.1 = (f32[6144,128]{1,0:T(8,128)S(1)}, bf16[32,48,128]{2,1,0:T(8,128)(2,1)S(1)}) custom-call(s32[12]{0:T(128)S(1)} %copy-done.6, s32[1]{0:T(128)} %bitcast.core_ref, bf16[6144,128]{1,0:T(8,128)(2,1)S(1)} %bitcast.29, bf16[32,48,128]{2,1,0:T(8,128)(2,1)S(1)} %get-tuple-element.60.qp_ref, bf16[32,48,128]{2,1,0:T(8,128)(2,1)S(1)} %get-tuple-element.69.dp_ref, ...), custom_call_target="tpu_custom_call" | custom-call | flops 40000000000 | bytes 8388608 | tf_op jit(solution)/shard_map/mix_back/pallas_call | solution.py:564
  154.3 0.0 collective-permute-done.1
  154.3 0.0 collective-permute-done.2
  154.3 95.5 %finish.1 = (f32[192,1024]{1,0:T(8,128)S(1)}, f32[32,1024]{1,0:T(8,128)S(1)}, f32[32,1024]{1,0:T(8,128)S(1)}, f32[32,1024]{1,0:T(8,128)S(1)}, f32[32,1024]{1,0:T...) custom-call(f32[32,2,96,128]{3,2,1,0:T(8,128)S(1)} %bitcast.21, ...), custom_call_target="tpu_custom_call" | custom-call | tf_op jit(solution)/shard_map/finish/pallas_call | solution.py:1398
  249.8 2.3 emit.1
  (16 shorter events, 0.0 us)
Async XLA Ops:
  0.6 30.3 %copy-start.6 = (s32[12]{0:T(128)S(1)}, s32[12]{0:T(128)}, u32[]{:S(2)}) copy-start(s32[12]{0:T(128)} %len_ref.3) | copy-start | bytes 148
  0.7 30.3 %copy-start.7 = (s32[1,3072]{1,0:T(1,128)S(1)}, s32[1,3072]{1,0:T(1,128)}, u32[]{:S(2)}) copy-start(s32[1,3072]{1,0:T(1,128)} %constant.14.clone.qpos_ref) | copy-start | bytes 36868
  31.0 46.9 %slice-start = ((s8[8388608]{0:T(1024)(128)(4,1)}), s8[4194304]{0:T(1024)(128)(4,1)S(1)}, s32[]{:S(2)}) async-start(s8[8388608]{0:T(1024)(128)(4,1)} %bitcast.17), calls=%async_computation | async-start | bytes 8388608
  31.0 46.9 %slice-start.2 = ((s8[8388608]{0:T(1024)(128)(4,1)}), s8[4194304]{0:T(1024)(128)(4,1)S(1)}, s32[]{:S(2)}) async-start(s8[8388608]{0:T(1024)(128)(4,1)} %bitcast.19), calls=%async_computation.2 | async-start | bytes 8388608
  31.0 46.8 %slice-start.1 = ((s8[8388608]{0:T(1024)(128)(4,1)}), s8[4194304]{0:T(1024)(128)(4,1)S(1)}, s32[]{:S(2)}) async-start(s8[8388608]{0:T(1024)(128)(4,1)} %bitcast.17), calls=%async_computation.1 | async-start | bytes 8388608
  31.0 46.8 %slice-start.3 = ((s8[8388608]{0:T(1024)(128)(4,1)}), s8[4194304]{0:T(1024)(128)(4,1)S(1)}, s32[]{:S(2)}) async-start(s8[8388608]{0:T(1024)(128)(4,1)} %bitcast.19), calls=%async_computation.3 | async-start | bytes 8388608
  31.0 46.8 %copy-start = (f32[192,1024]{1,0:T(8,128)S(1)}, f32[192,1024]{1,0:T(8,128)}, u32[]{:S(2)}) copy-start(f32[192,1024]{1,0:T(8,128)} %frames_in.3) | copy-start | bytes 2359300
  31.0 46.8 %copy-start.1 = (bf16[1024,1024]{1,0:T(8,128)(2,1)S(1)}, bf16[1024,1024]{1,0:T(8,128)(2,1)}, u32[]{:S(2)}) copy-start(bf16[1024,1024]{1,0:T(8,128)(2,1)} %w_out_ref.1) | copy-start | bytes 6291460
  31.1 46.8 %copy-start.2 = (f32[192,1024]{1,0:T(8,128)S(1)}, f32[192,1024]{1,0:T(8,128)}, u32[]{:S(2)}) copy-start(f32[192,1024]{1,0:T(8,128)} %cot_ref.1) | copy-start | bytes 2359300
  31.1 46.8 %copy-start.3 = (f32[4096]{0:T(1024)S(1)}, f32[4096]{0:T(1024)}, u32[]{:S(2)}) copy-start(f32[4096]{0:T(1024)} %param.23) | copy-start | bytes 49156
  31.1 46.8 %copy-start.4 = (f32[1024]{0:T(1024)S(1)}, f32[1024]{0:T(1024)}, u32[]{:S(2)}) copy-start(f32[1024]{0:T(1024)} %param.21) | copy-start | bytes 12292
  31.1 46.8 %copy-start.5 = (f32[1024]{0:T(1024)S(1)}, f32[1024]{0:T(1024)}, u32[]{:S(2)}) copy-start(f32[1024]{0:T(1024)} %param.25) | copy-start | bytes 12292
  113.7 40.5 %collective-permute-start = (bf16[8,96,1024]{2,1,0:T(8,128)(2,1)}, bf16[8,96,1024]{2,1,0:T(8,128)(2,1)S(1)}, u32[]{:S(2)}, u32[]{:S(2)}) collective-permute-start(bf16[8,96,1024]{2,1,0:T(8,128)(2,1)} %get-tuple-element.77), channel_id=1, source_target_pairs={{0,1},{1,0},{2,3},{3,2},{4,5},{5,4},{6,7},{7,6},{8,9},{9,8},{10,11... | collective-permute-start | bytes 4718600 | tf_op jit(solution)/shard_map/ppermute | solution.py:986
  114.3 39.9 %collective-permute-start.1 = (bf16[8,96,1024]{2,1,0:T(8,128)(2,1)}, bf16[8,96,1024]{2,1,0:T(8,128)(2,1)S(1)}, u32[]{:S(2)}, u32[]{:S(2)}) collective-permute-start(bf16[8,96,1024]{2,1,0:T(8,128)(2,1)} %get-tuple-element.78), channel_id=1, source_target_pairs={{0,4},{2,6},{4,0},{6,2},{8,12},{10,14},{12,8},{14,10},{16,20},{18,... | collective-permute-start | bytes 4718600 | tf_op jit(solution)/shard_map/ppermute | solution.py:987
  115.3 39.0 %collective-permute-start.2 = (bf16[8,96,1024]{2,1,0:T(8,128)(2,1)}, bf16[8,96,1024]{2,1,0:T(8,128)(2,1)S(1)}, u32[]{:S(2)}, u32[]{:S(2)}) collective-permute-start(bf16[8,96,1024]{2,1,0:T(8,128)(2,1)} %get-tuple-element.79), channel_id=1, source_target_pairs={{0,8},{2,10},{4,12},{6,14},{8,0},{10,2},{12,4},{14,6},{16,24},{18,... | collective-permute-start | bytes 4718600 | tf_op jit(solution)/shard_map/ppermute | solution.py:987
